TPU v7x, 32 devices: a whole 2x2x4 slice. The times are simulated.
32 devices in a mesh: slab: 8 (over z, x), pencil: 4 (over y, core).
Axes of the slice: x: 2, y: 2, z: 4, core: 2. Of those that a mesh axis runs over, the one named last changes fastest.
Arguments:
- a_blocks: float32 [128, 32, 20480], P('slab', 'pencil'), may hold values from -1 to 8, as said below
- col_codes: int32 [128, 32, 5], P('slab', 'pencil'), may hold values from 0 to 8, as said below
- agg_of: int32 [128, 32], P('slab', 'pencil'), may hold values from 0 to 511, as said below
- test_vectors: float32 [128, 32, 2048], P('slab', 'pencil'), may hold values from -36 to 36
Outputs:
- relaxed: float32 [128, 32, 2048], P('slab', 'pencil')
- tiles: float32 [128, 32, 512], P('slab', 'pencil')
- products: float32 [128, 32, 2560], P('slab', 'pencil')
Inputs may be any that keep to these rules, and one draw needn't show every extreme that they name: `col_codes`: slot 0 of every block row is code 4, the block row itself; slots 1 to 4 hold different codes among the other eight of the 3 x 3 neighbourhood. `agg_of`: aggregate g is owned by device g // 16, devices numbered slab-major. On each device the block rows, in row-major order, form 16 groups of 8 consecutive block rows; all block rows of a group belong to aggregates of one owner, and the groups of one device go to different owners. Some owners receive a group from every device. `a_blocks`: the diagonal entries of every slot-0 block lie in [1.99, 8].
All inputs are finite; a program needn't handle non-finite values.
Results may differ from a plain program's by a relative error of at most 0.0003.
Values sent between devices are 32-bit elements; how exact they have to be, the bound alone decides.
No kernel may reach another device: no remote copies, remote signals or barrier semaphores. Data moves between devices by JAX's collectives and lax.ppermute only.
A program may use at most 320 MiB of HBM per device.

v0:
```python
import math

import jax
import jax.numpy as jnp
from jax import lax
from jax.sharding import PartitionSpec as P

BLK = 64
NV = 32
NC = 8
KS = 5
ITERS = 2


OMEGA = 2.0 / 3.0
FULL_PRECISION = lax.Precision.HIGHEST


def with_halo(cells, sides, width):
    for axis, dim in sides:
        count = lax.axis_size(axis)
        ends = count - 1
        head = lax.slice_in_dim(cells, 0, width, axis=dim)
        tail = lax.slice_in_dim(cells, cells.shape[dim] - width, cells.shape[dim], axis=dim)
        cells = jnp.concatenate(
            [
                lax.ppermute(tail, axis, [(i, (i + 1) % count) for i in range(ends)]),
                cells,
                lax.ppermute(head, axis, [((i + 1) % count, i) for i in range(ends)]),
            ],
            axis=dim,
        )
    return cells


def coarse_modes(cells, coarse):
    centre = jnp.arange(cells, dtype=jnp.float32) + 0.5
    order = jnp.arange(coarse, dtype=jnp.float32)
    return jnp.cos(math.pi * centre[:, None] * order[None, :] / cells)


def solve_maps(coarse):
    gram = jnp.einsum("gkv,glv->gkl", coarse, coarse, precision=FULL_PRECISION)
    trace_sum = jnp.trace(gram, axis1=1, axis2=2)
    ridge = 0.1 * trace_sum / NC + 1e-06
    gram = gram + ridge[:, None, None] * jnp.eye(NC, dtype=jnp.float32)[None]
    lower = jnp.linalg.cholesky(gram)
    half_solved = jax.scipy.linalg.solve_triangular(lower, coarse, lower=True)
    solved = jax.scipy.linalg.solve_triangular(lower, half_solved, lower=True, trans=1)
    return jnp.swapaxes(solved, 1, 2)


def slot_index(col_codes):
    height, across_devices = (col_codes.shape[0], col_codes.shape[1])
    row_pos = jnp.arange(height, dtype=jnp.int32)[:, None, None] + col_codes // 3
    col_pos = jnp.arange(across_devices, dtype=jnp.int32)[None, :, None] + col_codes % 3
    return (row_pos * (across_devices + 2) + col_pos).reshape(-1)


def pick_rows(padded, flat_index, height, across_devices):
    features = padded.shape[2]
    flat = padded.reshape(padded.shape[0] * padded.shape[1], features)
    picked = jnp.take(flat, flat_index, axis=0)
    return picked.reshape(height, across_devices, KS, features)


def fit_slots(slot_coefficient, slot_ids, per_owner):
    members = (slot_ids[None, :] == jnp.arange(per_owner, dtype=jnp.int32)[:, None]).astype(
        jnp.float32
    )
    counts = jnp.sum(members, axis=1)
    summed = jnp.dot(
        members,
        slot_coefficient.reshape(slot_coefficient.shape[0], NC * NV),
        precision=FULL_PRECISION,
    )
    coarse = summed.reshape(per_owner, NC, NV) / jnp.maximum(counts, 1.0)[:, None, None]
    maps = solve_maps(coarse)
    return jnp.dot(members.T, maps.reshape(per_owner, NV * NC), precision=FULL_PRECISION)


def pack_slots(chosen_f, payload, group_list, capacity):
    flat = payload.reshape(group_list, capacity * payload.shape[1])
    packed = jnp.dot(chosen_f, flat, precision=FULL_PRECISION)
    return packed.reshape(chosen_f.shape[0], capacity, payload.shape[1])


def unpack_slots(chosen_f, received, block_rows):
    flat = received.reshape(received.shape[0], received.shape[1] * received.shape[2])
    return jnp.dot(chosen_f.T, flat, precision=FULL_PRECISION).reshape(
        block_rows, received.shape[2]
    )


def send_owner(payload, slot_ids):
    arrived, arrived_ids = (
        lax.all_to_all(payload, ("slab", "pencil"), split_axis=0, concat_axis=0, tiled=True),
        lax.all_to_all(slot_ids, ("slab", "pencil"), split_axis=0, concat_axis=0, tiled=True),
    )
    return (arrived, arrived_ids)


def send_back(payload):
    returned = lax.all_to_all(payload, ("slab", "pencil"), split_axis=0, concat_axis=0, tiled=True)
    return returned


def shards(a_blocks, col_codes, agg_of, test_vectors):
    height, across_devices = (agg_of.shape[0], agg_of.shape[1])
    n_slab = lax.axis_size("slab")
    n_pencil = lax.axis_size("pencil")
    devices = n_slab * n_pencil
    blocks = a_blocks.reshape(height, across_devices, KS, BLK, BLK)
    diagonal = jnp.diagonal(blocks[:, :, 0], axis1=-2, axis2=-1)
    block_wide = jnp.transpose(blocks, (0, 1, 3, 2, 4)).reshape(
        height, across_devices, BLK, KS * BLK
    )
    flat_index = slot_index(col_codes)
    candidate_vectors = test_vectors.reshape(height, across_devices, BLK, NV)
    for sweep in range(ITERS):
        padded = with_halo(
            candidate_vectors.reshape(height, across_devices, BLK * NV),
            (("slab", 0), ("pencil", 1)),
            1,
        )
        picked = pick_rows(padded, flat_index, height, across_devices).reshape(
            height, across_devices, KS * BLK, NV
        )
        image = jnp.einsum("ijor,ijrw->ijow", block_wide, picked, precision=FULL_PRECISION)
        candidate_vectors = candidate_vectors - OMEGA * image / diagonal[:, :, :, None]
    squares = jnp.sum(candidate_vectors * candidate_vectors, axis=(0, 1, 2))
    totals = lax.psum(squares, ("slab", "pencil"))
    scale = jnp.sqrt(totals / (height * across_devices * BLK * devices) + 1e-06)
    relaxed = candidate_vectors / scale
    block_rows = height * across_devices
    capacity = 2 * block_rows // devices
    group_list = devices // 2
    per_owner = block_rows // 8
    near_null_modes = coarse_modes(BLK, NC)
    row_vectors = relaxed.reshape(block_rows, BLK, NV)
    group_agg = agg_of.reshape(group_list, capacity)
    group_owner = group_agg[:, 0] // per_owner
    chosen = group_owner[None, :] == jnp.arange(devices, dtype=jnp.int32)[:, None]
    chosen_f = chosen.astype(jnp.float32)
    slot_ids = (
        jnp.sum(jnp.where(chosen[:, :, None], group_agg[None] % per_owner + 1, 0), axis=1) - 1
    )
    slot_count = devices * capacity
    own_coef = jnp.einsum("ck,rcv->rkv", near_null_modes, row_vectors, precision=FULL_PRECISION)
    outgoing = pack_slots(chosen_f, own_coef.reshape(block_rows, NC * NV), group_list, capacity)
    arrived, arrived_ids = send_owner(outgoing, slot_ids)
    slot_maps = fit_slots(
        arrived.reshape(slot_count, NC, NV), arrived_ids.reshape(slot_count), per_owner
    )
    returned = send_back(slot_maps.reshape(devices, capacity, NV * NC))
    row_maps = unpack_slots(chosen_f, returned, block_rows).reshape(block_rows, NV, NC)
    tile_rows = jnp.einsum("rcv,rvk->rck", row_vectors, row_maps, precision=FULL_PRECISION)
    tile_grid = tile_rows.reshape(height, across_devices, BLK * NC)
    padded_tiles = with_halo(tile_grid, (("slab", 0), ("pencil", 1)), 1)
    picked_tiles = pick_rows(padded_tiles, flat_index, height, across_devices).reshape(
        height, across_devices, KS, BLK, NC
    )
    products = jnp.einsum("ijkoc,ijkcw->ijkow", blocks, picked_tiles, precision=FULL_PRECISION)
    return (
        relaxed.reshape(height, across_devices, BLK * NV),
        tile_grid,
        products.reshape(height, across_devices, KS * BLK * NC),
    )


def solution(mesh):
    in_specs = (
        P("slab", "pencil", None),
        P("slab", "pencil", None),
        P("slab", "pencil"),
        P("slab", "pencil", None),
    )
    out_specs = (P("slab", "pencil", None), P("slab", "pencil", None), P("slab", "pencil", None))
    return jax.shard_map(shards, mesh=mesh, in_specs=in_specs, out_specs=out_specs, check_vma=False)
```

profile of v0, /device:TPU:9, one launch (start us, length us, event | category | flops | bytes accessed | tf_op | source)
XLA Modules:
  0.0 561.5 jit_solution(3663114962406438115)
XLA Ops:
  12.4 39.0 %copy.182 = f32[16,8,20480]{0,1,2:T(8,128)} copy(f32[16,8,20480]{2,1,0:T(8,128)} %param.6) | data formatting | bytes 20971520 | tf_op args[0]
  51.4 11.6 %slice_bitcast_fusion = f32[16,8,64,64]{0,1,3,2:T(8,128)} fusion(f32[16,8,5,64,64]{0,1,4,3,2:T(8,128)} %bitcast), kind=kLoop, calls=%fused_computation.6 | loop fusion | bytes 4194304 | tf_op jit(solution)/shard_map/squeeze | solution.py:114
  63.0 4.4 collective-permute-start.2
  72.2 3.8 copy.187
  76.0 6.4 %gather_fusion = f32[64,16,8]{1,2,0:T(8,128)S(1)} fusion(f32[16,8,64,64]{0,1,3,2:T(8,128)} %slice_bitcast_fusion, s32[64]{0:T(128)S(1)} %or_bitcast_fusion), kind=kCustom, calls=%fused_computation.2 | custom fusion | bytes 66048 | tf_op jit(solution)/shard_map/jit(diagonal)/gather | solution.py:114
  82.6 63.2 %copy.183 = f32[16,8,64,5,64]{2,4,3,1,0:T(8,128)} copy(f32[16,8,64,5,64]{0,1,4,2,3:T(8,128)} %bitcast.1) | data formatting | bytes 20971520 | tf_op jit(solution)/shard_map/transpose | solution.py:115
  150.1 4.6 gather_fusion.2
  154.7 5.2 broadcast_select_fusion.1
  159.9 13.7 %reshape_reshape.16 = f32[16,8,320,32]{3,2,1,0:T(8,128)} reshape(f32[640,2048]{1,0:T(8,128)} %broadcast_select_fusion.1) | data formatting | bytes 10485760 | tf_op jit(solution)/shard_map/reshape;reshape | solution.py:126
  173.6 37.9 %bitcast_subtract_fusion.1 = f32[16,8,64,32]{2,3,1,0:T(8,128)S(1)} fusion(f32[16,8,64,32]{2,3,1,0:T(8,128)} %copy.187, f32[16,8,320,32]{3,2,1,0:T(8,128)} %reshape_reshape.16, f32[16,8,64,320]{2,3,1,0:T(8,128)} %bitcast.89, f32[16,8,64]{2,1,0:T(8,128)S(1)} %copy.186), kind=kOutput, calls=%fused_computation.13 | convolution fusion | flops 1007419392 | bytes 17858560 | tf_op jit(solution)/shard_map/ijor,ijrw->ijow/dot_general | solution.py:129
  211.8 4.0 collective-permute-start.4
  216.5 4.7 all-to-all-start
  237.1 4.4 collective-permute-done.7
  245.2 4.6 gather_fusion.3
  249.8 5.2 broadcast_select_fusion
  255.0 13.8 %reshape_reshape.17 = f32[16,8,320,32]{3,2,1,0:T(8,128)} reshape(f32[640,2048]{1,0:T(8,128)} %broadcast_select_fusion) | data formatting | bytes 10485760 | tf_op jit(solution)/shard_map/reshape;reshape | solution.py:126
  268.8 38.3 %multiply_reduce_fusion = (f32[32]{0:T(128)S(1)}, f32[16,8,64,32]{2,3,1,0:T(8,128)}) fusion(f32[16,8,64,32]{2,3,1,0:T(8,128)S(1)} %copy-done.1, f32[16,8,64]{2,1,0:T(8,128)S(1)} %copy.186, f32[16,8,320,32]{3,2,1,0:T(8,128)} %reshape_reshape.17, f32[16,8,64,320]{2,3,1,0:T(8,128)} %bitcast.90), kind=kOutput, calls=%fused_computation.16 | convolution fusion | flops 1007943680 | bytes 17858688 | tf_op jit(solution)/shard_map/ijor,ijrw->ijow/dot_general | solution.py:129
  307.1 37.1 %psum.7 = f32[32]{0:T(128)S(1)} all-reduce(f32[32]{0:T(128)S(1)} %get-tuple-element.33), channel_id=1, replica_groups=mesh['slab'=8,'pencil'=4] {'slab','pencil'}, use_global_device_ids=true, to_apply=%region_1.3 | all-reduce | flops 32 | bytes 256 | tf_op jit(solution)/shard_map/psum | solution.py:132
  351.1 6.6 %all-to-all-start.1 = ((f32[32,8,256]{2,1,0:T(8,128)}), f32[32,8,256]{2,1,0:T(8,128)S(1)}, u32[]{:S(2)}, u32[]{:S(2)}) async-start(f32[32,8,256]{2,1,0:T(8,128)} %copy.199), calls=%async_computation.1 | async-start | bytes 524288 | tf_op jit(solution)/shard_map/all_to_all | solution.py:97
  359.2 7.3 %all-to-all-done.1 = f32[32,8,256]{2,1,0:T(8,128)S(1)} async-done(((f32[32,8,256]{2,1,0:T(8,128)}), f32[32,8,256]{2,1,0:T(8,128)S(1)}, u32[]{:S(2)}, u32[]{:S(2)}) %all-to-all-start.1) | async-done | bytes 262176 | tf_op jit(solution)/shard_map/all_to_all | solution.py:97
  367.6 11.7 %custom-call.11 = f32[16,8,8]{2,1,0:T(8,128)S(1)} custom-call(f32[16,8,8]{2,1,0:T(8,128)S(1)} %fusion.24), custom_call_target="Cholesky" | custom-call | tf_op jit(solution)/shard_map/jit(cholesky)/cholesky | solution.py:47
  379.6 10.0 %custom-call.12 = f32[16,1,8,8]{2,3,1,0:T(8,128)S(1)} custom-call(f32[16,1,8,8]{3,2,1,0:T(8,128)S(1)} %select_bitcast_fusion), custom_call_target="InvertDiagBlocksLowerTriangular" | custom-call | tf_op jit(solution)/shard_map/jit(_solve_triangular)/vmap()/triangular_solve | solution.py:49
  391.4 4.4 all-to-all-start.2
  396.0 8.6 %all-to-all-done.2 = f32[32,8,256]{2,1,0:T(8,128)S(1)} async-done(((f32[32,8,256]{2,1,0:T(8,128)}), f32[32,8,256]{2,1,0:T(8,128)S(1)}, u32[]{:S(2)}, u32[]{:S(2)}) %all-to-all-start.2) | async-done | bytes 262176 | tf_op jit(solution)/shard_map/all_to_all | solution.py:104
  407.4 5.0 fusion.61
  421.9 4.2 reshape.237
  431.5 55.5 %copy.217 = f32[16,8,5,64,64]{4,3,2,1,0:T(8,128)} copy(f32[16,8,5,64,64]{0,1,4,3,2:T(8,128)} %bitcast) | data formatting | bytes 20971520 | tf_op jit(solution)/shard_map/reshape | solution.py:113
  489.8 4.4 reshape.233
  496.6 13.6 %gather.15 = f32[16,8,5,64,8]{4,3,2,1,0:T(8,128)} reshape(f32[640,512]{1,0:T(8,128)S(1)} %gather_fusion.1) | data formatting | bytes 2621440 | tf_op jit(solution)/shard_map/jit(_take)/gather | solution.py:63
  510.2 37.9 %fusion.6 = f32[16,8,5,64,8]{3,4,2,1,0:T(8,128)S(1)} fusion(f32[16,8,5,64,64]{4,3,2,1,0:T(8,128)} %copy.217, f32[16,8,5,64,8]{4,3,2,1,0:T(8,128)} %gather.15, pred[16,8,5]{2,1,0:T(8,128)(4,1)S(1)} %copy.212), kind=kOutput, calls=%fused_computation.18 | convolution fusion | flops 251985920 | bytes 13107840 | tf_op jit(solution)/shard_map/ijkoc,ijkcw->ijkow/dot_general | solution.py:163
  548.1 6.2 %copy.218 = f32[16,8,5,64,8]{0,4,3,2,1:T(8,128)} copy(f32[16,8,5,64,8]{3,4,2,1,0:T(8,128)S(1)} %fusion.6) | data formatting | bytes 2621440 | tf_op jit(solution)/shard_map/ijkoc,ijkcw->ijkow/dot_general | solution.py:163
  554.3 6.8 %copy.219 = f32[16,8,2560]{2,1,0:T(8,128)} copy(f32[16,8,2560]{0,2,1:T(8,128)} %bitcast.91) | data formatting | bytes 2621440
  (128 shorter events, 75.8 us)
Async XLA Ops:
  1.6 61.3 %collective-permute-start.1 = (f32[1,8,2048]{2,0,1:T(1,128)S(1)}, f32[1,8,2048]{2,0,1:T(1,128)S(1)}, u32[]{:S(2)}, u32[]{:S(2)}) collective-permute-start(f32[1,8,2048]{2,0,1:T(1,128)S(1)} %copy.179), channel_id=1, source_target_pairs={{4,0},{8,4},{12,8},{16,12},{20,16},{24,20},{28,24},{5,1},{9,5},{13... | collective-permute-start | bytes 196616 | tf_op jit(solution)/shard_map/ppermute | solution.py:29
  4.7 58.3 %collective-permute-start = (f32[1,8,2048]{2,0,1:T(1,128)S(1)}, f32[1,8,2048]{2,0,1:T(1,128)S(1)}, u32[]{:S(2)}, u32[]{:S(2)}) collective-permute-start(f32[1,8,2048]{2,0,1:T(1,128)S(1)} %copy.178), channel_id=1, source_target_pairs={{0,4},{4,8},{8,12},{12,16},{16,20},{20,24},{24,28},{1,5},{5,9},{9,... | collective-permute-start | bytes 196616 | tf_op jit(solution)/shard_map/ppermute | solution.py:27
  7.7 43.7 %copy-start.7 = (s32[16]{0:T(128)}, s32[16]{0:T(128)S(1)}, u32[]{:S(2)}) copy-start(s32[16]{0:T(128)S(1)} %and_select_fusion) | copy-start | bytes 196
  9.8 0.6 copy-start.4
  62.9 6.4 %copy-start.2 = (f32[16,8,2048]{2,1,0:T(8,128)S(1)}, f32[16,8,2048]{2,1,0:T(8,128)}, u32[]{:S(2)}) copy-start(f32[16,8,2048]{2,1,0:T(8,128)} %param.9) | copy-start | bytes 3145732
  63.0 82.8 %collective-permute-start.2 = (f32[18,1,2048]{2,0,1:T(8,128)S(1)}, f32[18,1,2048]{2,0,1:T(8,128)S(1)}, u32[]{:S(2)}, u32[]{:S(2)}) collective-permute-start(f32[18,1,2048]{2,0,1:T(8,128)S(1)} %get-tuple-element.25), channel_id=1, source_target_pairs={{0,1},{1,2},{2,3},{4,5},{5,6},{6,7},{8,9},{9,10},{10,11},{12,13},{... | collective-permute-start | bytes 442376 | tf_op jit(solution)/shard_map/ppermute | solution.py:27
  67.4 78.4 %collective-permute-start.3 = (f32[18,1,2048]{2,0,1:T(8,128)S(1)}, f32[18,1,2048]{2,0,1:T(8,128)S(1)}, u32[]{:S(2)}, u32[]{:S(2)}) collective-permute-start(f32[18,1,2048]{2,0,1:T(8,128)S(1)} %get-tuple-element.26), channel_id=1, source_target_pairs={{1,0},{2,1},{3,2},{5,4},{6,5},{7,6},{9,8},{10,9},{11,10},{13,12},{... | collective-permute-start | bytes 442376 | tf_op jit(solution)/shard_map/ppermute | solution.py:29
  211.5 12.6 %copy-start = (f32[16,8,64,32]{2,3,1,0:T(8,128)}, f32[16,8,64,32]{2,3,1,0:T(8,128)S(1)}, u32[]{:S(2)}) copy-start(f32[16,8,64,32]{2,3,1,0:T(8,128)S(1)} %bitcast_subtract_fusion.1) | copy-start | bytes 3145732
  211.8 19.3 %collective-permute-start.4 = (f32[1,8,2048]{2,1,0:T(8,128)S(1)}, f32[1,8,2048]{2,1,0:T(8,128)S(1)}, u32[]{:S(2)}, u32[]{:S(2)}) collective-permute-start(f32[1,8,2048]{2,1,0:T(8,128)S(1)} %slice.78), channel_id=1, source_target_pairs={{0,4},{4,8},{8,12},{12,16},{16,20},{20,24},{24,28},{1,5},{5,9},{9,... | collective-permute-start | bytes 196616 | tf_op jit(solution)/shard_map/ppermute | solution.py:27
  216.5 134.6 %all-to-all-start = ((s32[32,1,8]{2,1,0:T(1,128)}), s32[32,1,8]{2,1,0:T(1,128)S(1)}, u32[]{:S(2)}, u32[]{:S(2)}) async-start(s32[32,1,8]{2,1,0:T(1,128)} %copy.195), calls=%async_computation | async-start | bytes 32768 | tf_op jit(solution)/shard_map/all_to_all | solution.py:98
  224.3 6.8 %collective-permute-start.5 = (f32[1,8,2048]{2,1,0:T(8,128)S(1)}, f32[1,8,2048]{2,1,0:T(8,128)S(1)}, u32[]{:S(2)}, u32[]{:S(2)}) collective-permute-start(f32[1,8,2048]{2,1,0:T(8,128)S(1)} %slice.80), channel_id=1, source_target_pairs={{4,0},{8,4},{12,8},{16,12},{20,16},{24,20},{28,24},{5,1},{9,5},{13... | collective-permute-start | bytes 196616 | tf_op jit(solution)/shard_map/ppermute | solution.py:29
  231.4 5.7 %collective-permute-start.6 = (f32[18,1,2048]{2,1,0:T(1,128)S(1)}, f32[18,1,2048]{2,1,0:T(1,128)S(1)}, u32[]{:S(2)}, u32[]{:S(2)}) collective-permute-start(f32[18,1,2048]{2,1,0:T(1,128)S(1)} %get-tuple-element.23), channel_id=1, source_target_pairs={{0,1},{1,2},{2,3},{4,5},{5,6},{6,7},{8,9},{9,10},{10,11},{12,13},{... | collective-permute-start | bytes 442376 | tf_op jit(solution)/shard_map/ppermute | solution.py:27
  235.0 6.5 %collective-permute-start.7 = (f32[18,1,2048]{2,1,0:T(1,128)S(1)}, f32[18,1,2048]{2,1,0:T(1,128)S(1)}, u32[]{:S(2)}, u32[]{:S(2)}) collective-permute-start(f32[18,1,2048]{2,1,0:T(1,128)S(1)} %get-tuple-element.24), channel_id=1, source_target_pairs={{1,0},{2,1},{3,2},{5,4},{6,5},{7,6},{9,8},{10,9},{11,10},{13,12},{... | collective-permute-start | bytes 442376 | tf_op jit(solution)/shard_map/ppermute | solution.py:29
  255.0 13.9 %copy-start.1 = (f32[16,8,64,32]{2,3,1,0:T(8,128)S(1)}, f32[16,8,64,32]{2,3,1,0:T(8,128)}, u32[]{:S(2)}) copy-start(f32[16,8,64,32]{2,3,1,0:T(8,128)} %copy-done) | copy-start | bytes 3145732
  346.3 3.6 copy-start.8
  350.3 45.5 %copy-start.5 = (s32[16,8,5]{2,1,0:T(8,128)S(1)}, s32[16,8,5]{2,1,0:T(8,128)}, u32[]{:S(2)}) copy-start(s32[16,8,5]{2,1,0:T(8,128)} %copy-done.4) | copy-start | bytes 7684
  351.1 15.3 %all-to-all-start.1 = ((f32[32,8,256]{2,1,0:T(8,128)}), f32[32,8,256]{2,1,0:T(8,128)S(1)}, u32[]{:S(2)}, u32[]{:S(2)}) async-start(f32[32,8,256]{2,1,0:T(8,128)} %copy.199), calls=%async_computation.1 | async-start | bytes 524288 | tf_op jit(solution)/shard_map/all_to_all | solution.py:97
  391.4 13.2 %all-to-all-start.2 = ((f32[32,8,256]{2,1,0:T(8,128)}), f32[32,8,256]{2,1,0:T(8,128)S(1)}, u32[]{:S(2)}, u32[]{:S(2)}) async-start(f32[32,8,256]{2,1,0:T(8,128)} %fusion.15), calls=%async_computation.2 | async-start | bytes 524288 | tf_op jit(solution)/shard_map/all_to_all | solution.py:104
  412.7 13.4 %collective-permute-start.8 = (f32[1,8,512]{2,1,0:T(8,128)S(1)}, f32[1,8,512]{2,1,0:T(8,128)S(1)}, u32[]{:S(2)}, u32[]{:S(2)}) collective-permute-start(f32[1,8,512]{2,1,0:T(8,128)S(1)} %slice.85), channel_id=1, source_target_pairs={{0,4},{4,8},{8,12},{12,16},{16,20},{20,24},{24,28},{1,5},{5,9},{9,... | collective-permute-start | bytes 49160 | tf_op jit(solution)/shard_map/ppermute | solution.py:27
  418.8 7.4 %collective-permute-start.9 = (f32[1,8,512]{2,1,0:T(8,128)S(1)}, f32[1,8,512]{2,1,0:T(8,128)S(1)}, u32[]{:S(2)}, u32[]{:S(2)}) collective-permute-start(f32[1,8,512]{2,1,0:T(8,128)S(1)} %slice.87), channel_id=1, source_target_pairs={{4,0},{8,4},{12,8},{16,12},{20,16},{24,20},{28,24},{5,1},{9,5},{13... | collective-permute-start | bytes 49160 | tf_op jit(solution)/shard_map/ppermute | solution.py:29
  426.1 60.8 %copy-start.3 = (f32[16,8,512]{2,1,0:T(8,128)}, f32[16,8,512]{2,1,0:T(8,128)S(1)}, u32[]{:S(2)}) copy-start(f32[16,8,512]{2,1,0:T(8,128)S(1)} %reshape.237) | copy-start | bytes 786436
  426.2 68.0 %collective-permute-start.10 = (f32[18,1,512]{2,1,0:T(1,128)S(1)}, f32[18,1,512]{2,1,0:T(1,128)S(1)}, u32[]{:S(2)}, u32[]{:S(2)}) collective-permute-start(f32[18,1,512]{2,1,0:T(1,128)S(1)} %get-tuple-element.31), channel_id=1, source_target_pairs={{0,1},{1,2},{2,3},{4,5},{5,6},{6,7},{8,9},{9,10},{10,11},{12,13},{... | collective-permute-start | bytes 110600 | tf_op jit(solution)/shard_map/ppermute | solution.py:27
  429.4 64.8 %collective-permute-start.11 = (f32[18,1,512]{2,1,0:T(1,128)S(1)}, f32[18,1,512]{2,1,0:T(1,128)S(1)}, u32[]{:S(2)}, u32[]{:S(2)}) collective-permute-start(f32[18,1,512]{2,1,0:T(1,128)S(1)} %get-tuple-element.32), channel_id=1, source_target_pairs={{1,0},{2,1},{3,2},{5,4},{6,5},{7,6},{9,8},{10,9},{11,10},{13,12},{... | collective-permute-start | bytes 110600 | tf_op jit(solution)/shard_map/ppermute | solution.py:29
  431.4 55.5 %copy-start.6 = (pred[16,8,5]{0,1,2:T(8,128)(4,1)S(1)}, pred[16,8,5]{0,1,2:T(8,128)(4,1)}, u32[]{:S(2)}) copy-start(pred[16,8,5]{0,1,2:T(8,128)(4,1)} %get-tuple-element.19) | copy-start | bytes 1924
where the time goes:
time: 573 us; the launch traced here: 562 us
  local copies, waits for them, and re-layouts  285 us (50%)
  matrix products  125 us (22%)
  starting transfers between devices  51.3 us (9%)
  other arithmetic  40.5 us (7%)
  blocking collectives  37.1 us (6%)
  waiting for transfers between devices  20.4 us (4%)
    dot_general x2, matrix products, shards(): jnp.einsum('ijor,ijrw->ijow', block_wide, picked, precision=FULL_PRECISION)  76.2 us
    transpose x1, local copies, waits for them, and re-layouts, shards(): jnp.transpose(blocks, (0, 1, 3, 2, 4))  63.2 us
    reshape x1, local copies, waits for them, and re-layouts, shards(): blocks = a_blocks.reshape(height, across_devices, KS, BLK, BLK)  55.5 us
    unnamed x26, local copies, waits for them, and re-layouts  48.2 us
    dot_general x1, matrix products, shards(): jnp.einsum('ijkoc,ijkcw->ijkow', blocks, picked_tiles, precision=FULL_PRE...  37.9 us
    psum x1, blocking collectives, shards(): totals = lax.psum(squares, ('slab', 'pencil'))  37.1 us
    another operation x2, local copies, waits for them, and re-layouts, shards(): pick_rows(padded, flat_index, height, across_devices)  27.5 us
    gather x4, local copies, waits for them, and re-layouts, pick_rows(): picked = jnp.take(flat, flat_index, axis=0)  24.9 us
  transfers between devices with their start and end apart: 15, of which 4 were waited for; matrix products, arithmetic and copies ran while one was open for 51% of the time, Pallas kernels for 0%

commit v1 on v0

v1 whole, which is shorter than its diff:
```python
import functools
import math

import jax
import jax.numpy as jnp
import numpy as np
from jax import lax
from jax.experimental import pallas as pl
from jax.experimental.pallas import tpu as pltpu
from jax.sharding import PartitionSpec as P

BLK = 64
NV = 32
NC = 8
KS = 5
ITERS = 2
OMEGA = 2.0 / 3.0
LANES = 128
F32 = jnp.float32
BF16 = jnp.bfloat16
PAIRS = BLK // 2
VROWS = BLK * NV // LANES
TROWS = BLK * NC // LANES
VM = pl.BlockSpec(memory_space=pltpu.VMEM)
SM = pl.BlockSpec(memory_space=pltpu.SMEM)
HB = pl.BlockSpec(memory_space=pl.ANY)
LIMIT = 48 * 1024 * 1024


def lane_iota(rows):
    return lax.broadcasted_iota(jnp.int32, (rows, LANES), 1)


def row_iota(rows):
    return lax.broadcasted_iota(jnp.int32, (rows, LANES), 0)


def roll(x, shift):
    return pltpu.roll(x, shift, 1)


def upper(x):
    return x.astype(BF16).astype(F32)


def hi_lo_lanes(x):
    return x - jnp.where(lane_iota(x.shape[0]) < 64, 0.0, upper(x))


def put_weights(pairs, rep_ref, w_ref, index, half):
    low = (lane_iota(PAIRS) & half) == 0
    turned = roll(pairs, half)
    rep_ref[pl.ds(0, PAIRS, stride=2), :] = jnp.where(low, pairs, turned)
    rep_ref[pl.ds(1, PAIRS, stride=2), :] = jnp.where(low, turned, pairs)
    y = hi_lo_lanes(rep_ref[...])
    low = (lane_iota(BLK) & half) == 0
    w_ref[index, 0:BLK, :] = jnp.where(low, y, 0.0).astype(BF16)
    w_ref[index, BLK : 2 * BLK, :] = jnp.where(low, 0.0, y).astype(BF16)


def rows_to_pairs(rows, out_ref, start):
    low = lane_iota(VROWS) < 64
    turned = roll(rows, 64)
    out_ref[pl.ds(start, VROWS, stride=2), :] = jnp.where(low, rows, turned)
    out_ref[pl.ds(start + 1, VROWS, stride=2), :] = jnp.where(low, turned, rows)


def pairs_to_rows(ref, start):
    even = ref[pl.ds(start, VROWS, stride=2), :]
    odd = ref[pl.ds(start + 1, VROWS, stride=2), :]
    return jnp.where(lane_iota(VROWS) < 64, even, odd)


def mm(a, b):
    return jnp.dot(a, b, preferred_element_type=F32)


def fold_rows(parts):
    sub = row_iota(8)
    step = 4
    while len(parts) > 1:
        half = len(parts) // 2
        parts = [
            jnp.where(
                (sub & step) == 0,
                parts[u] + pltpu.roll(parts[u], 8 - step, 0),
                parts[u + half] + pltpu.roll(parts[u + half], step, 0),
            )
            for u in range(half)
        ]
        step //= 2
    return parts[0]


def neighbour(codes_ref, b, i, j, k, wide):
    if k == 0:
        return (i + 1) * wide + j + 1
    c = codes_ref[b * KS + k]
    return (i + c // 3) * wide + j + c % 3


def prepare_kernel(height, across, meta_ref, a_hbm, tv_ref, ones_ref, hl_ref, rd_ref, v_ref, buf, sem):
    tiles = KS * PAIRS
    chunk = tiles * across
    depth = buf.shape[0]

    def copy(i):
        slot = lax.rem(i, depth)
        return pltpu.make_async_copy(
            a_hbm.at[pl.ds(i * chunk, chunk), :], buf.at[slot], sem.at[slot]
        )

    for i in range(depth - 1):
        copy(i).start()
    lane = lane_iota(PAIRS)
    on_diagonal = (lane & 63) == 2 * row_iota(PAIRS) + (lane >> 6)

    def body(i, carry):
        @pl.when(i + depth - 1 < height)
        def _():
            copy(i + depth - 1).start()

        copy(i).wait()
        slot = lax.rem(i, depth)
        for j in range(across):
            b = i * across + j
            rows_to_pairs(
                tv_ref[pl.ds(i * VROWS * across + j, VROWS, stride=across), :], v_ref, b * PAIRS
            )
            for k in range(KS):
                x = buf[slot, pl.ds(k * PAIRS * across + j, PAIRS, stride=across), :]
                hi = x.astype(BF16)
                lo = (x - hi.astype(F32)).astype(BF16)
                hl_ref[b, 0:PAIRS, k * LANES : (k + 1) * LANES] = hi
                hl_ref[b, PAIRS : 2 * PAIRS, k * LANES : (k + 1) * LANES] = lo
                if k == 0:
                    d = jnp.where(on_diagonal, x, 0.0)
                    d_hi = d.astype(BF16)
                    d_lo = (d - d_hi.astype(F32)).astype(BF16)
                    s = mm(jnp.concatenate([d_hi, d_lo], axis=0), ones_ref[...])
                    rd_ref[pl.ds(b * PAIRS, PAIRS), :] = OMEGA / (s[:PAIRS] + s[PAIRS:])
        return carry

    lax.fori_loop(0, height, body, 0)


def halo_slots(meta_ref, height, across):
    slab_odd, pencil_odd = meta_ref[0], meta_ref[1]
    col_a = jnp.where(pencil_odd == 0, across + 1, 0)
    row_a = jnp.where(slab_odd == 0, height + 1, 0)
    return row_a, height + 1 - row_a, col_a, across + 1 - col_a


def sweep_core(height, across, codes_ref, meta_ref, hl_ref, rd_ref, v_ref, halo, w_ref, rep_ref, tmp_ref, store):
    wide = across + 2
    pa_ref, pb_ref, sa_ref, sb_ref = halo
    row_a, row_b, col_a, col_b = halo_slots(meta_ref, height, across)

    def own(i, carry):
        for j in range(across):
            put_weights(
                v_ref[pl.ds((i * across + j) * PAIRS, PAIRS), :],
                rep_ref.at[j], w_ref, (i + 1) * wide + j + 1, NV,
            )
        for s, (ref, col) in enumerate(((pa_ref, col_a), (pb_ref, col_b))):
            rows_to_pairs(ref[pl.ds(i * VROWS, VROWS), :], tmp_ref.at[s], 0)
            put_weights(tmp_ref[s], rep_ref.at[s], w_ref, (i + 1) * wide + col, NV)
        return carry

    lax.fori_loop(0, height, own, 0)
    for s, (ref, row) in enumerate(((sa_ref, row_a), (sb_ref, row_b))):
        for j in range(wide):
            col = j + 1 if j < across else (col_a if j == across else col_b)
            q = (s * wide + j) % across
            rows_to_pairs(ref[j * VROWS : (j + 1) * VROWS, :], tmp_ref.at[q], 0)
            put_weights(tmp_ref[q], rep_ref.at[q], w_ref, row * wide + col, NV)

    def body(i, carry):
        for j in range(across):
            b = i * across + j
            w = jnp.concatenate(
                [w_ref[neighbour(codes_ref, b, i, j, k, wide)] for k in range(KS)], axis=0
            )
            r = mm(hl_ref[b], w)
            s = r[:PAIRS] + r[PAIRS:]
            s = s + roll(s, 64)
            at = pl.ds(b * PAIRS, PAIRS)
            store(i, j, b, v_ref[at, :] - s * rd_ref[at, :])
        return carry

    lax.fori_loop(0, height, body, 0)


def sweep_kernel(height, across, codes_ref, meta_ref, hl_ref, rd_ref, v_ref, pa, pb, sa, sb,
                 out_ref, ea_ref, eb_ref, ra_ref, rb_ref, w_ref, rep_ref, tmp_ref):
    def store(i, j, b, value):
        out_ref[pl.ds(b * PAIRS, PAIRS), :] = value

    sweep_core(height, across, codes_ref, meta_ref, hl_ref, rd_ref, v_ref, (pa, pb, sa, sb),
               w_ref, rep_ref, tmp_ref, store)
    row_a, row_b, col_a, col_b = halo_slots(meta_ref, height, across)

    def edge(i, carry):
        for ref, col in ((ea_ref, col_a), (eb_ref, col_b)):
            j = jnp.where(col == 0, 0, across - 1)
            ref[pl.ds(i * VROWS, VROWS), :] = pairs_to_rows(out_ref, (i * across + j) * PAIRS)
        return carry

    lax.fori_loop(0, height, edge, 0)
    for ref, row in ((ra_ref, row_a), (rb_ref, row_b)):
        i = jnp.where(row == 0, 0, height - 1)
        for j in range(across):
            ref[j * VROWS : (j + 1) * VROWS, :] = pairs_to_rows(out_ref, (i * across + j) * PAIRS)


def last_sweep_kernel(height, across, capacity, codes_ref, meta_ref, owner_ref, hl_ref, rd_ref, v_ref,
                      pa, pb, sa, sb, ids_ref, modes_ref, out_ref, pay_ref, w_ref, rep_ref, tmp_ref,
                      coef_ref):
    devices = ids_ref.shape[0]
    hcount = -(-capacity // 4)
    slot_rows = hcount * NC + 1

    def store(i, j, b, value):
        out_ref[pl.ds(b * PAIRS, PAIRS), :] = value

    sweep_core(height, across, codes_ref, meta_ref, hl_ref, rd_ref, v_ref, (pa, pb, sa, sb),
               w_ref, rep_ref, tmp_ref, store)
    pay_ref[...] = jnp.zeros(pay_ref.shape, F32)
    low = (lane_iota(NC) & NV) == 0
    modes = modes_ref[...]
    group_lane = lane_iota(NC) // NV

    def coefs(i, acc):
        for j in range(across):
            b = i * across + j
            v = out_ref[pl.ds(b * PAIRS, PAIRS), :]
            acc = acc + v * v
            r = mm(modes, hi_lo_lanes(v).astype(BF16))
            c = jnp.where(low, r[0:8] + r[16:24], r[8:16] + r[24:32])
            c = c + roll(c, NV)
            coef_ref[pl.ds(b * NC, NC), :] = c + roll(c, 64)
        return acc

    acc = lax.fori_loop(0, height, coefs, jnp.zeros((PAIRS, LANES), F32))
    total = jnp.sum(acc, axis=0, keepdims=True)
    total = total + roll(total, NV)
    pay_ref[pl.ds(slot_rows - 1, devices, stride=slot_rows), :] = jnp.where(
        lane_iota(devices) < NV, total, ids_ref[...]
    )

    def pack(g, carry):
        owner = owner_ref[g]
        for h in range(hcount):
            parts = [
                coef_ref[pl.ds((g * capacity + h * 4 + s) * NC, NC), :]
                for s in range(min(4, capacity - h * 4))
            ]
            c = jnp.zeros((NC, LANES), F32)
            for s, part in enumerate(parts):
                c = jnp.where(group_lane == s, part, c)
            pay_ref[pl.ds(owner * slot_rows + h * NC, NC), :] = c
        return carry

    lax.fori_loop(0, height * across // capacity, pack, 0)


def solve_kernel(cells, per_owner, capacity, got_ref, ret_ref, inv_ref):
    hcount = -(-capacity // 4)
    slot_rows = hcount * NC + 1
    devices = got_ref.shape[0] // slot_rows
    lane = lane_iota(devices)
    extra = got_ref[pl.ds(slot_rows - 1, devices, stride=slot_rows), :]
    total = jnp.sum(jnp.where(lane < NV, extra, 0.0), axis=0, keepdims=True)
    total = jnp.broadcast_to(total, (8, LANES))
    total = total + roll(total, NV)
    total = total + roll(total, 64)
    inv = 1.0 / jnp.sqrt(total / cells + 1e-06)
    inv_ref[...] = inv
    width = 4 * per_owner
    inner = lane & (width - 1)
    hot = []
    for h in range(hcount):
        want = jnp.full((devices, LANES), -1.0, F32)
        for s in range(min(4, capacity - 4 * h)):
            column = extra[:, NV + 4 * h + s : NV + 4 * h + s + 1]
            want = jnp.where(inner // per_owner == s, column, want)
        same = want == (inner & (per_owner - 1)).astype(F32)
        hot.append(jnp.where(same & (lane < 2 * width), 1.0, 0.0))
    hot = jnp.concatenate(hot, axis=0)
    hot_t = jnp.transpose(hot)[:width]
    parts = [
        jnp.concatenate(
            [got_ref[pl.ds(h * NC + m, devices, stride=slot_rows), :] for h in range(hcount)], axis=0
        )
        for m in range(NC)
    ]
    data = jnp.concatenate(parts, axis=1)
    ones = jnp.ones((hcount * devices, LANES), F32)
    high = jnp.concatenate([data, ones], axis=1).astype(BF16)
    rest = jnp.concatenate([data - upper(data), jnp.zeros_like(ones)], axis=1).astype(BF16)
    hot_b = hot_t.astype(BF16)
    sums = mm(hot_b, high) + mm(hot_b, rest)
    group_lane = lane_iota(per_owner) // NV

    def block(s, m):
        return sums[s * per_owner : (s + 1) * per_owner, m * LANES : (m + 1) * LANES]

    count = sum(block(s, NC) for s in range(4))
    weight = inv[0:1] / jnp.maximum(count, 1.0)
    coarse = []
    for m in range(NC):
        c = jnp.zeros((per_owner, LANES), F32)
        for s in range(4):
            c = jnp.where(group_lane == s, block(s, m), c)
        c = c + roll(c, NV)
        c = c + roll(c, 64)
        coarse.append(c * weight)

    def dot_all(x):
        for shift in (16, 8, 4, 2, 1):
            x = x + roll(x, shift)
        return x

    gram = {(a, c): dot_all(coarse[a] * coarse[c]) for a in range(NC) for c in range(a + 1)}
    ridge = 0.1 * sum(gram[m, m] for m in range(NC)) / NC + 1e-06
    for m in range(NC):
        gram[m, m] = gram[m, m] + ridge
    recip = []
    for m in range(NC):
        root = 1.0 / jnp.sqrt(gram[m, m])
        recip.append(root)
        for a in range(m + 1, NC):
            gram[a, m] = gram[a, m] * root
        for a in range(m + 1, NC):
            for c in range(m + 1, a + 1):
                gram[a, c] = gram[a, c] - gram[a, m] * gram[c, m]
    solved = list(coarse)
    for m in range(NC):
        solved[m] = solved[m] * recip[m]
        for a in range(m + 1, NC):
            solved[a] = solved[a] - gram[a, m] * solved[m]
    for m in reversed(range(NC)):
        solved[m] = solved[m] * recip[m]
        for a in range(m):
            solved[a] = solved[a] - gram[m, a] * solved[m]
    table = jnp.concatenate(
        [
            jnp.concatenate([jnp.where(group_lane == s, solved[m], 0.0) for s in range(4)], axis=0)
            for m in range(NC)
        ],
        axis=1,
    )
    stacked = jnp.concatenate([table.astype(BF16), (table - upper(table)).astype(BF16)], axis=0)
    back = mm(hot[:, : 2 * width].astype(BF16), stacked)
    for h in range(hcount):
        for m in range(NC):
            ret_ref[pl.ds(h * NC + m, devices, stride=hcount * NC), :] = back[
                h * devices : (h + 1) * devices, m * LANES : (m + 1) * LANES
            ]


def relaxed_kernel(height, across, v_ref, inv_ref, rel_ref, left_ref):
    inv = inv_ref[0:1, :]

    def body(i, carry):
        for j in range(across):
            b = i * across + j
            rel_ref[pl.ds(i * VROWS * across + j, VROWS, stride=across), :] = (
                pairs_to_rows(v_ref, b * PAIRS) * inv
            )
            left_ref[b] = hi_lo_lanes(v_ref[pl.ds(b * PAIRS, PAIRS), :] * inv).astype(BF16)
        return carry

    lax.fori_loop(0, height, body, 0)


def tile_kernel(height, across, capacity, meta_ref, owner_ref, ret_ref, left_ref,
                pairs_ref, out_ref, ea_ref, eb_ref, ra_ref, rb_ref):
    hcount = -(-capacity // 4)
    low = (lane_iota(NC) & NV) == 0
    group_lane = lane_iota(NC) // NV
    picks = lane_iota(8) // 16 == row_iota(8)

    def body(i, carry):
        tiles = []
        for j in range(across):
            b = i * across + j
            g = b // capacity
            inner = b - g * capacity
            owner = owner_ref[g]
            h, s = inner // 4, inner % 4
            m = ret_ref[pl.ds(pl.multiple_of((owner * hcount + h) * NC, NC), NC), :]
            m = jnp.where(group_lane == s, m, 0.0)
            m = m + roll(m, NV)
            m = m + roll(m, 64)
            m_hi = upper(m)
            halves = []
            for part in (m_hi, m - m_hi):
                both = jnp.concatenate(
                    [jnp.where(low, part, 0.0), jnp.where(low, 0.0, part)], axis=0
                ).astype(BF16)
                halves.append(jnp.concatenate([both] * 8, axis=0))
            left = left_ref[b]
            t = lax.dot_general(
                jnp.concatenate([left, left], axis=1),
                jnp.concatenate(halves, axis=1),
                (((1,), (1,)), ((), ())),
                preferred_element_type=F32,
            )
            pairs_ref[pl.ds(b * PAIRS, PAIRS), :] = t
            tiles.append(t)
        for q in range(TROWS):
            rows = fold_rows([jnp.where(picks, t[q * 8 : (q + 1) * 8], 0.0) for t in tiles])
            out_ref[pl.ds((i * TROWS + q) * across, across), :] = rows
        return carry

    lax.fori_loop(0, height, body, 0)
    row_a, row_b, col_a, col_b = halo_slots(meta_ref, height, across)
    for ref, col in ((ea_ref, col_a), (eb_ref, col_b)):
        j = jnp.where(col == 0, 0, across - 1)
        ref[...] = out_ref[pl.ds(j, height * TROWS, stride=across), :]
    for ref, row in ((ra_ref, row_a), (rb_ref, row_b)):
        i = jnp.where(row == 0, 0, height - 1)
        ref[...] = out_ref[pl.ds(pl.multiple_of(i * TROWS * across, 8), TROWS * across), :]


def product_kernel(height, across, codes_ref, meta_ref, hl_ref, pairs_ref, pa_ref, pb_ref, sa_ref, sb_ref,
                   out_ref, w_ref, rep_ref):
    wide = across + 2
    row_a, row_b, col_a, col_b = halo_slots(meta_ref, height, across)
    picks = lane_iota(8) // 16 == row_iota(8)

    def spread(rows):
        parts = []
        for row in rows:
            x = jnp.where(picks, row, 0.0)
            for shift in (16, 32, 64):
                x = x + roll(x, shift)
            parts.append(x)
        return jnp.concatenate(parts, axis=0)

    def own(i, carry):
        for j in range(across):
            put_weights(
                pairs_ref[pl.ds((i * across + j) * PAIRS, PAIRS), :],
                rep_ref.at[j], w_ref, (i + 1) * wide + j + 1, NC,
            )
        for s, (ref, col) in enumerate(((pa_ref, col_a), (pb_ref, col_b))):
            rows = spread([ref[pl.ds(i * TROWS + q, 1), :] for q in range(TROWS)])
            put_weights(rows, rep_ref.at[s], w_ref, (i + 1) * wide + col, NC)
        return carry

    lax.fori_loop(0, height, own, 0)
    for s, (ref, row) in enumerate(((sa_ref, row_a), (sb_ref, row_b))):
        for j in range(wide):
            if j < across:
                col, rows = j + 1, [ref[q * across + j : q * across + j + 1, :] for q in range(TROWS)]
            else:
                col = col_a if j == across else col_b
                at = TROWS * j
                rows = [ref[at + q : at + q + 1, :] for q in range(TROWS)]
            put_weights(spread(rows), rep_ref.at[(s * wide + j) % across], w_ref, row * wide + col, NC)

    def body(i, carry):
        for k in range(KS):
            folded = [[] for _ in range(TROWS)]
            for j in range(across):
                b = i * across + j
                r = mm(
                    hl_ref[b, :, k * LANES : (k + 1) * LANES],
                    w_ref[neighbour(codes_ref, b, i, j, k, wide)],
                )
                x = r[:PAIRS] + r[PAIRS:]
                x = x + roll(x, 64)
                for q in range(TROWS):
                    folded[q].append(jnp.where(picks, x[q * 8 : (q + 1) * 8], 0.0))
            for q in range(TROWS):
                at = pl.multiple_of(((i * KS + k) * TROWS + q) * across, 8)
                out_ref[pl.ds(at, across), :] = fold_rows(folded[q])
        return carry

    lax.fori_loop(0, height, body, 0)


def swaps(count, first):
    pairs = [(i, i + 1) for i in range(first, count - 1, 2)]
    return pairs + [(b, a) for a, b in pairs]


def exchange(edges, rows, slab_odd, unit, height):
    pencils, slabs = lax.axis_size("pencil"), lax.axis_size("slab")
    got = [lax.ppermute(e, "pencil", swaps(pencils, s)) for s, e in enumerate(edges)]
    out = []
    for s, own in enumerate(rows):
        last = (slab_odd == 0) if s == 0 else (slab_odd == 1)
        corners = [
            jnp.where(last, g[(height - 1) * unit : height * unit], g[:unit]) for g in got
        ]
        out.append(
            lax.ppermute(jnp.concatenate([own] + corners, axis=0), "slab", swaps(slabs, s))
        )
    return got + out


def lines(x, features):
    height, across, _ = x.shape
    y = x.reshape(height, across, features // LANES, LANES).transpose(0, 2, 1, 3)
    return y.reshape(height * across * features // LANES, LANES)


def unlines(y, height, across, features):
    x = y.reshape(height, features // LANES, across, LANES).transpose(0, 2, 1, 3)
    return x.reshape(height, across, features)


def call(kernel, outs, ins, scratch=(), limit=LIMIT, specs=None):
    return pl.pallas_call(
        kernel,
        out_shape=outs,
        in_specs=specs,
        out_specs=[VM] * len(outs),
        scratch_shapes=list(scratch),
        compiler_params=pltpu.CompilerParams(vmem_limit_bytes=limit),
    )(*ins)


def sds(*shape, dtype=F32):
    return jax.ShapeDtypeStruct(shape, dtype)


def mode_table():
    centre = np.arange(BLK, dtype=np.float64) + 0.5
    q = np.cos(math.pi * centre[:, None] * np.arange(NC)[None, :] / BLK).astype(np.float32)
    return q


def shards(a_blocks, col_codes, agg_of, test_vectors):
    height, across = agg_of.shape
    slabs, pencils = lax.axis_size("slab"), lax.axis_size("pencil")
    devices = slabs * pencils
    block_rows = height * across
    capacity = 2 * block_rows // devices
    groups = devices // 2
    per_owner = block_rows // 8
    hcount = -(-capacity // 4)
    wide = across + 2
    slab_odd = lax.axis_index("slab") % 2
    pencil_odd = lax.axis_index("pencil") % 2
    meta = jnp.stack([slab_odd, pencil_odd]).astype(jnp.int32)
    codes = col_codes.reshape(block_rows * KS)
    group_agg = agg_of.reshape(groups, capacity)
    owner = (group_agg[:, 0] // per_owner).astype(jnp.int32)
    chosen = owner[None, :] == jnp.arange(devices, dtype=jnp.int32)[:, None]
    slot_ids = (
        jnp.sum(jnp.where(chosen[:, :, None], group_agg[None] % per_owner + 1, 0), axis=1) - 1
    ).astype(F32)
    ids = jnp.pad(slot_ids, ((0, 0), (NV, LANES - NV - capacity)))

    tv = lines(test_vectors, BLK * NV)
    by_row = test_vectors.reshape(height, across, VROWS, LANES)
    col_hi, col_lo = by_row[:, across - 1], by_row[:, 0]
    row_hi, row_lo = by_row[height - 1], by_row[0]
    flip = lambda odd, a, b: (jnp.where(odd == 0, a, b), jnp.where(odd == 0, b, a))
    edges = [e.reshape(height * VROWS, LANES) for e in flip(pencil_odd, col_hi, col_lo)]
    rows = [e.reshape(across * VROWS, LANES) for e in flip(slab_odd, row_hi, row_lo)]
    halo = exchange(edges, rows, slab_odd, VROWS, height)

    lane = np.arange(LANES)
    ones = jnp.asarray((lane[:, None] // 64) == (lane[None, :] // 32) % 2, BF16)
    chunk = KS * PAIRS * across
    hl, rd, v = call(
        functools.partial(prepare_kernel, height, across),
        [sds(block_rows, 2 * PAIRS, KS * LANES, dtype=BF16), sds(block_rows * PAIRS, LANES), sds(block_rows * PAIRS, LANES)],
        [meta, lines(a_blocks, KS * BLK * BLK), tv, ones],
        [pltpu.VMEM((4, chunk, LANES), F32), pltpu.SemaphoreType.DMA((4,))],
        specs=[SM, HB, VM, VM],
    )
    work = [
        pltpu.VMEM((wide * (height + 2), 2 * BLK, LANES), BF16),
        pltpu.VMEM((across, BLK, LANES), F32),
        pltpu.VMEM((across, PAIRS, LANES), F32),
    ]
    v, ea, eb, ra, rb = call(
        functools.partial(sweep_kernel, height, across),
        [sds(block_rows * PAIRS, LANES)] + [sds(height * VROWS, LANES)] * 2 + [sds(across * VROWS, LANES)] * 2,
        [codes, meta, hl, rd, v, *halo],
        work,
        specs=[SM, SM] + [VM] * 7,
    )
    halo = exchange([ea, eb], [ra, rb], slab_odd, VROWS, height)
    q = mode_table()
    q01 = np.concatenate([q[0::2].T, q[1::2].T], axis=0)
    q_hi = jnp.asarray(q01).astype(BF16)
    q_lo = (jnp.asarray(q01) - q_hi.astype(F32)).astype(BF16)
    modes = jnp.concatenate([q_hi, q_lo], axis=0)
    slot_rows = hcount * NC + 1
    v, pay = call(
        functools.partial(last_sweep_kernel, height, across, capacity),
        [sds(block_rows * PAIRS, LANES), sds(devices * slot_rows, LANES)],
        [codes, meta, owner, hl, rd, v, *halo, ids, modes],
        work + [pltpu.VMEM((block_rows * NC, LANES), F32)],
        specs=[SM, SM, SM] + [VM] * 9,
    )
    got = lax.all_to_all(
        pay.reshape(devices, slot_rows * LANES), ("slab", "pencil"), split_axis=0, concat_axis=0, tiled=True
    ).reshape(devices * slot_rows, LANES)
    ret, inv = call(
        functools.partial(solve_kernel, float(block_rows * BLK * devices), per_owner, capacity),
        [sds(devices * hcount * NC, LANES), sds(8, LANES)],
        [got],
        specs=[VM],
    )
    back = lax.all_to_all(
        ret.reshape(devices, hcount * NC * LANES), ("slab", "pencil"), split_axis=0, concat_axis=0, tiled=True
    ).reshape(devices * hcount * NC, LANES)
    relaxed, left = call(
        functools.partial(relaxed_kernel, height, across),
        [sds(block_rows * VROWS, LANES), sds(block_rows, PAIRS, LANES, dtype=BF16)],
        [v, inv],
        specs=[VM, VM],
    )
    pairs, tiles, ea, eb, ra, rb = call(
        functools.partial(tile_kernel, height, across, capacity),
        [sds(block_rows * PAIRS, LANES), sds(block_rows * TROWS, LANES)]
        + [sds(height * TROWS, LANES)] * 2 + [sds(across * TROWS, LANES)] * 2,
        [meta, owner, back, left],
        specs=[SM, SM, VM, VM],
    )
    halo = exchange([ea, eb], [ra, rb], slab_odd, TROWS, height)
    (products,) = call(
        functools.partial(product_kernel, height, across),
        [sds(block_rows * KS * TROWS, LANES)],
        [codes, meta, hl, pairs, *halo],
        work[:2],
        specs=[SM, SM] + [VM] * 6,
    )
    return (
        unlines(relaxed, height, across, BLK * NV),
        unlines(tiles, height, across, BLK * NC),
        unlines(products, height, across, KS * BLK * NC),
    )


def solution(mesh):
    in_specs = (P("slab", "pencil", None), P("slab", "pencil", None), P("slab", "pencil"), P("slab", "pencil", None))
    out_specs = (P("slab", "pencil", None),) * 3
    return jax.shard_map(shards, mesh=mesh, in_specs=in_specs, out_specs=out_specs, check_vma=False)
```

time: 573 us -> 154 us (0.27); the launches traced: 562 us -> 153 us
  local copies, waits for them, and re-layouts: 285 us -> 8.88 us
  matrix products: 125 us -> 0 us
  Pallas kernels: 0 us -> 81.4 us
  other arithmetic: 40.5 us -> 2.63 us
  starting transfers between devices: 51.3 us -> 26.1 us
  blocking collectives: 37.1 us -> 15.3 us
    dot_general x10 -> x0, matrix products: 125 us -> none  [the longest x2 76.2 us: shards(): jnp.einsum('ijor,ijrw->ijow', block_wide, picked, precision=FULL_PRECISION)]
    pallas_call x0 -> x7, Pallas kernels: none -> 81.4 us  [call(): pl.pallas_call(kernel, out_shape=outs, in_specs=specs, out_specs=[VM] * l...]
    reshape x11 -> x1, local copies, waits for them, and re-layouts: 78.3 us -> 0.2 us  [shards(): codes = col_codes.reshape(block_rows * KS)]
    transpose x2 -> x0, local copies, waits for them, and re-layouts: 63.4 us -> none  [the longest x1 63.2 us: shards(): jnp.transpose(blocks, (0, 1, 3, 2, 4))]
    unnamed x26 -> x15, local copies, waits for them, and re-layouts: 48.2 us -> 6.51 us
    psum x1 -> x0, blocking collectives: 37.1 us -> none  [shards(): totals = lax.psum(squares, ('slab', 'pencil'))]
    gather x6 -> x0, local copies, waits for them, and re-layouts: 31.5 us -> none  [the longest x4 24.9 us: pick_rows(): picked = jnp.take(flat, flat_index, axis=0)]
    another operation x6 -> x0, local copies, waits for them, and re-layouts: 30.5 us -> none  [the longest x2 27.5 us: shards(): pick_rows(padded, flat_index, height, across_devices)]
  transfers between devices with their start and end apart: 15 -> 13, of which waited for: 4 -> 7; matrix products, arithmetic and copies ran while one was open for 51% -> 3% of each run, Pallas kernels for 0% -> 9%
where the time goes in v1:
time: 154 us; the launch traced here: 153 us
  Pallas kernels  81.4 us (53%)
  starting transfers between devices  26.1 us (17%)
  waiting for transfers between devices  17.3 us (11%)
  blocking collectives  15.3 us (10%)
  local copies, waits for them, and re-layouts  8.88 us (6%)
  other arithmetic  2.63 us (2%)
    pallas_call x7, Pallas kernels, call(): pl.pallas_call(kernel, out_shape=outs, in_specs=specs, out_specs=[VM] * l...  81.4 us
    all_to_all x1, blocking collectives, shards(): lax.all_to_all(pay.reshape(devices, slot_rows * LANES), ('slab', 'pencil'...  15.3 us
    ppermute x6, starting transfers between devices, exchange(): lax.ppermute(jnp.concatenate([own] + corners, axis=0), 'slab', swaps(slab...  10.9 us
    ppermute x6, starting transfers between devices, exchange(): lax.ppermute(e, 'pencil', swaps(pencils, s))  10.6 us
    unnamed x15, local copies, waits for them, and re-layouts  6.51 us
    ppermute x6, waiting for transfers between devices, exchange(): lax.ppermute(e, 'pencil', swaps(pencils, s))  6.01 us
    all_to_all x1, waiting for transfers between devices, shards(): lax.all_to_all(ret.reshape(devices, hcount * NC * LANES), ('slab', 'penci...  5.71 us
    ppermute x6, waiting for transfers between devices, exchange(): lax.ppermute(jnp.concatenate([own] + corners, axis=0), 'slab', swaps(slab...  5.58 us
  transfers between devices with their start and end apart: 13, of which 7 were waited for; matrix products, arithmetic and copies ran while one was open for 3% of the time, Pallas kernels for 9%

profile of v1, /device:TPU:9, one launch (start us, length us, event | category | flops | bytes accessed | tf_op | source)
XLA Modules:
  0.0 152.6 jit_solution(18060220901961757335)
XLA Ops:
  0.7 1.9 %fusion.2 = (f32[16,1,16,128]{3,1,2,0:T(1,128)S(1)}, f32[16,1,16,128]{3,1,2,0:T(1,128)S(1)}) fusion(f32[16,8,16,128]{3,1,2,0:T(8,128)} %bitcast.43), kind=kLoop, calls=%fused_computation.36 | loop fusion | bytes 524288 | tf_op jit(solution)/shard_map/slice | solution.py:561
  2.6 0.7 collective-permute-start
  3.4 3.0 %collective-permute-start.1 = (f32[256,128]{1,0:T(8,128)S(1)}, f32[256,128]{1,0:T(8,128)S(1)}, u32[]{:S(2)}, u32[]{:S(2)}) collective-permute-start(f32[256,128]{1,0:T(8,128)S(1)} %bitcast.52), channel_id=1, source_target_pairs={{1,2},{2,1},{5,6},{6,5},{9,10},{10,9},{13,14},{14,13},{17,18},{18,... | collective-permute-start | bytes 393224 | tf_op jit(solution)/shard_map/ppermute | solution.py:492
  6.4 0.9 slice_select_fusion
  7.4 0.9 copy.29
  8.4 0.7 fusion.1
  9.9 1.3 collective-permute-start.2
  11.2 2.0 %collective-permute-start.3 = (f32[160,128]{1,0:T(8,128)S(1)}, f32[160,128]{1,0:T(8,128)S(1)}, u32[]{:S(2)}, u32[]{:S(2)}) collective-permute-start(f32[160,128]{1,0:T(8,128)S(1)} %pad_maximum_fusion.1), channel_id=1, source_target_pairs={{4,8},{12,16},{20,24},{8,4},{16,12},{24,20},{5,9},{13,17},{21,25},... | collective-permute-start | bytes 245768 | tf_op jit(solution)/shard_map/ppermute | solution.py:500
  13.3 11.5 %shard_map.85 = (bf16[128,64,640]{2,1,0:T(8,128)(2,1)}, f32[4096,128]{1,0:T(8,128)S(1)}, f32[4096,128]{1,0:T(8,128)S(1)}) custom-call(s32[2]{0:T(128)S(1)} %pad_add_fusion.meta_ref, f32[20480,128]{1,0:T(8,128)} %bitcast.48, f32[2048,128]{1,0:T(8,128)S(1)} %bitcast.44, bf16[128,128]{1,0:T(8,128)(2,1)S(1)} %copy-done.5), custom_call_target="tpu_custom_call" | custom-call | tf_op jit(solution)/shard_map/pallas_call | solution.py:517
  24.8 1.4 copy-done.1
  26.2 16.3 %shard_map.86 = (f32[4096,128]{1,0:T(8,128)S(1)}, f32[256,128]{1,0:T(8,128)S(1)}, f32[256,128]{1,0:T(8,128)S(1)}, f32[128,128]{1,0:T(8,128)S(1)}, f32[128,128]{1,0:T(8,128)S(1)}) custom-call(s32[640]{0:T(1024)S(1)} %reshape.135.codes_ref, s32[2]{0:T(128)S(1)} %pad_add_fusion.meta_ref, bf16[128,64,640]{2,1,0:T(8,128)(2,1)} %get-tuple-element.23.hl_ref, ...), custom_call_target="tpu_custom_call" | custom-call | tf_op jit(solution)/shard_map/pallas_call | solution.py:517
  42.5 1.4 copy-done
  44.2 3.4 %collective-permute-start.5 = (f32[256,128]{1,0:T(8,128)S(1)}, f32[256,128]{1,0:T(8,128)S(1)}, u32[]{:S(2)}, u32[]{:S(2)}) collective-permute-start(f32[256,128]{1,0:T(8,128)S(1)} %get-tuple-element.28), channel_id=1, source_target_pairs={{1,2},{2,1},{5,6},{6,5},{9,10},{10,9},{13,14},{14,13},{17,18},{18,... | collective-permute-start | bytes 393224 | tf_op jit(solution)/shard_map/ppermute | solution.py:492
  47.6 2.9 %collective-permute-done.5.pb = f32[256,128]{1,0:T(8,128)S(1)} collective-permute-done((f32[256,128]{1,0:T(8,128)S(1)}, f32[256,128]{1,0:T(8,128)S(1)}, u32[]{:S(2)}, u32[]{:S(2)}) %collective-permute-start.5) | collective-permute-done | bytes 131104 | tf_op jit(solution)/shard_map/ppermute | solution.py:492
  50.5 4.1 %collective-permute-start.7 = (f32[160,128]{1,0:T(8,128)S(1)}, f32[160,128]{1,0:T(8,128)S(1)}, u32[]{:S(2)}, u32[]{:S(2)}) collective-permute-start(f32[160,128]{1,0:T(8,128)S(1)} %pad_maximum_fusion.3), channel_id=1, source_target_pairs={{4,8},{12,16},{20,24},{8,4},{16,12},{24,20},{5,9},{13,17},{21,25},... | collective-permute-start | bytes 245768 | tf_op jit(solution)/shard_map/ppermute | solution.py:500
  55.0 1.5 collective-permute-done.7.sb
  56.6 1.4 collective-permute-done.6.sa
  58.0 21.0 %shard_map.87 = (f32[4096,128]{1,0:T(8,128)S(1)}, f32[544,128]{1,0:T(8,128)S(1)}) custom-call(s32[640]{0:T(1024)S(1)} %reshape.135.codes_ref, s32[2]{0:T(128)S(1)} %pad_add_fusion.meta_ref, s32[16]{0:T(128)S(1)} %and_select_fusion.owner_ref, bf16[128,64,640]{2,1,0:T(8,128)(2,1)} %get-tuple-element.23.hl_ref, f32[4096,128]{1,0:T(8,128)S(1)} %get-tuple-element.24.rd_ref, ...), custom_call_target="tpu_custom_call" | custom-call | tf_op jit(solution)/shard_map/pallas_call | solution.py:517
  79.0 1.4 copy-done.2
  80.3 15.3 %all_to_all.18 = f32[32,1,2176]{2,1,0:T(1,128)S(1)} all-to-all(f32[32,1,2176]{2,1,0:T(1,128)S(1)} %bitcast.47), channel_id=1, replica_groups=mesh['slab'=8,'pencil'=4] {'slab','pencil'}, dimensions={0} | all-to-all | bytes 557056 | tf_op jit(solution)/shard_map/all_to_all | solution.py:604
  95.6 2.0 %shard_map.88 = (f32[512,128]{1,0:T(8,128)}, f32[8,128]{1,0:T(8,128)S(1)}) custom-call(f32[544,128]{1,0:T(8,128)S(1)} %bitcast.45), custom_call_target="tpu_custom_call" | custom-call | tf_op jit(solution)/shard_map/pallas_call | solution.py:517
  97.7 4.6 %all-to-all-start.1 = ((f32[32,1,2048]{2,1,0:T(1,128)}), f32[32,1,2048]{2,1,0:T(1,128)S(1)}, u32[]{:S(2)}, u32[]{:S(2)}) async-start(f32[32,1,2048]{2,1,0:T(1,128)} %bitcast.16), calls=%async_computation.1 | async-start | bytes 524288 | tf_op jit(solution)/shard_map/all_to_all | solution.py:613
  102.3 1.6 %copy-done.3 = f32[4096,128]{1,0:T(8,128)S(1)} copy-done((f32[4096,128]{1,0:T(8,128)S(1)}, f32[4096,128]{1,0:T(8,128)}, u32[]{:S(2)}) %copy-start.3) | copy-done | bytes 2097176
  103.8 1.5 shard_map.89
  105.3 5.7 %all-to-all-done.1 = f32[32,1,2048]{2,1,0:T(1,128)S(1)} async-done(((f32[32,1,2048]{2,1,0:T(1,128)}), f32[32,1,2048]{2,1,0:T(1,128)S(1)}, u32[]{:S(2)}, u32[]{:S(2)}) %all-to-all-start.1) | async-done | bytes 262176 | tf_op jit(solution)/shard_map/all_to_all | solution.py:613
  111.0 8.2 %shard_map.90 = (f32[4096,128]{1,0:T(8,128)S(1)}, f32[512,128]{1,0:T(8,128)}, f32[64,128]{1,0:T(8,128)S(1)}, f32[64,128]{1,0:T(8,128)S(1)}, f32[32,128]{1,0:T(8,128)S(1)}, /*index=5*/f32[32,128]{1,0:T(8,128)S(1)}) custom-call(s32[2]{0:T(128)S(1)} %pad_add_fusion.meta_ref, s32[16]{0:T(128)S(1)} %and_select_fusion.owner_ref, f32[512,128]{1,0:T(8,128)S(1)} %bitcast.46, ...), custom_call_target="tpu_custom_call" | custom-call | tf_op jit(solution)/shard_map/pallas_call | solution.py:517
  119.2 1.4 collective-permute-start.8
  120.6 2.1 %collective-permute-start.9 = (f32[64,128]{1,0:T(8,128)S(1)}, f32[64,128]{1,0:T(8,128)S(1)}, u32[]{:S(2)}, u32[]{:S(2)}) collective-permute-start(f32[64,128]{1,0:T(8,128)S(1)} %get-tuple-element.40), channel_id=1, source_target_pairs={{1,2},{2,1},{5,6},{6,5},{9,10},{10,9},{13,14},{14,13},{17,18},{18,... | collective-permute-start | bytes 98312 | tf_op jit(solution)/shard_map/ppermute | solution.py:492
  122.7 3.1 %collective-permute-done.9.pb_ref = f32[64,128]{1,0:T(8,128)S(1)} collective-permute-done((f32[64,128]{1,0:T(8,128)S(1)}, f32[64,128]{1,0:T(8,128)S(1)}, u32[]{:S(2)}, u32[]{:S(2)}) %collective-permute-start.9) | collective-permute-done | bytes 32800 | tf_op jit(solution)/shard_map/ppermute | solution.py:492
  125.9 3.1 %collective-permute-start.11 = (f32[40,128]{1,0:T(8,128)S(1)}, f32[40,128]{1,0:T(8,128)S(1)}, u32[]{:S(2)}, u32[]{:S(2)}) collective-permute-start(f32[40,128]{1,0:T(8,128)S(1)} %pad_maximum_fusion.5), channel_id=1, source_target_pairs={{4,8},{12,16},{20,24},{8,4},{16,12},{24,20},{5,9},{13,17},{21,25},... | collective-permute-start | bytes 61448 | tf_op jit(solution)/shard_map/ppermute | solution.py:500
  129.0 2.2 %collective-permute-done.11.sb_ref = f32[40,128]{1,0:T(8,128)S(1)} collective-permute-done((f32[40,128]{1,0:T(8,128)S(1)}, f32[40,128]{1,0:T(8,128)S(1)}, u32[]{:S(2)}, u32[]{:S(2)}) %collective-permute-start.11) | collective-permute-done | bytes 20512 | tf_op jit(solution)/shard_map/ppermute | solution.py:500
  131.7 21.0 %shard_map.91 = f32[2560,128]{1,0:T(8,128)} custom-call(s32[640]{0:T(1024)S(1)} %reshape.135.codes_ref, s32[2]{0:T(128)S(1)} %pad_add_fusion.meta_ref, bf16[128,64,640]{2,1,0:T(8,128)(2,1)} %get-tuple-element.23.hl_ref, f32[4096,128]{1,0:T(8,128)S(1)} %get-tuple-element.38.pairs_ref, f32[64,128]{1,0:T(8,128)S(1)} %collective-permute-done.8.pa_ref, ...), custom_call_target="tpu_custom_call" | custom-call | tf_op jit(solution)/shard_map/pallas_call | solution.py:517
  (44 shorter events, 2.3 us)
Async XLA Ops:
  0.6 12.7 %copy-start.5 = (bf16[128,128]{1,0:T(8,128)(2,1)S(1)}, bf16[128,128]{1,0:T(8,128)(2,1)}, u32[]{:S(2)}) copy-start(bf16[128,128]{1,0:T(8,128)(2,1)} %constant.63.clone.ones_ref) | copy-start | bytes 98308
  0.6 12.6 %copy-start.4 = (f32[16,8,2048]{2,1,0:T(8,128)S(1)}, f32[16,8,2048]{2,1,0:T(8,128)}, u32[]{:S(2)}) copy-start(f32[16,8,2048]{2,1,0:T(8,128)} %param.9) | copy-start | bytes 3145732
  2.6 7.2 %collective-permute-start = (f32[256,128]{1,0:T(8,128)S(1)}, f32[256,128]{1,0:T(8,128)S(1)}, u32[]{:S(2)}, u32[]{:S(2)}) collective-permute-start(f32[256,128]{1,0:T(8,128)S(1)} %bitcast.53), channel_id=1, source_target_pairs={{0,1},{2,3},{1,0},{3,2},{4,5},{6,7},{5,4},{7,6},{8,9},{10,11},{9,8... | collective-permute-start | bytes 393224 | tf_op jit(solution)/shard_map/ppermute | solution.py:492
  3.4 6.5 %collective-permute-start.1 = (f32[256,128]{1,0:T(8,128)S(1)}, f32[256,128]{1,0:T(8,128)S(1)}, u32[]{:S(2)}, u32[]{:S(2)}) collective-permute-start(f32[256,128]{1,0:T(8,128)S(1)} %bitcast.52), channel_id=1, source_target_pairs={{1,2},{2,1},{5,6},{6,5},{9,10},{10,9},{13,14},{14,13},{17,18},{18,... | collective-permute-start | bytes 393224 | tf_op jit(solution)/shard_map/ppermute | solution.py:492
  9.9 16.3 %collective-permute-start.2 = (f32[160,128]{1,0:T(8,128)S(1)}, f32[160,128]{1,0:T(8,128)S(1)}, u32[]{:S(2)}, u32[]{:S(2)}) collective-permute-start(f32[160,128]{1,0:T(8,128)S(1)} %pad_maximum_fusion), channel_id=1, source_target_pairs={{0,4},{8,12},{16,20},{24,28},{4,0},{12,8},{20,16},{28,24},{1,5},{9... | collective-permute-start | bytes 245768 | tf_op jit(solution)/shard_map/ppermute | solution.py:500
  11.2 15.0 %collective-permute-start.3 = (f32[160,128]{1,0:T(8,128)S(1)}, f32[160,128]{1,0:T(8,128)S(1)}, u32[]{:S(2)}, u32[]{:S(2)}) collective-permute-start(f32[160,128]{1,0:T(8,128)S(1)} %pad_maximum_fusion.1), channel_id=1, source_target_pairs={{4,8},{12,16},{20,24},{8,4},{16,12},{24,20},{5,9},{13,17},{21,25},... | collective-permute-start | bytes 245768 | tf_op jit(solution)/shard_map/ppermute | solution.py:500
  24.8 1.4 copy-start.1
  26.2 31.8 %copy-start.6 = (bf16[32,32]{1,0:T(8,128)(2,1)S(1)}, bf16[32,32]{1,0:T(8,128)(2,1)}, u32[]{:S(2)}) copy-start(bf16[32,32]{1,0:T(8,128)(2,1)} %constant.71.modes_ref) | copy-start | bytes 6148
  42.5 1.4 copy-start
  43.9 3.7 %collective-permute-start.4 = (f32[256,128]{1,0:T(8,128)S(1)}, f32[256,128]{1,0:T(8,128)S(1)}, u32[]{:S(2)}, u32[]{:S(2)}) collective-permute-start(f32[256,128]{1,0:T(8,128)S(1)} %get-tuple-element.27), channel_id=1, source_target_pairs={{0,1},{2,3},{1,0},{3,2},{4,5},{6,7},{5,4},{7,6},{8,9},{10,11},{9,8... | collective-permute-start | bytes 393224 | tf_op jit(solution)/shard_map/ppermute | solution.py:492
  44.2 6.3 %collective-permute-start.5 = (f32[256,128]{1,0:T(8,128)S(1)}, f32[256,128]{1,0:T(8,128)S(1)}, u32[]{:S(2)}, u32[]{:S(2)}) collective-permute-start(f32[256,128]{1,0:T(8,128)S(1)} %get-tuple-element.28), channel_id=1, source_target_pairs={{1,2},{2,1},{5,6},{6,5},{9,10},{10,9},{13,14},{14,13},{17,18},{18,... | collective-permute-start | bytes 393224 | tf_op jit(solution)/shard_map/ppermute | solution.py:492
  50.5 6.1 %collective-permute-start.7 = (f32[160,128]{1,0:T(8,128)S(1)}, f32[160,128]{1,0:T(8,128)S(1)}, u32[]{:S(2)}, u32[]{:S(2)}) collective-permute-start(f32[160,128]{1,0:T(8,128)S(1)} %pad_maximum_fusion.3), channel_id=1, source_target_pairs={{4,8},{12,16},{20,24},{8,4},{16,12},{24,20},{5,9},{13,17},{21,25},... | collective-permute-start | bytes 245768 | tf_op jit(solution)/shard_map/ppermute | solution.py:500
  54.6 3.4 %collective-permute-start.6 = (f32[160,128]{1,0:T(8,128)S(1)}, f32[160,128]{1,0:T(8,128)S(1)}, u32[]{:S(2)}, u32[]{:S(2)}) collective-permute-start(f32[160,128]{1,0:T(8,128)S(1)} %pad_maximum_fusion.2), channel_id=1, source_target_pairs={{0,4},{8,12},{16,20},{24,28},{4,0},{12,8},{20,16},{28,24},{1,5},{9... | collective-permute-start | bytes 245768 | tf_op jit(solution)/shard_map/ppermute | solution.py:500
  79.0 1.4 copy-start.2
  97.7 13.4 %all-to-all-start.1 = ((f32[32,1,2048]{2,1,0:T(1,128)}), f32[32,1,2048]{2,1,0:T(1,128)S(1)}, u32[]{:S(2)}, u32[]{:S(2)}) async-start(f32[32,1,2048]{2,1,0:T(1,128)} %bitcast.16), calls=%async_computation.1 | async-start | bytes 524288 | tf_op jit(solution)/shard_map/all_to_all | solution.py:613
  102.3 1.6 %copy-start.3 = (f32[4096,128]{1,0:T(8,128)S(1)}, f32[4096,128]{1,0:T(8,128)}, u32[]{:S(2)}) copy-start(f32[4096,128]{1,0:T(8,128)} %copy-done.2) | copy-start | bytes 6291460
  119.2 3.5 %collective-permute-start.8 = (f32[64,128]{1,0:T(8,128)S(1)}, f32[64,128]{1,0:T(8,128)S(1)}, u32[]{:S(2)}, u32[]{:S(2)}) collective-permute-start(f32[64,128]{1,0:T(8,128)S(1)} %get-tuple-element.39), channel_id=1, source_target_pairs={{0,1},{2,3},{1,0},{3,2},{4,5},{6,7},{5,4},{7,6},{8,9},{10,11},{9,8... | collective-permute-start | bytes 98312 | tf_op jit(solution)/shard_map/ppermute | solution.py:492
  120.6 5.2 %collective-permute-start.9 = (f32[64,128]{1,0:T(8,128)S(1)}, f32[64,128]{1,0:T(8,128)S(1)}, u32[]{:S(2)}, u32[]{:S(2)}) collective-permute-start(f32[64,128]{1,0:T(8,128)S(1)} %get-tuple-element.40), channel_id=1, source_target_pairs={{1,2},{2,1},{5,6},{6,5},{9,10},{10,9},{13,14},{14,13},{17,18},{18,... | collective-permute-start | bytes 98312 | tf_op jit(solution)/shard_map/ppermute | solution.py:492
  125.9 5.4 %collective-permute-start.11 = (f32[40,128]{1,0:T(8,128)S(1)}, f32[40,128]{1,0:T(8,128)S(1)}, u32[]{:S(2)}, u32[]{:S(2)}) collective-permute-start(f32[40,128]{1,0:T(8,128)S(1)} %pad_maximum_fusion.5), channel_id=1, source_target_pairs={{4,8},{12,16},{20,24},{8,4},{16,12},{24,20},{5,9},{13,17},{21,25},... | collective-permute-start | bytes 61448 | tf_op jit(solution)/shard_map/ppermute | solution.py:500
  129.0 2.7 %collective-permute-start.10 = (f32[40,128]{1,0:T(8,128)S(1)}, f32[40,128]{1,0:T(8,128)S(1)}, u32[]{:S(2)}, u32[]{:S(2)}) collective-permute-start(f32[40,128]{1,0:T(8,128)S(1)} %pad_maximum_fusion.4), channel_id=1, source_target_pairs={{0,4},{8,12},{16,20},{24,28},{4,0},{12,8},{20,16},{28,24},{1,5},{9... | collective-permute-start | bytes 61448 | tf_op jit(solution)/shard_map/ppermute | solution.py:500

commit v2 on v1

v2 whole, which is shorter than its diff:
```python
import functools
import math

import jax
import jax.numpy as jnp
import numpy as np
from jax import lax
from jax.experimental import pallas as pl
from jax.experimental.pallas import tpu as pltpu
from jax.sharding import PartitionSpec as P

BLK = 64
NV = 32
NC = 8
KS = 5
ITERS = 2
OMEGA = 2.0 / 3.0
LANES = 128
F32 = jnp.float32
BF16 = jnp.bfloat16
PAIRS = BLK // 2
VROWS = BLK * NV // LANES
TROWS = BLK * NC // LANES
VM = pl.BlockSpec(memory_space=pltpu.VMEM)
SM = pl.BlockSpec(memory_space=pltpu.SMEM)
HB = pl.BlockSpec(memory_space=pltpu.HBM)
LIMIT = 16 * 1024 * 1024


def lane_iota(rows):
    return lax.broadcasted_iota(jnp.int32, (rows, LANES), 1)


def row_iota(rows):
    return lax.broadcasted_iota(jnp.int32, (rows, LANES), 0)


def roll(x, shift):
    return pltpu.roll(x, shift, 1)


def upper(x):
    return x.astype(BF16).astype(F32)


def hi_lo_lanes(x):
    return x - jnp.where(lane_iota(x.shape[0]) < 64, 0.0, upper(x))


def split(x):
    hi = x.astype(BF16)
    return jnp.concatenate([hi, (x - hi.astype(F32)).astype(BF16)], axis=0)


def rows_to_columns(rows, fold_ref, spread_ref):
    group = lane_iota(VROWS) // NV
    for s in range(4):
        spread_ref[pl.ds(s, VROWS, stride=4), :] = jnp.where(group == s, rows, 0.0)
    x = mm_t(fold_ref[...], split(spread_ref[...]))
    return x + roll(x, 64)


def pack_columns(x):
    return jnp.where(lane_iota(VROWS) < 64, x[:VROWS], x[VROWS:])


def unpack_columns(x):
    low = lane_iota(VROWS) < 64
    turned = roll(x, 64)
    return jnp.concatenate([jnp.where(low, x, turned), jnp.where(low, turned, x)], axis=0)


def mm_t(a, b):
    return lax.dot_general(a, b, (((1,), (1,)), ((), ())), preferred_element_type=F32)


def mm(a, b):
    return jnp.dot(a, b, preferred_element_type=F32)


def fold_rows(parts):
    sub = row_iota(8)
    step = 4
    while len(parts) > 1:
        half = len(parts) // 2
        parts = [
            jnp.where(
                (sub & step) == 0,
                parts[u] + pltpu.roll(parts[u], 8 - step, 0),
                parts[u + half] + pltpu.roll(parts[u + half], step, 0),
            )
            for u in range(half)
        ]
        step //= 2
    return parts[0]


def neighbour(near_ref, b, i, j, k, wide):
    return (i + 1) * wide + j + 1 if k == 0 else near_ref[b * KS + k]


def prepare_kernel(height, across, ints_ref, a_hbm, tv_ref, fold_ref, sent_a, sent_b, at_ref, rd_ref, v_ref, buf, rep_ref, sem):
    tiles = KS * PAIRS
    chunk = tiles * across
    depth = buf.shape[0]

    def copy(i):
        slot = lax.rem(i, depth)
        return pltpu.make_async_copy(
            a_hbm.at[pl.ds(i * chunk, chunk), :], buf.at[slot], sem.at[slot]
        )

    for i in range(depth - 1):
        copy(i).start()
    low = lane_iota(PAIRS) < 64
    row = row_iota(BLK)
    on_diagonal = lane_iota(BLK) == 2 * (row & (PAIRS - 1)) + row // PAIRS

    def body(i, carry):
        @pl.when(i + depth - 1 < height)
        def _():
            copy(i + depth - 1).start()

        copy(i).wait()
        slot = lax.rem(i, depth)
        for j in range(across):
            b = i * across + j

            def part(k):
                return buf[slot, pl.ds(k * PAIRS * across + j, PAIRS, stride=across), :]

            for t in range(3):
                x = part(2 * t)
                y = part(2 * t + 1) if t < 2 else jnp.zeros((PAIRS, LANES), F32)
                y_turned = roll(y, 64) if t < 2 else y
                m = jnp.concatenate(
                    [jnp.where(low, x, y_turned), jnp.where(low, roll(x, 64), y)], axis=0
                )
                at_ref[b, :, t * LANES : (t + 1) * LANES] = split(m)
                if t == 0:
                    d = jnp.sum(jnp.where(on_diagonal, m, 0.0), axis=0, keepdims=True)
                    rd_ref[pl.ds(b, 1), :] = OMEGA / (d + roll(d, 64))
            v_ref[pl.ds(b * NV, NV), :] = rows_to_columns(
                tv_ref[pl.ds(i * VROWS * across + j, VROWS, stride=across), :],
                fold_ref, rep_ref.at[j],
            )
        return carry

    lax.fori_loop(0, height, body, 0, unroll=2)


def halo_slots(meta_ref, height, across):
    slab_odd, pencil_odd = meta_ref[0], meta_ref[1]
    col_a = jnp.where(pencil_odd == 0, across + 1, 0)
    row_a = jnp.where(slab_odd == 0, height + 1, 0)
    return row_a, height + 1 - row_a, col_a, across + 1 - col_a


def sweep_core(height, across, near_ref, meta_ref, at_ref, rd_ref, v_ref, halo, u_ref, convert, store):
    wide = across + 2
    pa_ref, pb_ref, sa_ref, sb_ref = halo
    row_a, row_b, col_a, col_b = halo_slots(meta_ref, height, across)

    def own(i, carry):
        for j in range(across):
            u_ref[(i + 1) * wide + j + 1] = split(v_ref[pl.ds((i * across + j) * NV, NV), :])
        for s, (ref, col) in enumerate(((pa_ref, col_a), (pb_ref, col_b))):
            u_ref[(i + 1) * wide + col] = split(convert(ref[pl.ds(i * VROWS, VROWS), :], s))
        return carry

    lax.fori_loop(0, height, own, 0)
    for s, (ref, row) in enumerate(((sa_ref, row_a), (sb_ref, row_b))):
        for j in range(wide):
            col = j + 1 if j < across else (col_a if j == across else col_b)
            u_ref[row * wide + col] = split(
                convert(ref[j * VROWS : (j + 1) * VROWS, :], (s * wide + j) % across)
            )
    low = lane_iota(2 * NV) < 64
    cell = lane_iota(NV) & (BLK - 1)
    stored = (cell & 1) * PAIRS + cell // 2

    def body(i, carry):
        for j in range(across):
            b = i * across + j
            u = [u_ref[neighbour(near_ref, b, i, j, k, wide)] for k in range(KS)]
            left = jnp.concatenate(
                [jnp.where(low, u[0], u[1]), jnp.where(low, u[2], u[3]), u[4]], axis=1
            )
            r = mm_t(left, at_ref[b])
            s = r[:NV] + r[NV:]
            s = jnp.take_along_axis(s + roll(s, 64), stored, axis=1)
            store(i, j, b, v_ref[pl.ds(b * NV, NV), :] - s * rd_ref[pl.ds(b, 1), :])
        return carry

    lax.fori_loop(0, height, body, 0, unroll=2)


def sweep_kernel(height, across, near_ref, meta_ref, at_ref, rd_ref, v_ref, pa, pb, sa, sb, fold_ref,
                 out_ref, ea_ref, eb_ref, ra_ref, rb_ref, u_ref, rep_ref):
    def convert(rows, slot):
        return rows_to_columns(rows, fold_ref, rep_ref.at[slot])

    def store(i, j, b, value):
        out_ref[pl.ds(b * NV, NV), :] = value

    sweep_core(height, across, near_ref, meta_ref, at_ref, rd_ref, v_ref, (pa, pb, sa, sb),
               u_ref, convert, store)
    row_a, row_b, col_a, col_b = halo_slots(meta_ref, height, across)

    def message(i, j):
        return pack_columns(out_ref[pl.ds((i * across + j) * NV, NV), :])

    def edge(i, carry):
        for ref, col in ((ea_ref, col_a), (eb_ref, col_b)):
            ref[pl.ds(i * VROWS, VROWS), :] = message(i, jnp.where(col == 0, 0, across - 1))
        return carry

    lax.fori_loop(0, height, edge, 0)
    for ref, row in ((ra_ref, row_a), (rb_ref, row_b)):
        i = jnp.where(row == 0, 0, height - 1)
        for j in range(across):
            ref[j * VROWS : (j + 1) * VROWS, :] = message(i, j)


def last_sweep_kernel(height, across, capacity, per_owner, near_ref, meta_ref, agg_ref, at_ref, rd_ref, v_ref,
                      pa, pb, sa, sb, modes_ref, out_ref, pay_ref, u_ref):
    hcount = -(-capacity // 4)
    slot_rows = hcount * NC + 1
    devices = pay_ref.shape[0] // slot_rows

    def store(i, j, b, value):
        out_ref[pl.ds(b * NV, NV), :] = value

    sweep_core(height, across, near_ref, meta_ref, at_ref, rd_ref, v_ref, (pa, pb, sa, sb),
               u_ref, lambda rows, slot: unpack_columns(rows), store)
    pay_ref[...] = jnp.zeros(pay_ref.shape, F32)

    def coefs(i, acc):
        values = [out_ref[pl.ds((i * across + j) * NV, NV), :] for j in range(across)]
        for v in values:
            acc = acc + v * v
        for g in range(across // capacity):
            owner = lax.div(agg_ref[i * across + g * capacity], per_owner)
            for h in range(hcount):
                upper_rows, lower_rows = [], []
                for s in range(4):
                    if h * 4 + s < capacity:
                        both = split(values[g * capacity + h * 4 + s])
                    else:
                        both = jnp.zeros((2 * NV, LANES), BF16)
                    upper_rows.append(both[:NV])
                    lower_rows.append(both[NV:])
                r = mm_t(modes_ref[...], jnp.concatenate(upper_rows + lower_rows, axis=0))
                pay_ref[pl.ds(owner * slot_rows + h * NC, NC), :] = r[:NC, :LANES] + r[:NC, LANES:]
        return acc

    acc = lax.fori_loop(0, height, coefs, jnp.zeros((NV, LANES), F32))
    square = jnp.concatenate([acc, jnp.zeros((LANES - NV, LANES), F32)], axis=0)
    total = 0.5 * jnp.sum(jnp.transpose(square), axis=0, keepdims=True)
    pay_ref[pl.ds(slot_rows - 1, devices, stride=slot_rows), :] = jnp.where(
        lane_iota(devices) < NV, total, -1.0
    )
    lane = lane_iota(1)

    def mark(g, carry):
        owner = lax.div(agg_ref[g * capacity], per_owner)
        row = jnp.where(lane < NV, total, -1.0)
        for s in range(capacity):
            local = agg_ref[g * capacity + s] - owner * per_owner
            row = jnp.where(lane == NV + s, local.astype(F32), row)
        pay_ref[pl.ds(owner * slot_rows + slot_rows - 1, 1), :] = row
        return carry

    lax.fori_loop(0, height * across // capacity, mark, 0)


def solve_kernel(cells, per_owner, capacity, got_ref, ret_ref, inv_ref):
    hcount = -(-capacity // 4)
    slot_rows = hcount * NC + 1
    devices = got_ref.shape[0] // slot_rows
    lane = lane_iota(devices)
    extra = got_ref[pl.ds(slot_rows - 1, devices, stride=slot_rows), :]
    total = jnp.sum(jnp.where(lane < NV, extra, 0.0), axis=0, keepdims=True)
    total = jnp.broadcast_to(total, (8, LANES))
    total = total + roll(total, NV)
    total = total + roll(total, 64)
    inv = 1.0 / jnp.sqrt(total / cells + 1e-06)
    inv_ref[...] = jnp.transpose(jnp.broadcast_to(inv[0:1], (LANES, LANES)))[:NV]
    width = 4 * per_owner
    inner = lane & (width - 1)
    hot = []
    for h in range(hcount):
        want = jnp.full((devices, LANES), -1.0, F32)
        for s in range(min(4, capacity - 4 * h)):
            column = extra[:, NV + 4 * h + s : NV + 4 * h + s + 1]
            want = jnp.where(inner // per_owner == s, column, want)
        same = want == (inner & (per_owner - 1)).astype(F32)
        hot.append(jnp.where(same & (lane < 2 * width), 1.0, 0.0))
    hot = jnp.concatenate(hot, axis=0)
    hot_t = jnp.transpose(hot)[:width]
    parts = [
        jnp.concatenate(
            [got_ref[pl.ds(h * NC + m, devices, stride=slot_rows), :] for h in range(hcount)], axis=0
        )
        for m in range(NC)
    ]
    data = jnp.concatenate(parts, axis=1)
    ones = jnp.ones((hcount * devices, LANES), F32)
    high = jnp.concatenate([data, ones], axis=1).astype(BF16)
    rest = jnp.concatenate([data - upper(data), jnp.zeros_like(ones)], axis=1).astype(BF16)
    hot_b = hot_t.astype(BF16)
    sums = mm(hot_b, high) + mm(hot_b, rest)
    group_lane = lane_iota(per_owner) // NV

    def block(s, m):
        return sums[s * per_owner : (s + 1) * per_owner, m * LANES : (m + 1) * LANES]

    count = sum(block(s, NC) for s in range(4))
    weight = inv[0:1] / jnp.maximum(count, 1.0)
    coarse = []
    for m in range(NC):
        c = jnp.zeros((per_owner, LANES), F32)
        for s in range(4):
            c = jnp.where(group_lane == s, block(s, m), c)
        c = c + roll(c, NV)
        c = c + roll(c, 64)
        coarse.append(c * weight)

    def dot_all(x):
        for shift in (16, 8, 4, 2, 1):
            x = x + roll(x, shift)
        return x

    gram = {(a, c): dot_all(coarse[a] * coarse[c]) for a in range(NC) for c in range(a + 1)}
    ridge = 0.1 * sum(gram[m, m] for m in range(NC)) / NC + 1e-06
    for m in range(NC):
        gram[m, m] = gram[m, m] + ridge
    recip = []
    for m in range(NC):
        root = 1.0 / jnp.sqrt(gram[m, m])
        recip.append(root)
        for a in range(m + 1, NC):
            gram[a, m] = gram[a, m] * root
        for a in range(m + 1, NC):
            for c in range(m + 1, a + 1):
                gram[a, c] = gram[a, c] - gram[a, m] * gram[c, m]
    solved = list(coarse)
    for m in range(NC):
        solved[m] = solved[m] * recip[m]
        for a in range(m + 1, NC):
            solved[a] = solved[a] - gram[a, m] * solved[m]
    for m in reversed(range(NC)):
        solved[m] = solved[m] * recip[m]
        for a in range(m):
            solved[a] = solved[a] - gram[m, a] * solved[m]
    table = jnp.concatenate(
        [
            jnp.concatenate([jnp.where(group_lane == s, solved[m], 0.0) for s in range(4)], axis=0)
            for m in range(NC)
        ],
        axis=1,
    )
    stacked = jnp.concatenate([table.astype(BF16), (table - upper(table)).astype(BF16)], axis=0)
    back = mm(hot[:, : 2 * width].astype(BF16), stacked)
    for h in range(hcount):
        for m in range(NC):
            ret_ref[pl.ds(h * NC + m, devices, stride=hcount * NC), :] = back[
                h * devices : (h + 1) * devices, m * LANES : (m + 1) * LANES
            ]


def relaxed_kernel(height, across, v_ref, inv_ref, order_ref, after_ref, rel_ref):
    inv = inv_ref[...]
    group = lane_iota(VROWS) // NV

    def body(i, carry):
        for j in range(across):
            both = split(v_ref[pl.ds((i * across + j) * NV, NV), :] * inv)
            r = mm_t(order_ref[...], jnp.concatenate([both, both], axis=0))
            r = r + roll(r, NV)
            rows = r[:VROWS]
            for s in range(1, 4):
                rows = jnp.where(group == s, r[s * VROWS : (s + 1) * VROWS], rows)
            rel_ref[pl.ds(i * VROWS * across + j, VROWS, stride=across), :] = rows
        return carry

    lax.fori_loop(0, height, body, 0, unroll=2)


def cell_rows(parts, place_ref):
    left = jnp.concatenate([hi_lo_lanes(x) for part in parts for x in part], axis=0).astype(BF16)
    r = mm(left, place_ref[...])
    picks = (lane_iota(8) & (NC - 1)) == row_iota(8)
    out = []
    for n in range(len(parts)):
        for q in range(TROWS):
            out.append(
                fold_rows(
                    [
                        jnp.where(
                            picks,
                            r[(n * 8 + u) * 8 : (n * 8 + u + 1) * 8, q * LANES : (q + 1) * LANES],
                            0.0,
                        )
                        for u in range(8)
                    ]
                )
            )
    return out


def tile_kernel(height, across, capacity, per_owner, meta_ref, agg_ref, ret_ref, v_ref, inv_ref, place_ref,
                tile_ref, out_ref, ea_ref, eb_ref, ra_ref, rb_ref):
    hcount = -(-capacity // 4)
    group_lane = lane_iota(NC) // NV
    inv = inv_ref[...]

    def body(i, carry):
        tiles = []
        for g in range(across // capacity):
            owner = lax.div(agg_ref[i * across + g * capacity], per_owner)
            for h in range(hcount):
                m = ret_ref[pl.ds(pl.multiple_of((owner * hcount + h) * NC, NC), NC), :]
                m_hi = upper(m)
                left = jnp.concatenate(
                    [jnp.where(group_lane == s, x, 0.0) for x in (m_hi, m - m_hi) for s in range(4)],
                    axis=0,
                ).astype(BF16)
                upper_rows, lower_rows = [], []
                for s in range(4):
                    if h * 4 + s < capacity:
                        b = i * across + g * capacity + h * 4 + s
                        both = split(v_ref[pl.ds(b * NV, NV), :] * inv)
                    else:
                        both = jnp.zeros((2 * NV, LANES), BF16)
                    upper_rows.append(both[:NV])
                    lower_rows.append(both[NV:])
                r = mm(
                    jnp.concatenate([left, left], axis=1),
                    jnp.concatenate(upper_rows + lower_rows, axis=0),
                )
                for s in range(min(4, capacity - h * 4)):
                    t = r[s * NC : (s + 1) * NC] + r[(4 + s) * NC : (5 + s) * NC]
                    b = i * across + g * capacity + h * 4 + s
                    tile_ref[pl.ds(b * NC, NC), :] = t
                    tiles.append(t)
        for q, rows in enumerate(cell_rows([tiles], place_ref)):
            out_ref[pl.ds((i * TROWS + q) * across, across), :] = rows
        return carry

    lax.fori_loop(0, height, body, 0, unroll=2)
    row_a, row_b, col_a, col_b = halo_slots(meta_ref, height, across)

    def edge(i, carry):
        for ref, col in ((ea_ref, col_a), (eb_ref, col_b)):
            j = jnp.where(col == 0, 0, across - 1)
            ref[pl.ds(i * NC, NC), :] = tile_ref[pl.ds((i * across + j) * NC, NC), :]
        return carry

    lax.fori_loop(0, height, edge, 0)
    for ref, row in ((ra_ref, row_a), (rb_ref, row_b)):
        i = jnp.where(row == 0, 0, height - 1)
        ref[...] = tile_ref[pl.ds(pl.multiple_of(i * across * NC, 8), across * NC), :]


def product_kernel(height, across, near_ref, meta_ref, at_ref, tile_ref, pa_ref, pb_ref, sa_ref, sb_ref,
                   place_ref, out_ref, u_ref):
    wide = across + 2
    row_a, row_b, col_a, col_b = halo_slots(meta_ref, height, across)
    low = lane_iota(NC) < 64

    def put(index, x):
        hi = upper(x)
        lo = x - hi
        u_ref[index] = jnp.concatenate(
            [
                jnp.where(low, hi, 0.0), jnp.where(low, lo, 0.0),
                jnp.where(low, 0.0, hi), jnp.where(low, 0.0, lo),
            ],
            axis=0,
        ).astype(BF16)

    def own(i, carry):
        for j in range(across):
            put((i + 1) * wide + j + 1, tile_ref[pl.ds((i * across + j) * NC, NC), :])
        for ref, col in ((pa_ref, col_a), (pb_ref, col_b)):
            put((i + 1) * wide + col, ref[pl.ds(i * NC, NC), :])
        return carry

    lax.fori_loop(0, height, own, 0)
    for ref, row in ((sa_ref, row_a), (sb_ref, row_b)):
        for j in range(wide):
            col = j + 1 if j < across else (col_a if j == across else col_b)
            put(row * wide + col, ref[j * NC : (j + 1) * NC, :])

    def body(i, carry):
        parts = [[] for _ in range(KS)]
        for j in range(across):
            b = i * across + j
            u = [
                u_ref[neighbour(near_ref, b, i, j, k, wide), (k % 2) * 2 * NC : (k % 2 + 1) * 2 * NC, :]
                for k in range(KS)
            ]
            for t in range(3):
                left = jnp.concatenate(u[2 * t : 2 * t + 2], axis=0)
                r = mm_t(left, at_ref[b, :, t * LANES : (t + 1) * LANES])
                for s in range(left.shape[0] // (2 * NC)):
                    x = r[s * 2 * NC : s * 2 * NC + NC] + r[s * 2 * NC + NC : (s + 1) * 2 * NC]
                    parts[2 * t + s].append(x + roll(x, 64))
        for n, rows in enumerate(cell_rows(parts, place_ref)):
            at = pl.multiple_of((i * KS * TROWS + n) * across, 8)
            out_ref[pl.ds(at, across), :] = rows
        return carry

    lax.fori_loop(0, height, body, 0, unroll=2)


def swaps(count, first):
    pairs = [(i, i + 1) for i in range(first, count - 1, 2)]
    return pairs + [(b, a) for a, b in pairs]


def exchange(edges, rows, slab_odd, unit, height, sent=None):
    pencils, slabs = lax.axis_size("pencil"), lax.axis_size("slab")
    got = [lax.ppermute(e, "pencil", swaps(pencils, s)) for s, e in enumerate(edges)]
    out = []
    for s, own in enumerate(rows):
        last = (slab_odd == 0) if s == 0 else (slab_odd == 1)
        corners = [
            jnp.where(last, g[(height - 1) * unit : height * unit], g[:unit]) for g in got
        ]
        message = jnp.concatenate([own] + corners, axis=0)
        if sent is not None:
            sent.append(message)
        out.append(lax.ppermute(message, "slab", swaps(slabs, s)))
    return got + out


def lines(x, features):
    height, across, _ = x.shape
    y = x.reshape(height, across, features // LANES, LANES).transpose(0, 2, 1, 3)
    return y.reshape(height * across * features // LANES, LANES)


def unlines(y, height, across, features):
    x = y.reshape(height, features // LANES, across, LANES).transpose(0, 2, 1, 3)
    return x.reshape(height, across, features)


def call(kernel, outs, ins, scratch=(), limit=LIMIT, specs=None):
    return pl.pallas_call(
        kernel,
        out_shape=outs,
        in_specs=specs,
        out_specs=[VM] * len(outs),
        scratch_shapes=list(scratch),
        compiler_params=pltpu.CompilerParams(vmem_limit_bytes=limit),
    )(*ins)


def sds(*shape, dtype=F32):
    return jax.ShapeDtypeStruct(shape, dtype)


def mode_table():
    centre = np.arange(BLK, dtype=np.float64) + 0.5
    q = np.cos(math.pi * centre[:, None] * np.arange(NC)[None, :] / BLK).astype(np.float32)
    return q


def shards(a_blocks, col_codes, agg_of, test_vectors):
    height, across = agg_of.shape
    slabs, pencils = lax.axis_size("slab"), lax.axis_size("pencil")
    devices = slabs * pencils
    block_rows = height * across
    capacity = 2 * block_rows // devices
    per_owner = block_rows // 8
    hcount = -(-capacity // 4)
    wide = across + 2
    slab_odd = lax.axis_index("slab") % 2
    pencil_odd = lax.axis_index("pencil") % 2
    meta = jnp.stack([slab_odd, pencil_odd]).astype(jnp.int32)
    down = jnp.arange(height, dtype=jnp.int32)[:, None, None] + col_codes // 3
    near = (down * wide + jnp.arange(across, dtype=jnp.int32)[None, :, None] + col_codes % 3).reshape(-1)
    aggs = agg_of.reshape(-1)

    tv = lines(test_vectors, BLK * NV)
    by_row = test_vectors.reshape(height, across, VROWS, LANES)
    col_hi, col_lo = by_row[:, across - 1], by_row[:, 0]
    row_hi, row_lo = by_row[height - 1], by_row[0]
    flip = lambda odd, a, b: (jnp.where(odd == 0, a, b), jnp.where(odd == 0, b, a))
    edges = [e.reshape(height * VROWS, LANES) for e in flip(pencil_odd, col_hi, col_lo)]
    rows = [e.reshape(across * VROWS, LANES) for e in flip(slab_odd, row_hi, row_lo)]
    sent = []
    halo = exchange(edges, rows, slab_odd, VROWS, height, sent)

    lane = np.arange(LANES)
    fold = jnp.asarray(np.arange(NV)[:, None] == lane[None, :] % NV, BF16)
    place_to = np.arange(TROWS * LANES) // NC
    place = jnp.asarray((lane[:, None] % BLK) == place_to[None, :], BF16)
    stored = 2 * (lane % PAIRS) + lane % BLK // PAIRS
    place_stored = jnp.asarray(stored[:, None] == place_to[None, :], BF16)
    order_row = np.arange(BLK)
    order = jnp.asarray(((order_row % VROWS) * 4 + order_row // VROWS)[:, None] == lane[None, :], BF16)
    q = mode_table()
    q_hi = jnp.asarray(q.T).astype(BF16)
    q_lo = (jnp.asarray(q.T) - q_hi.astype(F32)).astype(BF16)
    modes = jnp.pad(jnp.concatenate([q_hi, q_lo], axis=1), ((0, NC), (0, 0)))

    chunk = KS * PAIRS * across
    ints = jnp.concatenate([near, aggs, meta])
    at, rd, v = call(
        functools.partial(prepare_kernel, height, across),
        [sds(block_rows, 2 * BLK, 3 * LANES, dtype=BF16), sds(block_rows, LANES), sds(block_rows * NV, LANES)],
        [ints, pltpu.with_memory_space_constraint(lines(a_blocks, KS * BLK * BLK), pltpu.HBM), tv, fold, *sent],
        [
            pltpu.VMEM((4, chunk, LANES), F32),
            pltpu.VMEM((across, BLK, LANES), F32),
            pltpu.SemaphoreType.DMA((4,)),
        ],
        specs=[SM, HB, VM, VM, HB, HB],
        limit=16 * 1024 * 1024,
    )
    field = [pltpu.VMEM((wide * (height + 2), 2 * NV, LANES), BF16)]
    v, ea, eb, ra, rb = call(
        functools.partial(sweep_kernel, height, across),
        [sds(block_rows * NV, LANES)] + [sds(height * VROWS, LANES)] * 2 + [sds(across * VROWS, LANES)] * 2,
        [near, meta, at, rd, v, *halo, fold],
        field + [pltpu.VMEM((across, BLK, LANES), F32)],
        specs=[SM, SM] + [VM] * 8,
    )
    halo = exchange([ea, eb], [ra, rb], slab_odd, VROWS, height)
    slot_rows = hcount * NC + 1
    v, pay = call(
        functools.partial(last_sweep_kernel, height, across, capacity, per_owner),
        [sds(block_rows * NV, LANES), sds(devices * slot_rows, LANES)],
        [near, meta, aggs, at, rd, v, *halo, modes],
        field,
        specs=[SM, SM, SM] + [VM] * 8,
    )
    got = lax.all_to_all(
        pay.reshape(devices, slot_rows * LANES), ("slab", "pencil"), split_axis=0, concat_axis=0, tiled=True
    ).reshape(devices * slot_rows, LANES)
    ret, inv = call(
        functools.partial(solve_kernel, float(block_rows * BLK * devices), per_owner, capacity),
        [sds(devices * hcount * NC, LANES), sds(NV, LANES)],
        [got],
        specs=[VM],
    )
    back = lax.all_to_all(
        ret.reshape(devices, hcount * NC * LANES), ("slab", "pencil"), split_axis=0, concat_axis=0, tiled=True
    ).reshape(devices * hcount * NC, LANES)
    tile, tiles, ea, eb, ra, rb = call(
        functools.partial(tile_kernel, height, across, capacity, per_owner),
        [sds(block_rows * NC, LANES), sds(block_rows * TROWS, LANES)]
        + [sds(height * NC, LANES)] * 2 + [sds(across * NC, LANES)] * 2,
        [meta, aggs, back, v, inv, place],
        specs=[SM, SM, VM, VM, VM, VM],
    )
    (relaxed,) = call(
        functools.partial(relaxed_kernel, height, across),
        [sds(block_rows * VROWS, LANES)],
        [v, inv, order, tile],
        specs=[VM] * 4,
    )
    halo = exchange([ea, eb], [ra, rb], slab_odd, NC, height)
    (products,) = call(
        functools.partial(product_kernel, height, across),
        [sds(block_rows * KS * TROWS, LANES)],
        [near, meta, at, tile, *halo, place_stored],
        [pltpu.VMEM((wide * (height + 2), 4 * NC, LANES), BF16)],
        specs=[SM, SM] + [VM] * 7,
    )
    return (
        unlines(relaxed, height, across, BLK * NV),
        unlines(tiles, height, across, BLK * NC),
        unlines(products, height, across, KS * BLK * NC),
    )


def solution(mesh):
    in_specs = (P("slab", "pencil", None), P("slab", "pencil", None), P("slab", "pencil"), P("slab", "pencil", None))
    out_specs = (P("slab", "pencil", None),) * 3
    return jax.shard_map(shards, mesh=mesh, in_specs=in_specs, out_specs=out_specs, check_vma=False)
```

time: 154 us -> 127 us (0.82)
  Pallas kernels: 81.4 us -> 60.2 us
  blocking collectives: 15.3 us -> 26.5 us
  waiting for transfers between devices: 17.3 us -> 11.2 us
  local copies, waits for them, and re-layouts: 8.88 us -> 3.07 us
  starting transfers between devices: 26.1 us -> 22.7 us
    pallas_call x7, Pallas kernels: 81.4 us -> 60.2 us  [call(): pl.pallas_call(kernel, out_shape=outs, in_specs=specs, out_specs=[VM] * l...]
    all_to_all x0 -> x1, blocking collectives: none -> 12.8 us  [shards(): lax.all_to_all(ret.reshape(devices, hcount * NC * LANES), ('slab', 'penci...]
    unnamed x15 -> x13, local copies, waits for them, and re-layouts: 6.51 us -> 0.79 us
    all_to_all x1 -> x0, waiting for transfers between devices: 5.71 us -> none  [shards(): lax.all_to_all(ret.reshape(devices, hcount * NC * LANES), ('slab', 'penci...]
    all_to_all x1 -> x0, starting transfers between devices: 4.57 us -> none  [shards(): lax.all_to_all(ret.reshape(devices, hcount * NC * LANES), ('slab', 'penci...]
    all_to_all x1, blocking collectives: 15.3 us -> 13.7 us  [shards(): lax.all_to_all(pay.reshape(devices, slot_rows * LANES), ('slab', 'pencil'...]
  transfers between devices with their start and end apart: 13 -> 12, of which waited for: 7 -> 4; matrix products, arithmetic and copies ran while one was open for 3% -> 2% of each run, Pallas kernels for 9% -> 12%
where the time goes in v2:
time: 127 us; the launch traced here: 126 us
  Pallas kernels  60.2 us (47%)
  blocking collectives  26.5 us (21%)
  starting transfers between devices  22.7 us (18%)
  waiting for transfers between devices  11.2 us (9%)
  local copies, waits for them, and re-layouts  3.07 us (2%)
  other arithmetic  1.89 us (1%)
    pallas_call x7, Pallas kernels, call(): pl.pallas_call(kernel, out_shape=outs, in_specs=specs, out_specs=[VM] * l...  60.2 us
    all_to_all x1, blocking collectives, shards(): lax.all_to_all(pay.reshape(devices, slot_rows * LANES), ('slab', 'pencil'...  13.7 us
    all_to_all x1, blocking collectives, shards(): lax.all_to_all(ret.reshape(devices, hcount * NC * LANES), ('slab', 'penci...  12.8 us
    ppermute x6, starting transfers between devices, exchange(): out.append(lax.ppermute(message, 'slab', swaps(slabs, s)))  11.6 us
    ppermute x6, starting transfers between devices, exchange(): lax.ppermute(e, 'pencil', swaps(pencils, s))  11.1 us
    ppermute x6, waiting for transfers between devices, exchange(): lax.ppermute(e, 'pencil', swaps(pencils, s))  6.99 us
    ppermute x6, waiting for transfers between devices, exchange(): out.append(lax.ppermute(message, 'slab', swaps(slabs, s)))  4.17 us
  transfers between devices with their start and end apart: 12, of which 4 were waited for; matrix products, arithmetic and copies ran while one was open for 2% of the time, Pallas kernels for 12%

profile of v2, /device:TPU:9, one launch (start us, length us, event | category | flops | bytes accessed | tf_op | source)
XLA Modules:
  0.0 126.4 jit_solution(13160866852002377132)
XLA Ops:
  0.7 1.8 %fusion.5 = (f32[16,1,16,128]{3,1,2,0:T(1,128)S(1)}, f32[16,1,16,128]{3,1,2,0:T(1,128)S(1)}) fusion(f32[16,8,16,128]{3,1,2,0:T(8,128)} %bitcast.35), kind=kLoop, calls=%fused_computation.33 | loop fusion | bytes 524288 | tf_op jit(solution)/shard_map/slice | solution.py:589
  2.5 3.7 %collective-permute-start.1 = (f32[256,128]{1,0:T(8,128)S(1)}, f32[256,128]{1,0:T(8,128)S(1)}, u32[]{:S(2)}, u32[]{:S(2)}) collective-permute-start(f32[256,128]{1,0:T(8,128)S(1)} %bitcast.47), channel_id=1, source_target_pairs={{1,2},{2,1},{5,6},{6,5},{9,10},{10,9},{13,14},{14,13},{17,18},{18,... | collective-permute-start | bytes 393224 | tf_op jit(solution)/shard_map/ppermute | solution.py:525
  6.3 0.9 slice_select_fusion
  7.2 0.8 fusion.3
  8.0 0.8 copy.21
  8.7 0.1 reshape.84.agg_ref
  8.8 0.1 copy.20
  9.0 0.2 reshape.83.near_ref
  9.3 1.3 %collective-permute-start.2 = (f32[160,128]{1,0:T(8,128)S(1)}, f32[160,128]{1,0:T(8,128)S(1)}, u32[]{:S(2)}, u32[]{:S(2)}) collective-permute-start(f32[160,128]{1,0:T(8,128)S(1)} %pad_maximum_fusion.sent_a), channel_id=1, source_target_pairs={{0,4},{8,12},{16,20},{24,28},{4,0},{12,8},{20,16},{28,24},{1,5},{9... | collective-permute-start | bytes 245768 | tf_op jit(solution)/shard_map/ppermute | solution.py:535
  10.6 2.0 %collective-permute-start.3 = (f32[160,128]{1,0:T(8,128)S(1)}, f32[160,128]{1,0:T(8,128)S(1)}, u32[]{:S(2)}, u32[]{:S(2)}) collective-permute-start(f32[160,128]{1,0:T(8,128)S(1)} %pad_maximum_fusion.1.sent_b), channel_id=1, source_target_pairs={{4,8},{12,16},{20,24},{8,4},{16,12},{24,20},{5,9},{13,17},{21,25},... | collective-permute-start | bytes 245768 | tf_op jit(solution)/shard_map/ppermute | solution.py:535
  12.7 0.1 pad_add_fusion.1.meta_ref
  12.8 9.8 %shard_map.121 = (bf16[128,128,384]{2,1,0:T(8,128)(2,1)S(1)}, f32[128,128]{1,0:T(8,128)S(1)}, f32[4096,128]{1,0:T(8,128)S(1)}) custom-call(s32[770]{0:T(1024)S(1)} %pad_add_fusion.ints_ref, f32[20480,128]{1,0:T(8,128)} %bitcast.41, f32[2048,128]{1,0:T(8,128)S(1)} %bitcast.36, bf16[32,128]{1,0:T(8,128)(2,1)S(1)} %copy-done.3, ...), custom_call_target="tpu_custom_call" | custom-call | tf_op jit(solution)/shard_map/pallas_call | solution.py:551
  22.6 12.9 %shard_map.122 = (f32[4096,128]{1,0:T(8,128)S(1)}, f32[256,128]{1,0:T(8,128)S(1)}, f32[256,128]{1,0:T(8,128)S(1)}, f32[128,128]{1,0:T(8,128)S(1)}, f32[128,128]{1,0:T(8,128)S(1)}) custom-call(s32[640]{0:T(1024)S(1)} %reshape.83.near_ref, s32[2]{0:T(128)S(1)} %pad_add_fusion.1.meta_ref, bf16[128,128,384]{2,1,0:T(8,128)(2,1)S(1)} %get-tuple-element.21.at_ref, ...), custom_call_target="tpu_custom_call" | custom-call | tf_op jit(solution)/shard_map/pallas_call | solution.py:551
  35.5 1.1 collective-permute-start.4
  36.6 2.7 %collective-permute-start.5 = (f32[256,128]{1,0:T(8,128)S(1)}, f32[256,128]{1,0:T(8,128)S(1)}, u32[]{:S(2)}, u32[]{:S(2)}) collective-permute-start(f32[256,128]{1,0:T(8,128)S(1)} %get-tuple-element.26), channel_id=1, source_target_pairs={{1,2},{2,1},{5,6},{6,5},{9,10},{10,9},{13,14},{14,13},{17,18},{18,... | collective-permute-start | bytes 393224 | tf_op jit(solution)/shard_map/ppermute | solution.py:525
  39.4 3.5 %collective-permute-done.5.pb = f32[256,128]{1,0:T(8,128)S(1)} collective-permute-done((f32[256,128]{1,0:T(8,128)S(1)}, f32[256,128]{1,0:T(8,128)S(1)}, u32[]{:S(2)}, u32[]{:S(2)}) %collective-permute-start.5) | collective-permute-done | bytes 131104 | tf_op jit(solution)/shard_map/ppermute | solution.py:525
  42.9 2.4 %collective-permute-start.6 = (f32[160,128]{1,0:T(8,128)S(1)}, f32[160,128]{1,0:T(8,128)S(1)}, u32[]{:S(2)}, u32[]{:S(2)}) collective-permute-start(f32[160,128]{1,0:T(8,128)S(1)} %pad_maximum_fusion.2), channel_id=1, source_target_pairs={{0,4},{8,12},{16,20},{24,28},{4,0},{12,8},{20,16},{28,24},{1,5},{9... | collective-permute-start | bytes 245768 | tf_op jit(solution)/shard_map/ppermute | solution.py:535
  45.3 1.9 %collective-permute-start.7 = (f32[160,128]{1,0:T(8,128)S(1)}, f32[160,128]{1,0:T(8,128)S(1)}, u32[]{:S(2)}, u32[]{:S(2)}) collective-permute-start(f32[160,128]{1,0:T(8,128)S(1)} %pad_maximum_fusion.3), channel_id=1, source_target_pairs={{4,8},{12,16},{20,24},{8,4},{16,12},{24,20},{5,9},{13,17},{21,25},... | collective-permute-start | bytes 245768 | tf_op jit(solution)/shard_map/ppermute | solution.py:535
  47.2 0.8 collective-permute-done.6.sa
  48.0 3.4 %collective-permute-done.7.sb = f32[160,128]{1,0:T(8,128)S(1)} collective-permute-done((f32[160,128]{1,0:T(8,128)S(1)}, f32[160,128]{1,0:T(8,128)S(1)}, u32[]{:S(2)}, u32[]{:S(2)}) %collective-permute-start.7) | collective-permute-done | bytes 81952 | tf_op jit(solution)/shard_map/ppermute | solution.py:535
  51.4 12.3 %shard_map.123 = (f32[4096,128]{1,0:T(8,128)S(1)}, f32[544,128]{1,0:T(8,128)S(1)}) custom-call(s32[640]{0:T(1024)S(1)} %reshape.83.near_ref, s32[2]{0:T(128)S(1)} %pad_add_fusion.1.meta_ref, s32[128]{0:T(128)S(1)} %reshape.84.agg_ref, bf16[128,128,384]{2,1,0:T(8,128)(2,1)S(1)} %get-tuple-element.21.at_ref, f32[128,128]{1,0:T(8,128)S(1)} %get-tuple-element.22.rd_ref, ...), custom_call_target="tpu_custom_call" | custom-call | tf_op jit(solution)/shard_map/pallas_call | solution.py:551
  63.6 13.7 %all_to_all.18 = f32[32,1,2176]{2,1,0:T(1,128)S(1)} all-to-all(f32[32,1,2176]{2,1,0:T(1,128)S(1)} %bitcast.39), channel_id=1, replica_groups=mesh['slab'=8,'pencil'=4] {'slab','pencil'}, dimensions={0} | all-to-all | bytes 557056 | tf_op jit(solution)/shard_map/all_to_all | solution.py:641
  77.3 1.3 %shard_map.124 = (f32[512,128]{1,0:T(8,128)S(1)}, f32[32,128]{1,0:T(8,128)S(1)}) custom-call(f32[544,128]{1,0:T(8,128)S(1)} %bitcast.37), custom_call_target="tpu_custom_call" | custom-call | tf_op jit(solution)/shard_map/pallas_call | solution.py:551
  78.7 12.8 %all_to_all.19 = f32[32,1,2048]{2,1,0:T(1,128)S(1)} all-to-all(f32[32,1,2048]{2,1,0:T(1,128)S(1)} %bitcast.40), channel_id=1, replica_groups=mesh['slab'=8,'pencil'=4] {'slab','pencil'}, dimensions={0} | all-to-all | bytes 524288 | tf_op jit(solution)/shard_map/all_to_all | solution.py:650
  91.5 5.2 %shard_map.125 = (f32[1024,128]{1,0:T(8,128)S(1)}, f32[512,128]{1,0:T(8,128)}, f32[128,128]{1,0:T(8,128)S(1)}, f32[128,128]{1,0:T(8,128)S(1)}, f32[64,128]{1,0:T(8,128)S(1)}, /*index=5*/f32[64,128]{1,0:T(8,128)S(1)}) custom-call(s32[2]{0:T(128)S(1)} %pad_add_fusion.1.meta_ref, s32[128]{0:T(128)S(1)} %reshape.84.agg_ref, f32[512,128]{1,0:T(8,128)S(1)} %bitcast.38, ...), custom_call_target="tpu_custom_call" | custom-call | tf_op jit(solution)/shard_map/pallas_call | solution.py:551
  96.7 1.4 %collective-permute-start.8 = (f32[128,128]{1,0:T(8,128)S(1)}, f32[128,128]{1,0:T(8,128)S(1)}, u32[]{:S(2)}, u32[]{:S(2)}) collective-permute-start(f32[128,128]{1,0:T(8,128)S(1)} %get-tuple-element.35), channel_id=1, source_target_pairs={{0,1},{2,3},{1,0},{3,2},{4,5},{6,7},{5,4},{7,6},{8,9},{10,11},{9,8... | collective-permute-start | bytes 196616 | tf_op jit(solution)/shard_map/ppermute | solution.py:525
  98.1 2.1 %collective-permute-start.9 = (f32[128,128]{1,0:T(8,128)S(1)}, f32[128,128]{1,0:T(8,128)S(1)}, u32[]{:S(2)}, u32[]{:S(2)}) collective-permute-start(f32[128,128]{1,0:T(8,128)S(1)} %get-tuple-element.36), channel_id=1, source_target_pairs={{1,2},{2,1},{5,6},{6,5},{9,10},{10,9},{13,14},{14,13},{17,18},{18,... | collective-permute-start | bytes 196616 | tf_op jit(solution)/shard_map/ppermute | solution.py:525
  100.2 3.5 %collective-permute-done.9.pb_ref = f32[128,128]{1,0:T(8,128)S(1)} collective-permute-done((f32[128,128]{1,0:T(8,128)S(1)}, f32[128,128]{1,0:T(8,128)S(1)}, u32[]{:S(2)}, u32[]{:S(2)}) %collective-permute-start.9) | collective-permute-done | bytes 65568 | tf_op jit(solution)/shard_map/ppermute | solution.py:525
  103.7 0.4 collective-permute-start.10
  104.1 3.6 %collective-permute-start.11 = (f32[80,128]{1,0:T(8,128)S(1)}, f32[80,128]{1,0:T(8,128)S(1)}, u32[]{:S(2)}, u32[]{:S(2)}) collective-permute-start(f32[80,128]{1,0:T(8,128)S(1)} %pad_maximum_fusion.5), channel_id=1, source_target_pairs={{4,8},{12,16},{20,24},{8,4},{16,12},{24,20},{5,9},{13,17},{21,25},... | collective-permute-start | bytes 122888 | tf_op jit(solution)/shard_map/ppermute | solution.py:535
  107.7 5.3 %shard_map.126 = f32[2048,128]{1,0:T(8,128)} custom-call(f32[4096,128]{1,0:T(8,128)S(1)} %get-tuple-element.29.v_ref, f32[32,128]{1,0:T(8,128)S(1)} %get-tuple-element.31.inv_ref, bf16[64,128]{1,0:T(8,128)(2,1)S(1)} %copy-done.4, f32[1024,128]{1,0:T(8,128)S(1)} %get-tuple-element.33.after_ref.tile_ref), custom_call_target="tpu_custom_call" | custom-call | tf_op jit(solution)/shard_map/pallas_call | solution.py:551
  113.0 13.4 %shard_map.127 = f32[2560,128]{1,0:T(8,128)} custom-call(s32[640]{0:T(1024)S(1)} %reshape.83.near_ref, s32[2]{0:T(128)S(1)} %pad_add_fusion.1.meta_ref, bf16[128,128,384]{2,1,0:T(8,128)(2,1)S(1)} %get-tuple-element.21.at_ref, f32[1024,128]{1,0:T(8,128)S(1)} %get-tuple-element.33.after_ref.tile_ref, f32[128,128]{1,0:T(8,128)S(1)} %collective-permute-done.8.pa_ref, ...), custom_call_target="tpu_custom_call" | custom-call | tf_op jit(solution)/shard_map/pallas_call | solution.py:551
  (37 shorter events, 0.3 us)
Async XLA Ops:
  0.6 12.1 %copy-start.3 = (bf16[32,128]{1,0:T(8,128)(2,1)S(1)}, bf16[32,128]{1,0:T(8,128)(2,1)}, u32[]{:S(2)}) copy-start(bf16[32,128]{1,0:T(8,128)(2,1)} %constant.60.clone.fold_ref) | copy-start | bytes 24580
  0.6 12.1 %copy-start = (f32[16,8,2048]{2,1,0:T(8,128)S(1)}, f32[16,8,2048]{2,1,0:T(8,128)}, u32[]{:S(2)}) copy-start(f32[16,8,2048]{2,1,0:T(8,128)} %param.13) | copy-start | bytes 3145732
  2.5 6.8 %collective-permute-start.1 = (f32[256,128]{1,0:T(8,128)S(1)}, f32[256,128]{1,0:T(8,128)S(1)}, u32[]{:S(2)}, u32[]{:S(2)}) collective-permute-start(f32[256,128]{1,0:T(8,128)S(1)} %bitcast.47), channel_id=1, source_target_pairs={{1,2},{2,1},{5,6},{6,5},{9,10},{10,9},{13,14},{14,13},{17,18},{18,... | collective-permute-start | bytes 393224 | tf_op jit(solution)/shard_map/ppermute | solution.py:525
  6.2 3.1 %collective-permute-start = (f32[256,128]{1,0:T(8,128)S(1)}, f32[256,128]{1,0:T(8,128)S(1)}, u32[]{:S(2)}, u32[]{:S(2)}) collective-permute-start(f32[256,128]{1,0:T(8,128)S(1)} %bitcast.46), channel_id=1, source_target_pairs={{0,1},{2,3},{1,0},{3,2},{4,5},{6,7},{5,4},{7,6},{8,9},{10,11},{9,8... | collective-permute-start | bytes 393224 | tf_op jit(solution)/shard_map/ppermute | solution.py:525
  9.3 13.2 %collective-permute-start.2 = (f32[160,128]{1,0:T(8,128)S(1)}, f32[160,128]{1,0:T(8,128)S(1)}, u32[]{:S(2)}, u32[]{:S(2)}) collective-permute-start(f32[160,128]{1,0:T(8,128)S(1)} %pad_maximum_fusion.sent_a), channel_id=1, source_target_pairs={{0,4},{8,12},{16,20},{24,28},{4,0},{12,8},{20,16},{28,24},{1,5},{9... | collective-permute-start | bytes 245768 | tf_op jit(solution)/shard_map/ppermute | solution.py:535
  10.6 12.0 %collective-permute-start.3 = (f32[160,128]{1,0:T(8,128)S(1)}, f32[160,128]{1,0:T(8,128)S(1)}, u32[]{:S(2)}, u32[]{:S(2)}) collective-permute-start(f32[160,128]{1,0:T(8,128)S(1)} %pad_maximum_fusion.1.sent_b), channel_id=1, source_target_pairs={{4,8},{12,16},{20,24},{8,4},{16,12},{24,20},{5,9},{13,17},{21,25},... | collective-permute-start | bytes 245768 | tf_op jit(solution)/shard_map/ppermute | solution.py:535
  22.6 28.8 %copy-start.5 = (bf16[16,128]{1,0:T(8,128)(2,1)S(1)}, bf16[16,128]{1,0:T(8,128)(2,1)}, u32[]{:S(2)}) copy-start(bf16[16,128]{1,0:T(8,128)(2,1)} %constant.72.modes_ref) | copy-start | bytes 12292
  35.5 3.9 %collective-permute-start.4 = (f32[256,128]{1,0:T(8,128)S(1)}, f32[256,128]{1,0:T(8,128)S(1)}, u32[]{:S(2)}, u32[]{:S(2)}) collective-permute-start(f32[256,128]{1,0:T(8,128)S(1)} %get-tuple-element.25), channel_id=1, source_target_pairs={{0,1},{2,3},{1,0},{3,2},{4,5},{6,7},{5,4},{7,6},{8,9},{10,11},{9,8... | collective-permute-start | bytes 393224 | tf_op jit(solution)/shard_map/ppermute | solution.py:525
  36.6 6.3 %collective-permute-start.5 = (f32[256,128]{1,0:T(8,128)S(1)}, f32[256,128]{1,0:T(8,128)S(1)}, u32[]{:S(2)}, u32[]{:S(2)}) collective-permute-start(f32[256,128]{1,0:T(8,128)S(1)} %get-tuple-element.26), channel_id=1, source_target_pairs={{1,2},{2,1},{5,6},{6,5},{9,10},{10,9},{13,14},{14,13},{17,18},{18,... | collective-permute-start | bytes 393224 | tf_op jit(solution)/shard_map/ppermute | solution.py:525
  42.9 5.1 %collective-permute-start.6 = (f32[160,128]{1,0:T(8,128)S(1)}, f32[160,128]{1,0:T(8,128)S(1)}, u32[]{:S(2)}, u32[]{:S(2)}) collective-permute-start(f32[160,128]{1,0:T(8,128)S(1)} %pad_maximum_fusion.2), channel_id=1, source_target_pairs={{0,4},{8,12},{16,20},{24,28},{4,0},{12,8},{20,16},{28,24},{1,5},{9... | collective-permute-start | bytes 245768 | tf_op jit(solution)/shard_map/ppermute | solution.py:535
  45.3 6.1 %collective-permute-start.7 = (f32[160,128]{1,0:T(8,128)S(1)}, f32[160,128]{1,0:T(8,128)S(1)}, u32[]{:S(2)}, u32[]{:S(2)}) collective-permute-start(f32[160,128]{1,0:T(8,128)S(1)} %pad_maximum_fusion.3), channel_id=1, source_target_pairs={{4,8},{12,16},{20,24},{8,4},{16,12},{24,20},{5,9},{13,17},{21,25},... | collective-permute-start | bytes 245768 | tf_op jit(solution)/shard_map/ppermute | solution.py:535
  51.4 40.1 %copy-start.2 = (bf16[128,512]{1,0:T(8,128)(2,1)S(1)}, bf16[128,512]{1,0:T(8,128)(2,1)}, u32[]{:S(2)}) copy-start(bf16[128,512]{1,0:T(8,128)(2,1)} %constant.61.clone.place_ref) | copy-start | bytes 393220
  63.6 44.0 %copy-start.4 = (bf16[64,128]{1,0:T(8,128)(2,1)S(1)}, bf16[64,128]{1,0:T(8,128)(2,1)}, u32[]{:S(2)}) copy-start(bf16[64,128]{1,0:T(8,128)(2,1)} %constant.63.clone.order_ref) | copy-start | bytes 49156
  96.7 16.3 %copy-start.1 = (bf16[128,512]{1,0:T(8,128)(2,1)S(1)}, bf16[128,512]{1,0:T(8,128)(2,1)}, u32[]{:S(2)}) copy-start(bf16[128,512]{1,0:T(8,128)(2,1)} %constant.62.clone.place_ref) | copy-start | bytes 393220
  96.7 3.5 %collective-permute-start.8 = (f32[128,128]{1,0:T(8,128)S(1)}, f32[128,128]{1,0:T(8,128)S(1)}, u32[]{:S(2)}, u32[]{:S(2)}) collective-permute-start(f32[128,128]{1,0:T(8,128)S(1)} %get-tuple-element.35), channel_id=1, source_target_pairs={{0,1},{2,3},{1,0},{3,2},{4,5},{6,7},{5,4},{7,6},{8,9},{10,11},{9,8... | collective-permute-start | bytes 196616 | tf_op jit(solution)/shard_map/ppermute | solution.py:525
  98.1 5.6 %collective-permute-start.9 = (f32[128,128]{1,0:T(8,128)S(1)}, f32[128,128]{1,0:T(8,128)S(1)}, u32[]{:S(2)}, u32[]{:S(2)}) collective-permute-start(f32[128,128]{1,0:T(8,128)S(1)} %get-tuple-element.36), channel_id=1, source_target_pairs={{1,2},{2,1},{5,6},{6,5},{9,10},{10,9},{13,14},{14,13},{17,18},{18,... | collective-permute-start | bytes 196616 | tf_op jit(solution)/shard_map/ppermute | solution.py:525
  103.7 9.3 %collective-permute-start.10 = (f32[80,128]{1,0:T(8,128)S(1)}, f32[80,128]{1,0:T(8,128)S(1)}, u32[]{:S(2)}, u32[]{:S(2)}) collective-permute-start(f32[80,128]{1,0:T(8,128)S(1)} %pad_maximum_fusion.4), channel_id=1, source_target_pairs={{0,4},{8,12},{16,20},{24,28},{4,0},{12,8},{20,16},{28,24},{1,5},{9... | collective-permute-start | bytes 122888 | tf_op jit(solution)/shard_map/ppermute | solution.py:535
  104.1 8.9 %collective-permute-start.11 = (f32[80,128]{1,0:T(8,128)S(1)}, f32[80,128]{1,0:T(8,128)S(1)}, u32[]{:S(2)}, u32[]{:S(2)}) collective-permute-start(f32[80,128]{1,0:T(8,128)S(1)} %pad_maximum_fusion.5), channel_id=1, source_target_pairs={{4,8},{12,16},{20,24},{8,4},{16,12},{24,20},{5,9},{13,17},{21,25},... | collective-permute-start | bytes 122888 | tf_op jit(solution)/shard_map/ppermute | solution.py:535

commit v3 on v2

--- a/solution.py
+++ b/solution.py
@@ -99,7 +99,7 @@
     return (i + 1) * wide + j + 1 if k == 0 else near_ref[b * KS + k]
 
 
-def prepare_kernel(height, across, ints_ref, a_hbm, tv_ref, fold_ref, sent_a, sent_b, at_ref, rd_ref, v_ref, buf, rep_ref, sem):
+def prepare_kernel(height, across, ints_ref, a_hbm, tv_ref, fold_ref, turn_ref, sent_a, sent_b, at_ref, rd_ref, v_ref, buf, rep_ref, sem):
     tiles = KS * PAIRS
     chunk = tiles * across
     depth = buf.shape[0]
@@ -112,9 +112,9 @@
 
     for i in range(depth - 1):
         copy(i).start()
-    low = lane_iota(PAIRS) < 64
-    row = row_iota(BLK)
-    on_diagonal = lane_iota(BLK) == 2 * (row & (PAIRS - 1)) + row // PAIRS
+    low = lane_iota(2 * PAIRS) < 64
+    lane = lane_iota(PAIRS)
+    on_diagonal = (lane & (BLK - 1)) == 2 * row_iota(PAIRS) + lane // BLK
 
     def body(i, carry):
         @pl.when(i + depth - 1 < height)
@@ -129,17 +129,20 @@
             def part(k):
                 return buf[slot, pl.ds(k * PAIRS * across + j, PAIRS, stride=across), :]
 
-            for t in range(3):
-                x = part(2 * t)
-                y = part(2 * t + 1) if t < 2 else jnp.zeros((PAIRS, LANES), F32)
-                y_turned = roll(y, 64) if t < 2 else y
-                m = jnp.concatenate(
-                    [jnp.where(low, x, y_turned), jnp.where(low, roll(x, 64), y)], axis=0
-                )
-                at_ref[b, :, t * LANES : (t + 1) * LANES] = split(m)
-                if t == 0:
-                    d = jnp.sum(jnp.where(on_diagonal, m, 0.0), axis=0, keepdims=True)
-                    rd_ref[pl.ds(b, 1), :] = OMEGA / (d + roll(d, 64))
+            for first, slots in ((0, 2), (2, 2), (4, 1)):
+                halves = []
+                for k in range(first, first + slots):
+                    x = part(k)
+                    if k == 0:
+                        d = jnp.sum(jnp.where(on_diagonal, x, 0.0), axis=0, keepdims=True)
+                        rd_ref[pl.ds(b, 1), :] = OMEGA / (d + roll(d, 64))
+                    m = split(x)
+                    zero = jnp.zeros_like(m)
+                    halves += [jnp.where(low, m, zero), jnp.where(low, zero, m)]
+                y = mm_t(turn_ref[...], jnp.concatenate(halves, axis=0)).astype(BF16)
+                for u in range(slots):
+                    k = first + u
+                    at_ref[b, k * BLK : (k + 1) * BLK, :] = y[:, u * LANES : (u + 1) * LANES]
             v_ref[pl.ds(b * NV, NV), :] = rows_to_columns(
                 tv_ref[pl.ds(i * VROWS * across + j, VROWS, stride=across), :],
                 fold_ref, rep_ref.at[j],
@@ -156,43 +159,56 @@
     return row_a, height + 1 - row_a, col_a, across + 1 - col_a
 
 
-def sweep_core(height, across, near_ref, meta_ref, at_ref, rd_ref, v_ref, halo, u_ref, convert, store):
+def fill_own(height, across, meta_ref, v_ref, pencil, u_ref, convert):
     wide = across + 2
-    pa_ref, pb_ref, sa_ref, sb_ref = halo
-    row_a, row_b, col_a, col_b = halo_slots(meta_ref, height, across)
+    _, _, col_a, col_b = halo_slots(meta_ref, height, across)
 
     def own(i, carry):
         for j in range(across):
             u_ref[(i + 1) * wide + j + 1] = split(v_ref[pl.ds((i * across + j) * NV, NV), :])
-        for s, (ref, col) in enumerate(((pa_ref, col_a), (pb_ref, col_b))):
+        for s, (ref, col) in enumerate(zip(pencil, (col_a, col_b))):
             u_ref[(i + 1) * wide + col] = split(convert(ref[pl.ds(i * VROWS, VROWS), :], s))
         return carry
 
-    lax.fori_loop(0, height, own, 0)
-    for s, (ref, row) in enumerate(((sa_ref, row_a), (sb_ref, row_b))):
+    lax.fori_loop(0, height, own, 0, unroll=2)
+
+
+def fill_slab(height, across, meta_ref, slab, u_ref, convert):
+    wide = across + 2
+    row_a, row_b, col_a, col_b = halo_slots(meta_ref, height, across)
+    for s, (ref, row) in enumerate(zip(slab, (row_a, row_b))):
         for j in range(wide):
             col = j + 1 if j < across else (col_a if j == across else col_b)
             u_ref[row * wide + col] = split(
                 convert(ref[j * VROWS : (j + 1) * VROWS, :], (s * wide + j) % across)
             )
+
+
+def sweep_rows(height, across, first, last, near_ref, at_ref, rd_ref, v_ref, u_ref, out_ref):
+    wide = across + 2
     low = lane_iota(2 * NV) < 64
     cell = lane_iota(NV) & (BLK - 1)
-    stored = (cell & 1) * PAIRS + cell // 2
+    stored = (cell & 1) * BLK + cell // 2
 
     def body(i, carry):
         for j in range(across):
             b = i * across + j
             u = [u_ref[neighbour(near_ref, b, i, j, k, wide)] for k in range(KS)]
             left = jnp.concatenate(
-                [jnp.where(low, u[0], u[1]), jnp.where(low, u[2], u[3]), u[4]], axis=1
+                [jnp.where(low, u[0], u[1]), jnp.where(low, u[2], u[3]), u[4][:, :BLK]], axis=1
             )
-            r = mm_t(left, at_ref[b])
+            r = mm(left, at_ref[b])
             s = r[:NV] + r[NV:]
-            s = jnp.take_along_axis(s + roll(s, 64), stored, axis=1)
-            store(i, j, b, v_ref[pl.ds(b * NV, NV), :] - s * rd_ref[pl.ds(b, 1), :])
-        return carry
-
-    lax.fori_loop(0, height, body, 0, unroll=2)
+            s = jnp.take_along_axis(s, stored, axis=1) + jnp.take_along_axis(s, stored + PAIRS, axis=1)
+            at = pl.ds(b * NV, NV)
+            out_ref[at, :] = v_ref[at, :] - s * rd_ref[pl.ds(b, 1), :]
+        return carry
+
+    if last is None:
+        for i in first:
+            body(i, 0)
+    else:
+        lax.fori_loop(first, last, body, 0, unroll=2)
 
 
 def sweep_kernel(height, across, near_ref, meta_ref, at_ref, rd_ref, v_ref, pa, pb, sa, sb, fold_ref,
@@ -200,11 +216,9 @@
     def convert(rows, slot):
         return rows_to_columns(rows, fold_ref, rep_ref.at[slot])
 
-    def store(i, j, b, value):
-        out_ref[pl.ds(b * NV, NV), :] = value
-
-    sweep_core(height, across, near_ref, meta_ref, at_ref, rd_ref, v_ref, (pa, pb, sa, sb),
-               u_ref, convert, store)
+    fill_own(height, across, meta_ref, v_ref, (pa, pb), u_ref, convert)
+    fill_slab(height, across, meta_ref, (sa, sb), u_ref, convert)
+    sweep_rows(height, across, 0, height, near_ref, at_ref, rd_ref, v_ref, u_ref, out_ref)
     row_a, row_b, col_a, col_b = halo_slots(meta_ref, height, across)
 
     def message(i, j):
@@ -222,39 +236,54 @@
             ref[j * VROWS : (j + 1) * VROWS, :] = message(i, j)
 
 
-def last_sweep_kernel(height, across, capacity, per_owner, near_ref, meta_ref, agg_ref, at_ref, rd_ref, v_ref,
-                      pa, pb, sa, sb, modes_ref, out_ref, pay_ref, u_ref):
+def unpack_received(rows, slot):
+    return unpack_columns(rows)
+
+
+def coefficients(across, capacity, per_owner, i, acc, agg_ref, modes_ref, out_ref, pay_ref):
+    hcount = -(-capacity // 4)
+    slot_rows = hcount * NC + 1
+    values = [out_ref[pl.ds((i * across + j) * NV, NV), :] for j in range(across)]
+    for v in values:
+        acc = acc + v * v
+    for g in range(across // capacity):
+        owner = lax.div(agg_ref[i * across + g * capacity], per_owner)
+        for h in range(hcount):
+            upper_rows, lower_rows = [], []
+            for s in range(4):
+                if h * 4 + s < capacity:
+                    both = split(values[g * capacity + h * 4 + s])
+                else:
+                    both = jnp.zeros((2 * NV, LANES), BF16)
+                upper_rows.append(both[:NV])
+                lower_rows.append(both[NV:])
+            r = mm_t(modes_ref[...], jnp.concatenate(upper_rows + lower_rows, axis=0))
+            pay_ref[pl.ds(owner * slot_rows + h * NC, NC), :] = r[:NC, :LANES] + r[:NC, LANES:]
+    return acc
+
+
+def inner_sweep_kernel(height, across, capacity, per_owner, near_ref, meta_ref, agg_ref, at_ref, rd_ref, v_ref,
+                       pa, pb, modes_ref, out_ref, u_ref, pay_ref, acc_ref):
+    fill_own(height, across, meta_ref, v_ref, (pa, pb), u_ref, unpack_received)
+    sweep_rows(height, across, 1, height - 1, near_ref, at_ref, rd_ref, v_ref, u_ref, out_ref)
+    pay_ref[...] = jnp.zeros(pay_ref.shape, F32)
+
+    def coefs(i, acc):
+        return coefficients(across, capacity, per_owner, i, acc, agg_ref, modes_ref, out_ref, pay_ref)
+
+    acc_ref[...] = lax.fori_loop(1, height - 1, coefs, jnp.zeros((NV, LANES), F32), unroll=2)
+
+
+def outer_sweep_kernel(height, across, capacity, per_owner, near_ref, meta_ref, agg_ref, at_ref, rd_ref, v_ref,
+                       sa, sb, modes_ref, acc_ref, out_in, u_in, pay_in, out_ref, u_ref, pay_ref):
     hcount = -(-capacity // 4)
     slot_rows = hcount * NC + 1
     devices = pay_ref.shape[0] // slot_rows
-
-    def store(i, j, b, value):
-        out_ref[pl.ds(b * NV, NV), :] = value
-
-    sweep_core(height, across, near_ref, meta_ref, at_ref, rd_ref, v_ref, (pa, pb, sa, sb),
-               u_ref, lambda rows, slot: unpack_columns(rows), store)
-    pay_ref[...] = jnp.zeros(pay_ref.shape, F32)
-
-    def coefs(i, acc):
-        values = [out_ref[pl.ds((i * across + j) * NV, NV), :] for j in range(across)]
-        for v in values:
-            acc = acc + v * v
-        for g in range(across // capacity):
-            owner = lax.div(agg_ref[i * across + g * capacity], per_owner)
-            for h in range(hcount):
-                upper_rows, lower_rows = [], []
-                for s in range(4):
-                    if h * 4 + s < capacity:
-                        both = split(values[g * capacity + h * 4 + s])
-                    else:
-                        both = jnp.zeros((2 * NV, LANES), BF16)
-                    upper_rows.append(both[:NV])
-                    lower_rows.append(both[NV:])
-                r = mm_t(modes_ref[...], jnp.concatenate(upper_rows + lower_rows, axis=0))
-                pay_ref[pl.ds(owner * slot_rows + h * NC, NC), :] = r[:NC, :LANES] + r[:NC, LANES:]
-        return acc
-
-    acc = lax.fori_loop(0, height, coefs, jnp.zeros((NV, LANES), F32))
+    fill_slab(height, across, meta_ref, (sa, sb), u_ref, unpack_received)
+    sweep_rows(height, across, (0, height - 1), None, near_ref, at_ref, rd_ref, v_ref, u_ref, out_ref)
+    acc = acc_ref[...]
+    for i in (0, height - 1):
+        acc = coefficients(across, capacity, per_owner, i, acc, agg_ref, modes_ref, out_ref, pay_ref)
     square = jnp.concatenate([acc, jnp.zeros((LANES - NV, LANES), F32)], axis=0)
     total = 0.5 * jnp.sum(jnp.transpose(square), axis=0, keepdims=True)
     pay_ref[pl.ds(slot_rows - 1, devices, stride=slot_rows), :] = jnp.where(
@@ -271,7 +300,7 @@
         pay_ref[pl.ds(owner * slot_rows + slot_rows - 1, 1), :] = row
         return carry
 
-    lax.fori_loop(0, height * across // capacity, mark, 0)
+    lax.fori_loop(0, height * across // capacity, mark, 0, unroll=4)
 
 
 def solve_kernel(cells, per_owner, capacity, got_ref, ret_ref, inv_ref):
@@ -388,8 +417,9 @@
 
 
 def cell_rows(parts, place_ref):
-    left = jnp.concatenate([hi_lo_lanes(x) for part in parts for x in part], axis=0).astype(BF16)
-    r = mm(left, place_ref[...])
+    x = jnp.concatenate([x for part in parts for x in part], axis=0)
+    hi = x.astype(BF16)
+    r = mm(jnp.concatenate([hi, (x - hi.astype(F32)).astype(BF16)], axis=1), place_ref[...])
     picks = (lane_iota(8) & (NC - 1)) == row_iota(8)
     out = []
     for n in range(len(parts)):
@@ -444,11 +474,22 @@
                     b = i * across + g * capacity + h * 4 + s
                     tile_ref[pl.ds(b * NC, NC), :] = t
                     tiles.append(t)
-        for q, rows in enumerate(cell_rows([tiles], place_ref)):
-            out_ref[pl.ds((i * TROWS + q) * across, across), :] = rows
         return carry
 
     lax.fori_loop(0, height, body, 0, unroll=2)
+    step = 4 if height % 4 == 0 else 1
+
+    def rows(s, carry):
+        parts = [
+            [tile_ref[pl.ds(((s * step + i) * across + j) * NC, NC), :] for j in range(across)]
+            for i in range(step)
+        ]
+        for n, x in enumerate(cell_rows(parts, place_ref)):
+            at = pl.multiple_of((s * step * TROWS + n) * across, 8)
+            out_ref[pl.ds(at, across), :] = x
+        return carry
+
+    lax.fori_loop(0, height // step, rows, 0)
     row_a, row_b, col_a, col_b = halo_slots(meta_ref, height, across)
 
     def edge(i, carry):
@@ -503,10 +544,14 @@
             ]
             for t in range(3):
                 left = jnp.concatenate(u[2 * t : 2 * t + 2], axis=0)
-                r = mm_t(left, at_ref[b, :, t * LANES : (t + 1) * LANES])
+                if t < 2:
+                    r = mm(left, at_ref[b, t * LANES : (t + 1) * LANES, :])
+                else:
+                    r = mm(left[:, :BLK], at_ref[b, 2 * LANES : 2 * LANES + BLK, :])
                 for s in range(left.shape[0] // (2 * NC)):
-                    x = r[s * 2 * NC : s * 2 * NC + NC] + r[s * 2 * NC + NC : (s + 1) * 2 * NC]
-                    parts[2 * t + s].append(x + roll(x, 64))
+                    parts[2 * t + s].append(
+                        r[s * 2 * NC : s * 2 * NC + NC] + r[s * 2 * NC + NC : (s + 1) * 2 * NC]
+                    )
         for n, rows in enumerate(cell_rows(parts, place_ref)):
             at = pl.multiple_of((i * KS * TROWS + n) * across, 8)
             out_ref[pl.ds(at, across), :] = rows
@@ -547,13 +592,14 @@
     return x.reshape(height, across, features)
 
 
-def call(kernel, outs, ins, scratch=(), limit=LIMIT, specs=None):
+def call(kernel, outs, ins, scratch=(), limit=LIMIT, specs=None, aliases=None):
     return pl.pallas_call(
         kernel,
         out_shape=outs,
         in_specs=specs,
         out_specs=[VM] * len(outs),
         scratch_shapes=list(scratch),
+        input_output_aliases=aliases or {},
         compiler_params=pltpu.CompilerParams(vmem_limit_bytes=limit),
     )(*ins)
 
@@ -597,9 +643,12 @@
     lane = np.arange(LANES)
     fold = jnp.asarray(np.arange(NV)[:, None] == lane[None, :] % NV, BF16)
     place_to = np.arange(TROWS * LANES) // NC
-    place = jnp.asarray((lane[:, None] % BLK) == place_to[None, :], BF16)
-    stored = 2 * (lane % PAIRS) + lane % BLK // PAIRS
-    place_stored = jnp.asarray(stored[:, None] == place_to[None, :], BF16)
+    place_one = ((lane[:, None] % BLK) == place_to[None, :]) & (lane[:, None] < BLK)
+    place = jnp.asarray(np.concatenate([place_one, place_one], axis=0), BF16)
+    turn = jnp.asarray(np.arange(BLK)[:, None] == lane[None, :] % BLK, BF16)
+    stored = 2 * (lane % PAIRS) + lane // BLK
+    place_one = stored[:, None] == place_to[None, :]
+    place_stored = jnp.asarray(np.concatenate([place_one, place_one], axis=0), BF16)
     order_row = np.arange(BLK)
     order = jnp.asarray(((order_row % VROWS) * 4 + order_row // VROWS)[:, None] == lane[None, :], BF16)
     q = mode_table()
@@ -611,14 +660,14 @@
     ints = jnp.concatenate([near, aggs, meta])
     at, rd, v = call(
         functools.partial(prepare_kernel, height, across),
-        [sds(block_rows, 2 * BLK, 3 * LANES, dtype=BF16), sds(block_rows, LANES), sds(block_rows * NV, LANES)],
-        [ints, pltpu.with_memory_space_constraint(lines(a_blocks, KS * BLK * BLK), pltpu.HBM), tv, fold, *sent],
+        [sds(block_rows, KS * BLK, LANES, dtype=BF16), sds(block_rows, LANES), sds(block_rows * NV, LANES)],
+        [ints, pltpu.with_memory_space_constraint(lines(a_blocks, KS * BLK * BLK), pltpu.HBM), tv, fold, turn, *sent],
         [
             pltpu.VMEM((4, chunk, LANES), F32),
             pltpu.VMEM((across, BLK, LANES), F32),
             pltpu.SemaphoreType.DMA((4,)),
         ],
-        specs=[SM, HB, VM, VM, HB, HB],
+        specs=[SM, HB, VM, VM, VM, HB, HB],
         limit=16 * 1024 * 1024,
     )
     field = [pltpu.VMEM((wide * (height + 2), 2 * NV, LANES), BF16)]
@@ -631,12 +680,24 @@
     )
     halo = exchange([ea, eb], [ra, rb], slab_odd, VROWS, height)
     slot_rows = hcount * NC + 1
-    v, pay = call(
-        functools.partial(last_sweep_kernel, height, across, capacity, per_owner),
-        [sds(block_rows * NV, LANES), sds(devices * slot_rows, LANES)],
-        [near, meta, aggs, at, rd, v, *halo, modes],
-        field,
-        specs=[SM, SM, SM] + [VM] * 8,
+    outs = [
+        sds(block_rows * NV, LANES),
+        sds(wide * (height + 2), 2 * NV, LANES, dtype=BF16),
+        sds(devices * slot_rows, LANES),
+    ]
+    sizes = (height, across, capacity, per_owner)
+    *partial, acc = call(
+        functools.partial(inner_sweep_kernel, *sizes),
+        outs + [sds(NV, LANES)],
+        [near, meta, aggs, at, rd, v, *halo[:2], modes],
+        specs=[SM, SM, SM] + [VM] * 6,
+    )
+    v, _, pay = call(
+        functools.partial(outer_sweep_kernel, *sizes),
+        outs,
+        [near, meta, aggs, at, rd, v, *halo[2:], modes, acc, *partial],
+        specs=[SM, SM, SM] + [VM] * 10,
+        aliases={10: 0, 11: 1, 12: 2},
     )
     got = lax.all_to_all(
         pay.reshape(devices, slot_rows * LANES), ("slab", "pencil"), split_axis=0, concat_axis=0, tiled=True

time: 127 us -> 113 us (0.89)
  Pallas kernels: 60.2 us -> 49.7 us
  waiting for transfers between devices: 11.2 us -> 7.03 us
    pallas_call x7 -> x8, Pallas kernels: 60.2 us -> 49.7 us  [call(): pl.pallas_call(kernel, out_shape=outs, in_specs=specs, out_specs=[VM] * l...]
    ppermute x6, waiting for transfers between devices: 4.17 us -> 0.03 us  [exchange(): out.append(lax.ppermute(message, 'slab', swaps(slabs, s)))]
  transfers between devices with their start and end apart: 12 -> 12, of which waited for: 4 -> 2; matrix products, arithmetic and copies ran while one was open for 2% -> 3% of each run, Pallas kernels for 12% -> 23%
where the time goes in v3:
time: 113 us; the launch traced here: 112 us
  Pallas kernels  49.7 us (44%)
  blocking collectives  26.8 us (24%)
  starting transfers between devices  22.7 us (20%)
  waiting for transfers between devices  7.03 us (6%)
  local copies, waits for them, and re-layouts  3.08 us (3%)
  other arithmetic  1.89 us (2%)
    pallas_call x8, Pallas kernels, call(): pl.pallas_call(kernel, out_shape=outs, in_specs=specs, out_specs=[VM] * l...  49.7 us
    all_to_all x1, blocking collectives, shards(): lax.all_to_all(pay.reshape(devices, slot_rows * LANES), ('slab', 'pencil'...  14 us
    all_to_all x1, blocking collectives, shards(): lax.all_to_all(ret.reshape(devices, hcount * NC * LANES), ('slab', 'penci...  12.8 us
    ppermute x6, starting transfers between devices, exchange(): out.append(lax.ppermute(message, 'slab', swaps(slabs, s)))  11.6 us
    ppermute x6, starting transfers between devices, exchange(): lax.ppermute(e, 'pencil', swaps(pencils, s))  11.1 us
    ppermute x6, waiting for transfers between devices, exchange(): lax.ppermute(e, 'pencil', swaps(pencils, s))  7 us
  transfers between devices with their start and end apart: 12, of which 2 were waited for; matrix products, arithmetic and copies ran while one was open for 3% of the time, Pallas kernels for 23%

profile of v3, /device:TPU:9, one launch (start us, length us, event | category | flops | bytes accessed | tf_op | source)
XLA Modules:
  0.0 112.2 jit_solution(15812272548483235619)
XLA Ops:
  0.7 1.8 %fusion.5 = (f32[16,1,16,128]{3,1,2,0:T(1,128)S(1)}, f32[16,1,16,128]{3,1,2,0:T(1,128)S(1)}) fusion(f32[16,8,16,128]{3,1,2,0:T(8,128)} %bitcast.35), kind=kLoop, calls=%fused_computation.33 | loop fusion | bytes 524288 | tf_op jit(solution)/shard_map/slice | solution.py:635
  2.5 3.7 %collective-permute-start.1 = (f32[256,128]{1,0:T(8,128)S(1)}, f32[256,128]{1,0:T(8,128)S(1)}, u32[]{:S(2)}, u32[]{:S(2)}) collective-permute-start(f32[256,128]{1,0:T(8,128)S(1)} %bitcast.47), channel_id=1, source_target_pairs={{1,2},{2,1},{5,6},{6,5},{9,10},{10,9},{13,14},{14,13},{17,18},{18,... | collective-permute-start | bytes 393224 | tf_op jit(solution)/shard_map/ppermute | solution.py:570
  6.3 0.9 slice_select_fusion
  7.2 0.8 fusion.3
  8.0 0.8 copy.25
  8.8 0.1 reshape.84.agg_ref
  8.8 0.1 copy.24
  9.0 0.2 reshape.83.near_ref
  9.2 0.1 pad_add_fusion.ints_ref
  9.4 1.3 %collective-permute-start.2 = (f32[160,128]{1,0:T(8,128)S(1)}, f32[160,128]{1,0:T(8,128)S(1)}, u32[]{:S(2)}, u32[]{:S(2)}) collective-permute-start(f32[160,128]{1,0:T(8,128)S(1)} %pad_maximum_fusion.sent_a), channel_id=1, source_target_pairs={{0,4},{8,12},{16,20},{24,28},{4,0},{12,8},{20,16},{28,24},{1,5},{9... | collective-permute-start | bytes 245768 | tf_op jit(solution)/shard_map/ppermute | solution.py:580
  10.6 2.0 %collective-permute-start.3 = (f32[160,128]{1,0:T(8,128)S(1)}, f32[160,128]{1,0:T(8,128)S(1)}, u32[]{:S(2)}, u32[]{:S(2)}) collective-permute-start(f32[160,128]{1,0:T(8,128)S(1)} %pad_maximum_fusion.1.sent_b), channel_id=1, source_target_pairs={{4,8},{12,16},{20,24},{8,4},{16,12},{24,20},{5,9},{13,17},{21,25},... | collective-permute-start | bytes 245768 | tf_op jit(solution)/shard_map/ppermute | solution.py:580
  12.7 0.1 pad_add_fusion.1.meta_ref
  12.8 14.5 %shard_map.130 = (bf16[128,320,128]{2,1,0:T(8,128)(2,1)S(1)}, f32[128,128]{1,0:T(8,128)S(1)}, f32[4096,128]{1,0:T(8,128)S(1)}) custom-call(s32[770]{0:T(1024)S(1)} %pad_add_fusion.ints_ref, f32[20480,128]{1,0:T(8,128)} %bitcast.41, f32[2048,128]{1,0:T(8,128)S(1)} %bitcast.36, bf16[32,128]{1,0:T(8,128)(2,1)S(1)} %copy-done.3, bf16[64,128]{1,0:T(8,128)(2,1)S(1)} %copy-done.5, ...), custom_call_target="tpu_custom_call" | custom-call | tf_op jit(solution)/shard_map/pallas_call | solution.py:596
  27.3 7.8 %shard_map.131 = (f32[4096,128]{1,0:T(8,128)S(1)}, f32[256,128]{1,0:T(8,128)S(1)}, f32[256,128]{1,0:T(8,128)S(1)}, f32[128,128]{1,0:T(8,128)S(1)}, f32[128,128]{1,0:T(8,128)S(1)}) custom-call(s32[640]{0:T(1024)S(1)} %reshape.83.near_ref, s32[2]{0:T(128)S(1)} %pad_add_fusion.1.meta_ref, bf16[128,320,128]{2,1,0:T(8,128)(2,1)S(1)} %get-tuple-element.25.at_ref, ...), custom_call_target="tpu_custom_call" | custom-call | tf_op jit(solution)/shard_map/pallas_call | solution.py:596
  35.1 1.1 collective-permute-start.4
  36.2 2.7 %collective-permute-start.5 = (f32[256,128]{1,0:T(8,128)S(1)}, f32[256,128]{1,0:T(8,128)S(1)}, u32[]{:S(2)}, u32[]{:S(2)}) collective-permute-start(f32[256,128]{1,0:T(8,128)S(1)} %get-tuple-element.31), channel_id=1, source_target_pairs={{1,2},{2,1},{5,6},{6,5},{9,10},{10,9},{13,14},{14,13},{17,18},{18,... | collective-permute-start | bytes 393224 | tf_op jit(solution)/shard_map/ppermute | solution.py:570
  39.0 3.5 %collective-permute-done.5.pb = f32[256,128]{1,0:T(8,128)S(1)} collective-permute-done((f32[256,128]{1,0:T(8,128)S(1)}, f32[256,128]{1,0:T(8,128)S(1)}, u32[]{:S(2)}, u32[]{:S(2)}) %collective-permute-start.5) | collective-permute-done | bytes 131104 | tf_op jit(solution)/shard_map/ppermute | solution.py:570
  42.5 2.4 %collective-permute-start.6 = (f32[160,128]{1,0:T(8,128)S(1)}, f32[160,128]{1,0:T(8,128)S(1)}, u32[]{:S(2)}, u32[]{:S(2)}) collective-permute-start(f32[160,128]{1,0:T(8,128)S(1)} %pad_maximum_fusion.2), channel_id=1, source_target_pairs={{0,4},{8,12},{16,20},{24,28},{4,0},{12,8},{20,16},{28,24},{1,5},{9... | collective-permute-start | bytes 245768 | tf_op jit(solution)/shard_map/ppermute | solution.py:580
  44.9 1.9 %collective-permute-start.7 = (f32[160,128]{1,0:T(8,128)S(1)}, f32[160,128]{1,0:T(8,128)S(1)}, u32[]{:S(2)}, u32[]{:S(2)}) collective-permute-start(f32[160,128]{1,0:T(8,128)S(1)} %pad_maximum_fusion.3), channel_id=1, source_target_pairs={{4,8},{12,16},{20,24},{8,4},{16,12},{24,20},{5,9},{13,17},{21,25},... | collective-permute-start | bytes 245768 | tf_op jit(solution)/shard_map/ppermute | solution.py:580
  46.9 6.4 %shard_map.132 = (f32[4096,128]{1,0:T(8,128)S(1)}, bf16[180,64,128]{2,1,0:T(8,128)(2,1)S(1)}, f32[544,128]{1,0:T(8,128)S(1)}, f32[32,128]{1,0:T(8,128)S(1)}) custom-call(s32[640]{0:T(1024)S(1)} %reshape.83.near_ref, s32[2]{0:T(128)S(1)} %pad_add_fusion.1.meta_ref, s32[128]{0:T(128)S(1)} %reshape.84.agg_ref, ...), custom_call_target="tpu_custom_call" | custom-call | tf_op jit(solution)/shard_map/pallas_call | solution.py:596
  53.3 1.5 %shard_map.133 = (f32[4096,128]{1,0:T(8,128)S(1)}, bf16[180,64,128]{2,1,0:T(8,128)(2,1)S(1)}, f32[544,128]{1,0:T(8,128)S(1)}) custom-call(s32[640]{0:T(1024)S(1)} %reshape.83.near_ref, s32[2]{0:T(128)S(1)} %pad_add_fusion.1.meta_ref, s32[128]{0:T(128)S(1)} %reshape.84.agg_ref, ...), custom_call_target="tpu_custom_call", output_to_operand_aliasing={{0}: (10, {}), {1}: (11, {}), {2}: (12, {})} | custom-call | tf_op jit(solution)/shard_map/pallas_call | solution.py:596
  54.8 14.0 %all_to_all.18 = f32[32,1,2176]{2,1,0:T(1,128)S(1)} all-to-all(f32[32,1,2176]{2,1,0:T(1,128)S(1)} %bitcast.38), channel_id=1, replica_groups=mesh['slab'=8,'pencil'=4] {'slab','pencil'}, dimensions={0} | all-to-all | bytes 557056 | tf_op jit(solution)/shard_map/all_to_all | solution.py:702
  68.8 1.3 %shard_map.134 = (f32[512,128]{1,0:T(8,128)S(1)}, f32[32,128]{1,0:T(8,128)S(1)}) custom-call(f32[544,128]{1,0:T(8,128)S(1)} %bitcast.37), custom_call_target="tpu_custom_call" | custom-call | tf_op jit(solution)/shard_map/pallas_call | solution.py:596
  70.1 12.8 %all_to_all.19 = f32[32,1,2048]{2,1,0:T(1,128)S(1)} all-to-all(f32[32,1,2048]{2,1,0:T(1,128)S(1)} %bitcast.40), channel_id=1, replica_groups=mesh['slab'=8,'pencil'=4] {'slab','pencil'}, dimensions={0} | all-to-all | bytes 524288 | tf_op jit(solution)/shard_map/all_to_all | solution.py:711
  82.9 3.9 %shard_map.135 = (f32[1024,128]{1,0:T(8,128)S(1)}, f32[512,128]{1,0:T(8,128)}, f32[128,128]{1,0:T(8,128)S(1)}, f32[128,128]{1,0:T(8,128)S(1)}, f32[64,128]{1,0:T(8,128)S(1)}, /*index=5*/f32[64,128]{1,0:T(8,128)S(1)}) custom-call(s32[2]{0:T(128)S(1)} %pad_add_fusion.1.meta_ref, s32[128]{0:T(128)S(1)} %reshape.84.agg_ref, f32[512,128]{1,0:T(8,128)S(1)} %bitcast.39, ...), custom_call_target="tpu_custom_call" | custom-call | tf_op jit(solution)/shard_map/pallas_call | solution.py:596
  86.9 1.4 %collective-permute-start.8 = (f32[128,128]{1,0:T(8,128)S(1)}, f32[128,128]{1,0:T(8,128)S(1)}, u32[]{:S(2)}, u32[]{:S(2)}) collective-permute-start(f32[128,128]{1,0:T(8,128)S(1)} %get-tuple-element.43), channel_id=1, source_target_pairs={{0,1},{2,3},{1,0},{3,2},{4,5},{6,7},{5,4},{7,6},{8,9},{10,11},{9,8... | collective-permute-start | bytes 196616 | tf_op jit(solution)/shard_map/ppermute | solution.py:570
  88.3 2.1 %collective-permute-start.9 = (f32[128,128]{1,0:T(8,128)S(1)}, f32[128,128]{1,0:T(8,128)S(1)}, u32[]{:S(2)}, u32[]{:S(2)}) collective-permute-start(f32[128,128]{1,0:T(8,128)S(1)} %get-tuple-element.44), channel_id=1, source_target_pairs={{1,2},{2,1},{5,6},{6,5},{9,10},{10,9},{13,14},{14,13},{17,18},{18,... | collective-permute-start | bytes 196616 | tf_op jit(solution)/shard_map/ppermute | solution.py:570
  90.4 3.5 %collective-permute-done.9.pb_ref = f32[128,128]{1,0:T(8,128)S(1)} collective-permute-done((f32[128,128]{1,0:T(8,128)S(1)}, f32[128,128]{1,0:T(8,128)S(1)}, u32[]{:S(2)}, u32[]{:S(2)}) %collective-permute-start.9) | collective-permute-done | bytes 65568 | tf_op jit(solution)/shard_map/ppermute | solution.py:570
  93.9 0.4 collective-permute-start.10
  94.3 3.5 %collective-permute-start.11 = (f32[80,128]{1,0:T(8,128)S(1)}, f32[80,128]{1,0:T(8,128)S(1)}, u32[]{:S(2)}, u32[]{:S(2)}) collective-permute-start(f32[80,128]{1,0:T(8,128)S(1)} %pad_maximum_fusion.5), channel_id=1, source_target_pairs={{4,8},{12,16},{20,24},{8,4},{16,12},{24,20},{5,9},{13,17},{21,25},... | collective-permute-start | bytes 122888 | tf_op jit(solution)/shard_map/ppermute | solution.py:580
  97.9 5.3 %shard_map.136 = f32[2048,128]{1,0:T(8,128)} custom-call(f32[4096,128]{1,0:T(8,128)S(1)} %get-tuple-element.37.v_ref, f32[32,128]{1,0:T(8,128)S(1)} %get-tuple-element.39.inv_ref, bf16[64,128]{1,0:T(8,128)(2,1)S(1)} %copy-done.4, f32[1024,128]{1,0:T(8,128)S(1)} %get-tuple-element.41.after_ref.tile_ref), custom_call_target="tpu_custom_call" | custom-call | tf_op jit(solution)/shard_map/pallas_call | solution.py:596
  103.2 9.0 %shard_map.137 = f32[2560,128]{1,0:T(8,128)} custom-call(s32[640]{0:T(1024)S(1)} %reshape.83.near_ref, s32[2]{0:T(128)S(1)} %pad_add_fusion.1.meta_ref, bf16[128,320,128]{2,1,0:T(8,128)(2,1)S(1)} %get-tuple-element.25.at_ref, f32[1024,128]{1,0:T(8,128)S(1)} %get-tuple-element.41.after_ref.tile_ref, f32[128,128]{1,0:T(8,128)S(1)} %collective-permute-done.8.pa_ref, ...), custom_call_target="tpu_custom_call" | custom-call | tf_op jit(solution)/shard_map/pallas_call | solution.py:596
  (40 shorter events, 0.3 us)
Async XLA Ops:
  0.6 12.1 %copy-start.3 = (bf16[32,128]{1,0:T(8,128)(2,1)S(1)}, bf16[32,128]{1,0:T(8,128)(2,1)}, u32[]{:S(2)}) copy-start(bf16[32,128]{1,0:T(8,128)(2,1)} %constant.62.clone.fold_ref) | copy-start | bytes 24580
  0.6 12.1 %copy-start.5 = (bf16[64,128]{1,0:T(8,128)(2,1)S(1)}, bf16[64,128]{1,0:T(8,128)(2,1)}, u32[]{:S(2)}) copy-start(bf16[64,128]{1,0:T(8,128)(2,1)} %constant.64.clone.turn_ref) | copy-start | bytes 49156
  0.7 12.1 %copy-start = (f32[16,8,2048]{2,1,0:T(8,128)S(1)}, f32[16,8,2048]{2,1,0:T(8,128)}, u32[]{:S(2)}) copy-start(f32[16,8,2048]{2,1,0:T(8,128)} %param.14) | copy-start | bytes 3145732
  2.5 6.8 %collective-permute-start.1 = (f32[256,128]{1,0:T(8,128)S(1)}, f32[256,128]{1,0:T(8,128)S(1)}, u32[]{:S(2)}, u32[]{:S(2)}) collective-permute-start(f32[256,128]{1,0:T(8,128)S(1)} %bitcast.47), channel_id=1, source_target_pairs={{1,2},{2,1},{5,6},{6,5},{9,10},{10,9},{13,14},{14,13},{17,18},{18,... | collective-permute-start | bytes 393224 | tf_op jit(solution)/shard_map/ppermute | solution.py:570
  6.3 3.1 %collective-permute-start = (f32[256,128]{1,0:T(8,128)S(1)}, f32[256,128]{1,0:T(8,128)S(1)}, u32[]{:S(2)}, u32[]{:S(2)}) collective-permute-start(f32[256,128]{1,0:T(8,128)S(1)} %bitcast.46), channel_id=1, source_target_pairs={{0,1},{2,3},{1,0},{3,2},{4,5},{6,7},{5,4},{7,6},{8,9},{10,11},{9,8... | collective-permute-start | bytes 393224 | tf_op jit(solution)/shard_map/ppermute | solution.py:570
  9.4 17.9 %collective-permute-start.2 = (f32[160,128]{1,0:T(8,128)S(1)}, f32[160,128]{1,0:T(8,128)S(1)}, u32[]{:S(2)}, u32[]{:S(2)}) collective-permute-start(f32[160,128]{1,0:T(8,128)S(1)} %pad_maximum_fusion.sent_a), channel_id=1, source_target_pairs={{0,4},{8,12},{16,20},{24,28},{4,0},{12,8},{20,16},{28,24},{1,5},{9... | collective-permute-start | bytes 245768 | tf_op jit(solution)/shard_map/ppermute | solution.py:580
  10.6 16.6 %collective-permute-start.3 = (f32[160,128]{1,0:T(8,128)S(1)}, f32[160,128]{1,0:T(8,128)S(1)}, u32[]{:S(2)}, u32[]{:S(2)}) collective-permute-start(f32[160,128]{1,0:T(8,128)S(1)} %pad_maximum_fusion.1.sent_b), channel_id=1, source_target_pairs={{4,8},{12,16},{20,24},{8,4},{16,12},{24,20},{5,9},{13,17},{21,25},... | collective-permute-start | bytes 245768 | tf_op jit(solution)/shard_map/ppermute | solution.py:580
  27.3 19.6 %copy-start.6 = (bf16[16,128]{1,0:T(8,128)(2,1)S(1)}, bf16[16,128]{1,0:T(8,128)(2,1)}, u32[]{:S(2)}) copy-start(bf16[16,128]{1,0:T(8,128)(2,1)} %constant.75.modes_ref) | copy-start | bytes 12292
  35.1 3.9 %collective-permute-start.4 = (f32[256,128]{1,0:T(8,128)S(1)}, f32[256,128]{1,0:T(8,128)S(1)}, u32[]{:S(2)}, u32[]{:S(2)}) collective-permute-start(f32[256,128]{1,0:T(8,128)S(1)} %get-tuple-element.30), channel_id=1, source_target_pairs={{0,1},{2,3},{1,0},{3,2},{4,5},{6,7},{5,4},{7,6},{8,9},{10,11},{9,8... | collective-permute-start | bytes 393224 | tf_op jit(solution)/shard_map/ppermute | solution.py:570
  36.2 6.3 %collective-permute-start.5 = (f32[256,128]{1,0:T(8,128)S(1)}, f32[256,128]{1,0:T(8,128)S(1)}, u32[]{:S(2)}, u32[]{:S(2)}) collective-permute-start(f32[256,128]{1,0:T(8,128)S(1)} %get-tuple-element.31), channel_id=1, source_target_pairs={{1,2},{2,1},{5,6},{6,5},{9,10},{10,9},{13,14},{14,13},{17,18},{18,... | collective-permute-start | bytes 393224 | tf_op jit(solution)/shard_map/ppermute | solution.py:570
  42.5 10.7 %collective-permute-start.6 = (f32[160,128]{1,0:T(8,128)S(1)}, f32[160,128]{1,0:T(8,128)S(1)}, u32[]{:S(2)}, u32[]{:S(2)}) collective-permute-start(f32[160,128]{1,0:T(8,128)S(1)} %pad_maximum_fusion.2), channel_id=1, source_target_pairs={{0,4},{8,12},{16,20},{24,28},{4,0},{12,8},{20,16},{28,24},{1,5},{9... | collective-permute-start | bytes 245768 | tf_op jit(solution)/shard_map/ppermute | solution.py:580
  44.9 8.3 %collective-permute-start.7 = (f32[160,128]{1,0:T(8,128)S(1)}, f32[160,128]{1,0:T(8,128)S(1)}, u32[]{:S(2)}, u32[]{:S(2)}) collective-permute-start(f32[160,128]{1,0:T(8,128)S(1)} %pad_maximum_fusion.3), channel_id=1, source_target_pairs={{4,8},{12,16},{20,24},{8,4},{16,12},{24,20},{5,9},{13,17},{21,25},... | collective-permute-start | bytes 245768 | tf_op jit(solution)/shard_map/ppermute | solution.py:580
  53.3 29.7 %copy-start.2 = (bf16[256,512]{1,0:T(8,128)(2,1)S(1)}, bf16[256,512]{1,0:T(8,128)(2,1)}, u32[]{:S(2)}) copy-start(bf16[256,512]{1,0:T(8,128)(2,1)} %constant.63.clone.place_ref) | copy-start | bytes 786436
  54.8 43.1 %copy-start.4 = (bf16[64,128]{1,0:T(8,128)(2,1)S(1)}, bf16[64,128]{1,0:T(8,128)(2,1)}, u32[]{:S(2)}) copy-start(bf16[64,128]{1,0:T(8,128)(2,1)} %constant.66.clone.order_ref) | copy-start | bytes 49156
  86.9 16.3 %copy-start.1 = (bf16[256,512]{1,0:T(8,128)(2,1)S(1)}, bf16[256,512]{1,0:T(8,128)(2,1)}, u32[]{:S(2)}) copy-start(bf16[256,512]{1,0:T(8,128)(2,1)} %constant.65.clone.place_ref) | copy-start | bytes 786436
  86.9 3.5 %collective-permute-start.8 = (f32[128,128]{1,0:T(8,128)S(1)}, f32[128,128]{1,0:T(8,128)S(1)}, u32[]{:S(2)}, u32[]{:S(2)}) collective-permute-start(f32[128,128]{1,0:T(8,128)S(1)} %get-tuple-element.43), channel_id=1, source_target_pairs={{0,1},{2,3},{1,0},{3,2},{4,5},{6,7},{5,4},{7,6},{8,9},{10,11},{9,8... | collective-permute-start | bytes 196616 | tf_op jit(solution)/shard_map/ppermute | solution.py:570
  88.3 5.6 %collective-permute-start.9 = (f32[128,128]{1,0:T(8,128)S(1)}, f32[128,128]{1,0:T(8,128)S(1)}, u32[]{:S(2)}, u32[]{:S(2)}) collective-permute-start(f32[128,128]{1,0:T(8,128)S(1)} %get-tuple-element.44), channel_id=1, source_target_pairs={{1,2},{2,1},{5,6},{6,5},{9,10},{10,9},{13,14},{14,13},{17,18},{18,... | collective-permute-start | bytes 196616 | tf_op jit(solution)/shard_map/ppermute | solution.py:570
  93.9 9.3 %collective-permute-start.10 = (f32[80,128]{1,0:T(8,128)S(1)}, f32[80,128]{1,0:T(8,128)S(1)}, u32[]{:S(2)}, u32[]{:S(2)}) collective-permute-start(f32[80,128]{1,0:T(8,128)S(1)} %pad_maximum_fusion.4), channel_id=1, source_target_pairs={{0,4},{8,12},{16,20},{24,28},{4,0},{12,8},{20,16},{28,24},{1,5},{9... | collective-permute-start | bytes 122888 | tf_op jit(solution)/shard_map/ppermute | solution.py:580
  94.3 8.9 %collective-permute-start.11 = (f32[80,128]{1,0:T(8,128)S(1)}, f32[80,128]{1,0:T(8,128)S(1)}, u32[]{:S(2)}, u32[]{:S(2)}) collective-permute-start(f32[80,128]{1,0:T(8,128)S(1)} %pad_maximum_fusion.5), channel_id=1, source_target_pairs={{4,8},{12,16},{20,24},{8,4},{16,12},{24,20},{5,9},{13,17},{21,25},... | collective-permute-start | bytes 122888 | tf_op jit(solution)/shard_map/ppermute | solution.py:580

commit v4 on v3

--- a/solution.py
+++ b/solution.py
@@ -78,28 +78,43 @@
     return jnp.dot(a, b, preferred_element_type=F32)
 
 
-def fold_rows(parts):
-    sub = row_iota(8)
+def pick_rows(parts):
+    sub, lane = row_iota(8), lane_iota(8)
     step = 4
     while len(parts) > 1:
         half = len(parts) // 2
-        parts = [
-            jnp.where(
-                (sub & step) == 0,
-                parts[u] + pltpu.roll(parts[u], 8 - step, 0),
-                parts[u + half] + pltpu.roll(parts[u + half], step, 0),
-            )
-            for u in range(half)
-        ]
+        first = (sub & step) == 0
+        same = first == ((lane & step) == 0)
+        merged = []
+        for u in range(half):
+            a, b = parts[u], parts[u + half]
+            other = jnp.where(first, b, a)
+            turned = pltpu.roll(other, step, 0)
+            if step < 4:
+                turned = jnp.where(first, pltpu.roll(other, 8 - step, 0), turned)
+            merged.append(jnp.where(same, jnp.where(first, a, b), turned))
+        parts = merged
         step //= 2
     return parts[0]
 
 
 def neighbour(near_ref, b, i, j, k, wide):
-    return (i + 1) * wide + j + 1 if k == 0 else near_ref[b * KS + k]
-
-
-def prepare_kernel(height, across, ints_ref, a_hbm, tv_ref, fold_ref, turn_ref, sent_a, sent_b, at_ref, rd_ref, v_ref, buf, rep_ref, sem):
+    return (i + 1) * wide + j + 1 if k == 0 else near_ref[b * (KS + 1) + k]
+
+
+def edge_kernel(height, across, meta_ref, tv_ref, ea_ref, eb_ref, ra_ref, rb_ref):
+    row_a, row_b, col_a, col_b = halo_slots(meta_ref, height, across)
+    for ref, col in ((ea_ref, col_a), (eb_ref, col_b)):
+        j = jnp.where(col == 0, 0, across - 1)
+        ref[...] = tv_ref[pl.ds(j, height * VROWS, stride=across), :]
+    for ref, row in ((ra_ref, row_a), (rb_ref, row_b)):
+        start = jnp.where(row == 0, 0, height - 1) * VROWS * across
+        for j in range(across):
+            ref[j * VROWS : (j + 1) * VROWS, :] = tv_ref[pl.ds(start + j, VROWS, stride=across), :]
+
+
+def prepare_kernel(across, start, stop, ints_ref, a_hbm, tv_ref, fold_ref, turn_ref, *refs):
+    at_ref, rd_ref, v_ref, buf, rep_ref, sem = refs[-6:]
     tiles = KS * PAIRS
     chunk = tiles * across
     depth = buf.shape[0]
@@ -111,13 +126,13 @@
         )
 
     for i in range(depth - 1):
-        copy(i).start()
+        copy(start + i).start()
     low = lane_iota(2 * PAIRS) < 64
     lane = lane_iota(PAIRS)
     on_diagonal = (lane & (BLK - 1)) == 2 * row_iota(PAIRS) + lane // BLK
 
     def body(i, carry):
-        @pl.when(i + depth - 1 < height)
+        @pl.when(i + depth - 1 < stop)
         def _():
             copy(i + depth - 1).start()
 
@@ -149,7 +164,7 @@
             )
         return carry
 
-    lax.fori_loop(0, height, body, 0, unroll=2)
+    lax.fori_loop(start, stop, body, 0)
 
 
 def halo_slots(meta_ref, height, across):
@@ -159,18 +174,27 @@
     return row_a, height + 1 - row_a, col_a, across + 1 - col_a
 
 
-def fill_own(height, across, meta_ref, v_ref, pencil, u_ref, convert):
+def fill_own(height, across, v_ref, u_ref):
     wide = across + 2
-    _, _, col_a, col_b = halo_slots(meta_ref, height, across)
 
     def own(i, carry):
         for j in range(across):
             u_ref[(i + 1) * wide + j + 1] = split(v_ref[pl.ds((i * across + j) * NV, NV), :])
+        return carry
+
+    lax.fori_loop(0, height, own, 0, unroll=2)
+
+
+def fill_pencil(height, across, meta_ref, pencil, u_ref, convert):
+    wide = across + 2
+    _, _, col_a, col_b = halo_slots(meta_ref, height, across)
+
+    def side(i, carry):
         for s, (ref, col) in enumerate(zip(pencil, (col_a, col_b))):
             u_ref[(i + 1) * wide + col] = split(convert(ref[pl.ds(i * VROWS, VROWS), :], s))
         return carry
 
-    lax.fori_loop(0, height, own, 0, unroll=2)
+    lax.fori_loop(0, height, side, 0, unroll=4)
 
 
 def fill_slab(height, across, meta_ref, slab, u_ref, convert):
@@ -184,14 +208,14 @@
             )
 
 
-def sweep_rows(height, across, first, last, near_ref, at_ref, rd_ref, v_ref, u_ref, out_ref):
+def sweep_rows(height, across, first, last, columns, near_ref, at_ref, rd_ref, v_ref, u_ref, out_ref):
     wide = across + 2
     low = lane_iota(2 * NV) < 64
     cell = lane_iota(NV) & (BLK - 1)
     stored = (cell & 1) * BLK + cell // 2
 
     def body(i, carry):
-        for j in range(across):
+        for j in columns:
             b = i * across + j
             u = [u_ref[neighbour(near_ref, b, i, j, k, wide)] for k in range(KS)]
             left = jnp.concatenate(
@@ -208,7 +232,7 @@
         for i in first:
             body(i, 0)
     else:
-        lax.fori_loop(first, last, body, 0, unroll=2)
+        lax.fori_loop(first, last, body, 0, unroll=7 if (last - first) % 7 == 0 else 4)
 
 
 def sweep_kernel(height, across, near_ref, meta_ref, at_ref, rd_ref, v_ref, pa, pb, sa, sb, fold_ref,
@@ -216,9 +240,10 @@
     def convert(rows, slot):
         return rows_to_columns(rows, fold_ref, rep_ref.at[slot])
 
-    fill_own(height, across, meta_ref, v_ref, (pa, pb), u_ref, convert)
+    fill_own(height, across, v_ref, u_ref)
+    fill_pencil(height, across, meta_ref, (pa, pb), u_ref, lambda rows, s: convert(rows, s))
     fill_slab(height, across, meta_ref, (sa, sb), u_ref, convert)
-    sweep_rows(height, across, 0, height, near_ref, at_ref, rd_ref, v_ref, u_ref, out_ref)
+    sweep_rows(height, across, 0, height, range(across), near_ref, at_ref, rd_ref, v_ref, u_ref, out_ref)
     row_a, row_b, col_a, col_b = halo_slots(meta_ref, height, across)
 
     def message(i, j):
@@ -247,7 +272,7 @@
     for v in values:
         acc = acc + v * v
     for g in range(across // capacity):
-        owner = lax.div(agg_ref[i * across + g * capacity], per_owner)
+        owner = lax.div(agg_ref[(i * across + g * capacity) * (KS + 1) + KS], per_owner)
         for h in range(hcount):
             upper_rows, lower_rows = [], []
             for s in range(4):
@@ -262,28 +287,36 @@
     return acc
 
 
-def inner_sweep_kernel(height, across, capacity, per_owner, near_ref, meta_ref, agg_ref, at_ref, rd_ref, v_ref,
-                       pa, pb, modes_ref, out_ref, u_ref, pay_ref, acc_ref):
-    fill_own(height, across, meta_ref, v_ref, (pa, pb), u_ref, unpack_received)
-    sweep_rows(height, across, 1, height - 1, near_ref, at_ref, rd_ref, v_ref, u_ref, out_ref)
+def inner_sweep_kernel(height, across, near_ref, meta_ref, at_ref, rd_ref, v_ref, out_ref, u_ref, mark_ref):
+    fill_own(height, across, v_ref, u_ref)
+    sweep_rows(height, across, 1, height - 1, range(1, across - 1), near_ref, at_ref, rd_ref, v_ref,
+               u_ref, out_ref)
+    mark_ref[...] = jnp.zeros(mark_ref.shape, F32)
+
+
+def side_sweep_kernel(height, across, capacity, per_owner, near_ref, meta_ref, at_ref, rd_ref, v_ref,
+                      pa, pb, modes_ref, out_in, u_in, out_ref, u_ref, pay_ref, acc_ref):
+    fill_pencil(height, across, meta_ref, (pa, pb), u_ref, unpack_received)
+    sweep_rows(height, across, 1, height - 1, (0, across - 1), near_ref, at_ref, rd_ref, v_ref,
+               u_ref, out_ref)
     pay_ref[...] = jnp.zeros(pay_ref.shape, F32)
 
     def coefs(i, acc):
-        return coefficients(across, capacity, per_owner, i, acc, agg_ref, modes_ref, out_ref, pay_ref)
+        return coefficients(across, capacity, per_owner, i, acc, near_ref, modes_ref, out_ref, pay_ref)
 
     acc_ref[...] = lax.fori_loop(1, height - 1, coefs, jnp.zeros((NV, LANES), F32), unroll=2)
 
 
-def outer_sweep_kernel(height, across, capacity, per_owner, near_ref, meta_ref, agg_ref, at_ref, rd_ref, v_ref,
+def outer_sweep_kernel(height, across, capacity, per_owner, near_ref, meta_ref, at_ref, rd_ref, v_ref,
                        sa, sb, modes_ref, acc_ref, out_in, u_in, pay_in, out_ref, u_ref, pay_ref):
     hcount = -(-capacity // 4)
     slot_rows = hcount * NC + 1
     devices = pay_ref.shape[0] // slot_rows
     fill_slab(height, across, meta_ref, (sa, sb), u_ref, unpack_received)
-    sweep_rows(height, across, (0, height - 1), None, near_ref, at_ref, rd_ref, v_ref, u_ref, out_ref)
+    sweep_rows(height, across, (0, height - 1), None, range(across), near_ref, at_ref, rd_ref, v_ref, u_ref, out_ref)
     acc = acc_ref[...]
     for i in (0, height - 1):
-        acc = coefficients(across, capacity, per_owner, i, acc, agg_ref, modes_ref, out_ref, pay_ref)
+        acc = coefficients(across, capacity, per_owner, i, acc, near_ref, modes_ref, out_ref, pay_ref)
     square = jnp.concatenate([acc, jnp.zeros((LANES - NV, LANES), F32)], axis=0)
     total = 0.5 * jnp.sum(jnp.transpose(square), axis=0, keepdims=True)
     pay_ref[pl.ds(slot_rows - 1, devices, stride=slot_rows), :] = jnp.where(
@@ -292,10 +325,10 @@
     lane = lane_iota(1)
 
     def mark(g, carry):
-        owner = lax.div(agg_ref[g * capacity], per_owner)
+        owner = lax.div(near_ref[g * capacity * (KS + 1) + KS], per_owner)
         row = jnp.where(lane < NV, total, -1.0)
         for s in range(capacity):
-            local = agg_ref[g * capacity + s] - owner * per_owner
+            local = near_ref[(g * capacity + s) * (KS + 1) + KS] - owner * per_owner
             row = jnp.where(lane == NV + s, local.astype(F32), row)
         pay_ref[pl.ds(owner * slot_rows + slot_rows - 1, 1), :] = row
         return carry
@@ -413,25 +446,20 @@
             rel_ref[pl.ds(i * VROWS * across + j, VROWS, stride=across), :] = rows
         return carry
 
-    lax.fori_loop(0, height, body, 0, unroll=2)
+    lax.fori_loop(0, height, body, 0, unroll=4)
 
 
 def cell_rows(parts, place_ref):
     x = jnp.concatenate([x for part in parts for x in part], axis=0)
     hi = x.astype(BF16)
     r = mm(jnp.concatenate([hi, (x - hi.astype(F32)).astype(BF16)], axis=1), place_ref[...])
-    picks = (lane_iota(8) & (NC - 1)) == row_iota(8)
     out = []
     for n in range(len(parts)):
         for q in range(TROWS):
             out.append(
-                fold_rows(
+                pick_rows(
                     [
-                        jnp.where(
-                            picks,
-                            r[(n * 8 + u) * 8 : (n * 8 + u + 1) * 8, q * LANES : (q + 1) * LANES],
-                            0.0,
-                        )
+                        r[(n * 8 + u) * 8 : (n * 8 + u + 1) * 8, q * LANES : (q + 1) * LANES]
                         for u in range(8)
                     ]
                 )
@@ -448,7 +476,7 @@
     def body(i, carry):
         tiles = []
         for g in range(across // capacity):
-            owner = lax.div(agg_ref[i * across + g * capacity], per_owner)
+            owner = lax.div(agg_ref[(i * across + g * capacity) * (KS + 1) + KS], per_owner)
             for h in range(hcount):
                 m = ret_ref[pl.ds(pl.multiple_of((owner * hcount + h) * NC, NC), NC), :]
                 m_hi = upper(m)
@@ -557,7 +585,7 @@
             out_ref[pl.ds(at, across), :] = rows
         return carry
 
-    lax.fori_loop(0, height, body, 0, unroll=2)
+    lax.fori_loop(0, height, body, 0, unroll=4)
 
 
 def swaps(count, first):
@@ -565,20 +593,21 @@
     return pairs + [(b, a) for a, b in pairs]
 
 
-def exchange(edges, rows, slab_odd, unit, height, sent=None):
+def exchange(edges, rows, slab_odd, unit, height, work=None):
     pencils, slabs = lax.axis_size("pencil"), lax.axis_size("slab")
     got = [lax.ppermute(e, "pencil", swaps(pencils, s)) for s, e in enumerate(edges)]
-    out = []
+    done = work() if work else None
+    messages = []
     for s, own in enumerate(rows):
         last = (slab_odd == 0) if s == 0 else (slab_odd == 1)
         corners = [
             jnp.where(last, g[(height - 1) * unit : height * unit], g[:unit]) for g in got
         ]
-        message = jnp.concatenate([own] + corners, axis=0)
-        if sent is not None:
-            sent.append(message)
-        out.append(lax.ppermute(message, "slab", swaps(slabs, s)))
-    return got + out
+        messages.append(jnp.concatenate([own] + corners, axis=0))
+    if work:
+        messages = [m + done[-1] for m in messages]
+    out = [lax.ppermute(m, "slab", swaps(slabs, s)) for s, m in enumerate(messages)]
+    return got + out, messages, done
 
 
 def lines(x, features):
@@ -627,18 +656,17 @@
     pencil_odd = lax.axis_index("pencil") % 2
     meta = jnp.stack([slab_odd, pencil_odd]).astype(jnp.int32)
     down = jnp.arange(height, dtype=jnp.int32)[:, None, None] + col_codes // 3
-    near = (down * wide + jnp.arange(across, dtype=jnp.int32)[None, :, None] + col_codes % 3).reshape(-1)
-    aggs = agg_of.reshape(-1)
+    near = down * wide + jnp.arange(across, dtype=jnp.int32)[None, :, None] + col_codes % 3
+    ints = jnp.concatenate([near, agg_of[:, :, None]], axis=2).reshape(-1)
 
     tv = lines(test_vectors, BLK * NV)
-    by_row = test_vectors.reshape(height, across, VROWS, LANES)
-    col_hi, col_lo = by_row[:, across - 1], by_row[:, 0]
-    row_hi, row_lo = by_row[height - 1], by_row[0]
-    flip = lambda odd, a, b: (jnp.where(odd == 0, a, b), jnp.where(odd == 0, b, a))
-    edges = [e.reshape(height * VROWS, LANES) for e in flip(pencil_odd, col_hi, col_lo)]
-    rows = [e.reshape(across * VROWS, LANES) for e in flip(slab_odd, row_hi, row_lo)]
-    sent = []
-    halo = exchange(edges, rows, slab_odd, VROWS, height, sent)
+    *edges, row_one, row_two = call(
+        functools.partial(edge_kernel, height, across),
+        [sds(height * VROWS, LANES)] * 2 + [sds(across * VROWS, LANES)] * 2,
+        [meta, tv],
+        specs=[SM, VM],
+    )
+    rows = [row_one, row_two]
 
     lane = np.arange(LANES)
     fold = jnp.asarray(np.arange(NV)[:, None] == lane[None, :] % NV, BF16)
@@ -657,47 +685,66 @@
     modes = jnp.pad(jnp.concatenate([q_hi, q_lo], axis=1), ((0, NC), (0, 0)))
 
     chunk = KS * PAIRS * across
-    ints = jnp.concatenate([near, aggs, meta])
-    at, rd, v = call(
-        functools.partial(prepare_kernel, height, across),
-        [sds(block_rows, KS * BLK, LANES, dtype=BF16), sds(block_rows, LANES), sds(block_rows * NV, LANES)],
-        [ints, pltpu.with_memory_space_constraint(lines(a_blocks, KS * BLK * BLK), pltpu.HBM), tv, fold, turn, *sent],
-        [
-            pltpu.VMEM((4, chunk, LANES), F32),
-            pltpu.VMEM((across, BLK, LANES), F32),
-            pltpu.SemaphoreType.DMA((4,)),
-        ],
-        specs=[SM, HB, VM, VM, VM, HB, HB],
-        limit=16 * 1024 * 1024,
-    )
+    stored_blocks = pltpu.with_memory_space_constraint(lines(a_blocks, KS * BLK * BLK), pltpu.HBM)
+
+    def prepare(start, stop, earlier, after=()):
+        count = 5 + len(after)
+        return call(
+            functools.partial(prepare_kernel, across, start, stop),
+            [
+                sds(block_rows, KS * BLK, LANES, dtype=BF16),
+                sds(block_rows, LANES),
+                sds(block_rows * NV, LANES),
+            ],
+            [ints, stored_blocks, tv, fold, turn, *after, *earlier],
+            [
+                pltpu.VMEM((4, chunk, LANES), F32),
+                pltpu.VMEM((across, BLK, LANES), F32),
+                pltpu.SemaphoreType.DMA((4,)),
+            ],
+            specs=[SM, HB, VM, VM, VM] + [HB] * len(after) + [VM] * len(earlier),
+            aliases={count + n: n for n in range(len(earlier))},
+        )
+
+    halo, sent, _ = exchange(edges, rows, slab_odd, VROWS, height)
+    at, rd, v = prepare(0, height, [], sent)
     field = [pltpu.VMEM((wide * (height + 2), 2 * NV, LANES), BF16)]
     v, ea, eb, ra, rb = call(
         functools.partial(sweep_kernel, height, across),
         [sds(block_rows * NV, LANES)] + [sds(height * VROWS, LANES)] * 2 + [sds(across * VROWS, LANES)] * 2,
-        [near, meta, at, rd, v, *halo, fold],
+        [ints, meta, at, rd, v, *halo, fold],
         field + [pltpu.VMEM((across, BLK, LANES), F32)],
         specs=[SM, SM] + [VM] * 8,
     )
-    halo = exchange([ea, eb], [ra, rb], slab_odd, VROWS, height)
-    slot_rows = hcount * NC + 1
     outs = [
         sds(block_rows * NV, LANES),
         sds(wide * (height + 2), 2 * NV, LANES, dtype=BF16),
-        sds(devices * slot_rows, LANES),
     ]
+    halo, _, partial = exchange(
+        [ea, eb], [ra, rb], slab_odd, VROWS, height,
+        lambda: call(
+            functools.partial(inner_sweep_kernel, height, across),
+            outs + [sds(wide * VROWS, LANES)],
+            [ints, meta, at, rd, v],
+            specs=[SM, SM] + [VM] * 3,
+        ),
+    )
+    slot_rows = hcount * NC + 1
+    outs = outs + [sds(devices * slot_rows, LANES)]
     sizes = (height, across, capacity, per_owner)
     *partial, acc = call(
-        functools.partial(inner_sweep_kernel, *sizes),
+        functools.partial(side_sweep_kernel, *sizes),
         outs + [sds(NV, LANES)],
-        [near, meta, aggs, at, rd, v, *halo[:2], modes],
-        specs=[SM, SM, SM] + [VM] * 6,
+        [ints, meta, at, rd, v, *halo[:2], modes, *partial[:2]],
+        specs=[SM, SM] + [VM] * 8,
+        aliases={8: 0, 9: 1},
     )
     v, _, pay = call(
         functools.partial(outer_sweep_kernel, *sizes),
         outs,
-        [near, meta, aggs, at, rd, v, *halo[2:], modes, acc, *partial],
-        specs=[SM, SM, SM] + [VM] * 10,
-        aliases={10: 0, 11: 1, 12: 2},
+        [ints, meta, at, rd, v, *halo[2:], modes, acc, *partial],
+        specs=[SM, SM] + [VM] * 10,
+        aliases={9: 0, 10: 1, 11: 2},
     )
     got = lax.all_to_all(
         pay.reshape(devices, slot_rows * LANES), ("slab", "pencil"), split_axis=0, concat_axis=0, tiled=True
@@ -715,7 +762,7 @@
         functools.partial(tile_kernel, height, across, capacity, per_owner),
         [sds(block_rows * NC, LANES), sds(block_rows * TROWS, LANES)]
         + [sds(height * NC, LANES)] * 2 + [sds(across * NC, LANES)] * 2,
-        [meta, aggs, back, v, inv, place],
+        [meta, ints, back, v, inv, place],
         specs=[SM, SM, VM, VM, VM, VM],
     )
     (relaxed,) = call(
@@ -724,11 +771,11 @@
         [v, inv, order, tile],
         specs=[VM] * 4,
     )
-    halo = exchange([ea, eb], [ra, rb], slab_odd, NC, height)
+    halo, _, _ = exchange([ea, eb], [ra, rb], slab_odd, NC, height)
     (products,) = call(
         functools.partial(product_kernel, height, across),
         [sds(block_rows * KS * TROWS, LANES)],
-        [near, meta, at, tile, *halo, place_stored],
+        [ints, meta, at, tile, *halo, place_stored],
         [pltpu.VMEM((wide * (height + 2), 4 * NC, LANES), BF16)],
         specs=[SM, SM] + [VM] * 7,
     )

time: 113 us -> 110 us (0.973)
  Pallas kernels: 49.7 us -> 47.8 us
    pallas_call x8 -> x10, Pallas kernels: 49.7 us -> 47.8 us  [call(): pl.pallas_call(kernel, out_shape=outs, in_specs=specs, out_specs=[VM] * l...]
    unnamed x15 -> x16, local copies, waits for them, and re-layouts: 0.8 us -> 2.66 us
    slice x1 -> x0, local copies, waits for them, and re-layouts: 1.82 us -> none  [shards(): col_hi, col_lo = (by_row[:, across - 1], by_row[:, 0])]
    all_to_all x1, blocking collectives: 14 us -> 15.1 us  [shards(): lax.all_to_all(pay.reshape(devices, slot_rows * LANES), ('slab', 'pencil'...]
  transfers between devices with their start and end apart: 12 -> 12, of which waited for: 2 -> 2; matrix products, arithmetic and copies ran while one was open for 3% -> 2% of each run, Pallas kernels for 23% -> 23%
where the time goes in v4:
time: 110 us
  Pallas kernels  47.8 us (43%)
  blocking collectives  27.9 us (25%)
  starting transfers between devices  22.7 us (21%)
  waiting for transfers between devices  5.95 us (5%)
  local copies, waits for them, and re-layouts  2.93 us (3%)
  other arithmetic  1.61 us (1%)
    pallas_call x10, Pallas kernels, call(): pl.pallas_call(kernel, out_shape=outs, in_specs=specs, out_specs=[VM] * l...  47.8 us
    all_to_all x1, blocking collectives, shards(): lax.all_to_all(pay.reshape(devices, slot_rows * LANES), ('slab', 'pencil'...  15.1 us
    all_to_all x1, blocking collectives, shards(): lax.all_to_all(ret.reshape(devices, hcount * NC * LANES), ('slab', 'penci...  12.8 us
    ppermute x6, starting transfers between devices, exchange(): lax.ppermute(m, 'slab', swaps(slabs, s))  11.6 us
    ppermute x6, starting transfers between devices, exchange(): lax.ppermute(e, 'pencil', swaps(pencils, s))  11.1 us
    ppermute x6, waiting for transfers between devices, exchange(): lax.ppermute(e, 'pencil', swaps(pencils, s))  5.93 us
    unnamed x16, local copies, waits for them, and re-layouts  2.66 us
  transfers between devices with their start and end apart: 12, of which 2 were waited for; matrix products, arithmetic and copies ran while one was open for 2% of the time, Pallas kernels for 23%

profile of v4, /device:TPU:9, one launch (start us, length us, event | category | flops | bytes accessed | tf_op | source)
XLA Modules:
  0.0 109.8 jit_solution(812950787102043972)
XLA Ops:
  0.7 1.2 %copy-done = f32[16,8,2048]{2,1,0:T(8,128)S(1)} copy-done((f32[16,8,2048]{2,1,0:T(8,128)S(1)}, f32[16,8,2048]{2,1,0:T(8,128)}, u32[]{:S(2)}) %copy-start) | copy-done | bytes 1048600
  2.0 0.6 shard_map.130
  2.6 0.7 collective-permute-start
  3.3 3.0 %collective-permute-start.1 = (f32[256,128]{1,0:T(8,128)S(1)}, f32[256,128]{1,0:T(8,128)S(1)}, u32[]{:S(2)}, u32[]{:S(2)}) collective-permute-start(f32[256,128]{1,0:T(8,128)S(1)} %get-tuple-element.34), channel_id=1, source_target_pairs={{1,2},{2,1},{5,6},{6,5},{9,10},{10,9},{13,14},{14,13},{17,18},{18,... | collective-permute-start | bytes 393224 | tf_op jit(solution)/shard_map/ppermute | solution.py:598
  6.4 0.8 fusion.3
  7.2 2.4 %collective-permute-done.1.pb = f32[256,128]{1,0:T(8,128)S(1)} collective-permute-done((f32[256,128]{1,0:T(8,128)S(1)}, f32[256,128]{1,0:T(8,128)S(1)}, u32[]{:S(2)}, u32[]{:S(2)}) %collective-permute-start.1) | collective-permute-done | bytes 131104 | tf_op jit(solution)/shard_map/ppermute | solution.py:598
  9.6 1.3 %collective-permute-start.2 = (f32[160,128]{1,0:T(8,128)S(1)}, f32[160,128]{1,0:T(8,128)S(1)}, u32[]{:S(2)}, u32[]{:S(2)}) collective-permute-start(f32[160,128]{1,0:T(8,128)S(1)} %pad_maximum_fusion.refs_0_), channel_id=1, source_target_pairs={{0,4},{8,12},{16,20},{24,28},{4,0},{12,8},{20,16},{28,24},{1,5},{9... | collective-permute-start | bytes 245768 | tf_op jit(solution)/shard_map/ppermute | solution.py:609
  10.9 1.9 %collective-permute-start.3 = (f32[160,128]{1,0:T(8,128)S(1)}, f32[160,128]{1,0:T(8,128)S(1)}, u32[]{:S(2)}, u32[]{:S(2)}) collective-permute-start(f32[160,128]{1,0:T(8,128)S(1)} %pad_maximum_fusion.1.refs_1_), channel_id=1, source_target_pairs={{4,8},{12,16},{20,24},{8,4},{16,12},{24,20},{5,9},{13,17},{21,25},... | collective-permute-start | bytes 245768 | tf_op jit(solution)/shard_map/ppermute | solution.py:609
  12.8 0.7 pad_add_fusion
  13.5 0.1 copy.20
  13.7 0.1 reshape.55.ints_ref.near_ref.agg_ref
  13.8 0.7 copy-done.4
  14.5 0.7 copy-done.6
  15.2 14.5 %shard_map.131 = (bf16[128,320,128]{2,1,0:T(8,128)(2,1)S(1)}, f32[128,128]{1,0:T(8,128)S(1)}, f32[4096,128]{1,0:T(8,128)S(1)}) custom-call(s32[768]{0:T(1024)S(1)} %reshape.55.ints_ref.near_ref.agg_ref, f32[20480,128]{1,0:T(8,128)} %bitcast.38, f32[2048,128]{1,0:T(8,128)S(1)} %bitcast.33, bf16[32,128]{1,0:T(8,128)(2,1)S(1)} %copy-done.4, ...), custom_call_target="tpu_custom_call" | custom-call | tf_op jit(solution)/shard_map/pallas_call | solution.py:625
  29.7 6.5 %shard_map.132 = (f32[4096,128]{1,0:T(8,128)S(1)}, f32[256,128]{1,0:T(8,128)S(1)}, f32[256,128]{1,0:T(8,128)S(1)}, f32[128,128]{1,0:T(8,128)S(1)}, f32[128,128]{1,0:T(8,128)S(1)}) custom-call(s32[768]{0:T(1024)S(1)} %reshape.55.ints_ref.near_ref.agg_ref, s32[2]{0:T(128)S(1)} %pad_add_fusion.1.meta_ref, bf16[128,320,128]{2,1,0:T(8,128)(2,1)S(1)} %get-tuple-element.36.at_ref, ...), custom_call_target="tpu_custom_call" | custom-call | tf_op jit(solution)/shard_map/pallas_call | solution.py:625
  36.3 3.7 %collective-permute-start.5 = (f32[256,128]{1,0:T(8,128)S(1)}, f32[256,128]{1,0:T(8,128)S(1)}, u32[]{:S(2)}, u32[]{:S(2)}) collective-permute-start(f32[256,128]{1,0:T(8,128)S(1)} %get-tuple-element.42), channel_id=1, source_target_pairs={{1,2},{2,1},{5,6},{6,5},{9,10},{10,9},{13,14},{14,13},{17,18},{18,... | collective-permute-start | bytes 393224 | tf_op jit(solution)/shard_map/ppermute | solution.py:598
  40.1 3.1 %shard_map.133 = (f32[4096,128]{1,0:T(8,128)S(1)}, bf16[180,64,128]{2,1,0:T(8,128)(2,1)S(1)}, f32[160,128]{1,0:T(8,128)S(1)}) custom-call(s32[768]{0:T(1024)S(1)} %reshape.55.ints_ref.near_ref.agg_ref, s32[2]{0:T(128)S(1)} %pad_add_fusion.1.meta_ref, bf16[128,320,128]{2,1,0:T(8,128)(2,1)S(1)} %get-tuple-element.36.at_ref, ...), custom_call_target="tpu_custom_call" | custom-call | tf_op jit(solution)/shard_map/pallas_call | solution.py:625
  43.3 4.1 %collective-permute-start.7 = (f32[160,128]{1,0:T(8,128)S(1)}, f32[160,128]{1,0:T(8,128)S(1)}, u32[]{:S(2)}, u32[]{:S(2)}) collective-permute-start(f32[160,128]{1,0:T(8,128)S(1)} %get-tuple-element.69), channel_id=1, source_target_pairs={{4,8},{12,16},{20,24},{8,4},{16,12},{24,20},{5,9},{13,17},{21,25},... | collective-permute-start | bytes 245768 | tf_op jit(solution)/shard_map/ppermute | solution.py:609
  47.4 0.3 collective-permute-start.6
  47.7 3.3 %shard_map.134 = (f32[4096,128]{1,0:T(8,128)S(1)}, bf16[180,64,128]{2,1,0:T(8,128)(2,1)S(1)}, f32[544,128]{1,0:T(8,128)S(1)}, f32[32,128]{1,0:T(8,128)S(1)}) custom-call(s32[768]{0:T(1024)S(1)} %reshape.55.ints_ref.near_ref.agg_ref, s32[2]{0:T(128)S(1)} %pad_add_fusion.1.meta_ref, ...), custom_call_target="tpu_custom_call", output_to_operand_aliasing={{0}: (8, {}), {1}: (9, {})} | custom-call | tf_op jit(solution)/shard_map/pallas_call | solution.py:625
  51.1 1.6 %shard_map.135 = (f32[4096,128]{1,0:T(8,128)S(1)}, bf16[180,64,128]{2,1,0:T(8,128)(2,1)S(1)}, f32[544,128]{1,0:T(8,128)S(1)}) custom-call(s32[768]{0:T(1024)S(1)} %reshape.55.ints_ref.near_ref.agg_ref, s32[2]{0:T(128)S(1)} %pad_add_fusion.1.meta_ref, ...), custom_call_target="tpu_custom_call", output_to_operand_aliasing={{0}: (9, {}), {1}: (10, {}), {2}: (11, {})} | custom-call | tf_op jit(solution)/shard_map/pallas_call | solution.py:625
  52.7 15.1 %all_to_all.18 = f32[32,1,2176]{2,1,0:T(1,128)S(1)} all-to-all(f32[32,1,2176]{2,1,0:T(1,128)S(1)} %bitcast.34), channel_id=1, replica_groups=mesh['slab'=8,'pencil'=4] {'slab','pencil'}, dimensions={0} | all-to-all | bytes 557056 | tf_op jit(solution)/shard_map/all_to_all | solution.py:749
  67.8 1.3 %shard_map.136 = (f32[512,128]{1,0:T(8,128)S(1)}, f32[32,128]{1,0:T(8,128)S(1)}) custom-call(f32[544,128]{1,0:T(8,128)S(1)} %bitcast.35), custom_call_target="tpu_custom_call" | custom-call | tf_op jit(solution)/shard_map/pallas_call | solution.py:625
  69.2 12.8 %all_to_all.19 = f32[32,1,2048]{2,1,0:T(1,128)S(1)} all-to-all(f32[32,1,2048]{2,1,0:T(1,128)S(1)} %bitcast.37), channel_id=1, replica_groups=mesh['slab'=8,'pencil'=4] {'slab','pencil'}, dimensions={0} | all-to-all | bytes 524288 | tf_op jit(solution)/shard_map/all_to_all | solution.py:758
  82.0 3.9 %shard_map.137 = (f32[1024,128]{1,0:T(8,128)S(1)}, f32[512,128]{1,0:T(8,128)}, f32[128,128]{1,0:T(8,128)S(1)}, f32[128,128]{1,0:T(8,128)S(1)}, f32[64,128]{1,0:T(8,128)S(1)}, /*index=5*/f32[64,128]{1,0:T(8,128)S(1)}) custom-call(s32[2]{0:T(128)S(1)} %pad_add_fusion.1.meta_ref, s32[768]{0:T(1024)S(1)} %reshape.55.ints_ref.near_ref.agg_ref, ...), custom_call_target="tpu_custom_call" | custom-call | tf_op jit(solution)/shard_map/pallas_call | solution.py:625
  85.9 1.4 %collective-permute-start.8 = (f32[128,128]{1,0:T(8,128)S(1)}, f32[128,128]{1,0:T(8,128)S(1)}, u32[]{:S(2)}, u32[]{:S(2)}) collective-permute-start(f32[128,128]{1,0:T(8,128)S(1)} %get-tuple-element.57), channel_id=1, source_target_pairs={{0,1},{2,3},{1,0},{3,2},{4,5},{6,7},{5,4},{7,6},{8,9},{10,11},{9,8... | collective-permute-start | bytes 196616 | tf_op jit(solution)/shard_map/ppermute | solution.py:598
  87.4 2.1 %collective-permute-start.9 = (f32[128,128]{1,0:T(8,128)S(1)}, f32[128,128]{1,0:T(8,128)S(1)}, u32[]{:S(2)}, u32[]{:S(2)}) collective-permute-start(f32[128,128]{1,0:T(8,128)S(1)} %get-tuple-element.58), channel_id=1, source_target_pairs={{1,2},{2,1},{5,6},{6,5},{9,10},{10,9},{13,14},{14,13},{17,18},{18,... | collective-permute-start | bytes 196616 | tf_op jit(solution)/shard_map/ppermute | solution.py:598
  89.4 3.5 %collective-permute-done.9.pb_ref = f32[128,128]{1,0:T(8,128)S(1)} collective-permute-done((f32[128,128]{1,0:T(8,128)S(1)}, f32[128,128]{1,0:T(8,128)S(1)}, u32[]{:S(2)}, u32[]{:S(2)}) %collective-permute-start.9) | collective-permute-done | bytes 65568 | tf_op jit(solution)/shard_map/ppermute | solution.py:598
  92.9 0.4 collective-permute-start.10
  93.4 3.6 %collective-permute-start.11 = (f32[80,128]{1,0:T(8,128)S(1)}, f32[80,128]{1,0:T(8,128)S(1)}, u32[]{:S(2)}, u32[]{:S(2)}) collective-permute-start(f32[80,128]{1,0:T(8,128)S(1)} %pad_maximum_fusion.3), channel_id=1, source_target_pairs={{4,8},{12,16},{20,24},{8,4},{16,12},{24,20},{5,9},{13,17},{21,25},... | collective-permute-start | bytes 122888 | tf_op jit(solution)/shard_map/ppermute | solution.py:609
  96.9 4.6 %shard_map.138 = f32[2048,128]{1,0:T(8,128)} custom-call(f32[4096,128]{1,0:T(8,128)S(1)} %get-tuple-element.51.v_ref, f32[32,128]{1,0:T(8,128)S(1)} %get-tuple-element.53.inv_ref, bf16[64,128]{1,0:T(8,128)(2,1)S(1)} %copy-done.5, f32[1024,128]{1,0:T(8,128)S(1)} %get-tuple-element.55.after_ref.tile_ref), custom_call_target="tpu_custom_call" | custom-call | tf_op jit(solution)/shard_map/pallas_call | solution.py:625
  101.5 8.3 %shard_map.139 = f32[2560,128]{1,0:T(8,128)} custom-call(s32[768]{0:T(1024)S(1)} %reshape.55.ints_ref.near_ref.agg_ref, s32[2]{0:T(128)S(1)} %pad_add_fusion.1.meta_ref, bf16[128,320,128]{2,1,0:T(8,128)(2,1)S(1)} %get-tuple-element.36.at_ref, f32[1024,128]{1,0:T(8,128)S(1)} %get-tuple-element.55.after_ref.tile_ref, ...), custom_call_target="tpu_custom_call" | custom-call | tf_op jit(solution)/shard_map/pallas_call | solution.py:625
  (36 shorter events, 0.3 us)
Async XLA Ops:
  0.7 1.2 %copy-start = (f32[16,8,2048]{2,1,0:T(8,128)S(1)}, f32[16,8,2048]{2,1,0:T(8,128)}, u32[]{:S(2)}) copy-start(f32[16,8,2048]{2,1,0:T(8,128)} %param.14) | copy-start | bytes 3145732
  1.9 11.9 %copy-start.1 = (f32[16,8,2048]{2,1,0:T(8,128)S(1)}, f32[16,8,2048]{2,1,0:T(8,128)}, u32[]{:S(2)}) copy-start(f32[16,8,2048]{2,1,0:T(8,128)} %param.14) | copy-start | bytes 3145732
  2.6 4.6 %collective-permute-start = (f32[256,128]{1,0:T(8,128)S(1)}, f32[256,128]{1,0:T(8,128)S(1)}, u32[]{:S(2)}, u32[]{:S(2)}) collective-permute-start(f32[256,128]{1,0:T(8,128)S(1)} %get-tuple-element.33), channel_id=1, source_target_pairs={{0,1},{2,3},{1,0},{3,2},{4,5},{6,7},{5,4},{7,6},{8,9},{10,11},{9,8... | collective-permute-start | bytes 393224 | tf_op jit(solution)/shard_map/ppermute | solution.py:598
  3.3 6.3 %collective-permute-start.1 = (f32[256,128]{1,0:T(8,128)S(1)}, f32[256,128]{1,0:T(8,128)S(1)}, u32[]{:S(2)}, u32[]{:S(2)}) collective-permute-start(f32[256,128]{1,0:T(8,128)S(1)} %get-tuple-element.34), channel_id=1, source_target_pairs={{1,2},{2,1},{5,6},{6,5},{9,10},{10,9},{13,14},{14,13},{17,18},{18,... | collective-permute-start | bytes 393224 | tf_op jit(solution)/shard_map/ppermute | solution.py:598
  9.6 20.1 %collective-permute-start.2 = (f32[160,128]{1,0:T(8,128)S(1)}, f32[160,128]{1,0:T(8,128)S(1)}, u32[]{:S(2)}, u32[]{:S(2)}) collective-permute-start(f32[160,128]{1,0:T(8,128)S(1)} %pad_maximum_fusion.refs_0_), channel_id=1, source_target_pairs={{0,4},{8,12},{16,20},{24,28},{4,0},{12,8},{20,16},{28,24},{1,5},{9... | collective-permute-start | bytes 245768 | tf_op jit(solution)/shard_map/ppermute | solution.py:609
  10.9 18.8 %collective-permute-start.3 = (f32[160,128]{1,0:T(8,128)S(1)}, f32[160,128]{1,0:T(8,128)S(1)}, u32[]{:S(2)}, u32[]{:S(2)}) collective-permute-start(f32[160,128]{1,0:T(8,128)S(1)} %pad_maximum_fusion.1.refs_1_), channel_id=1, source_target_pairs={{4,8},{12,16},{20,24},{8,4},{16,12},{24,20},{5,9},{13,17},{21,25},... | collective-permute-start | bytes 245768 | tf_op jit(solution)/shard_map/ppermute | solution.py:609
  13.8 0.7 copy-start.4
  14.5 0.7 copy-start.6
  36.3 6.9 %collective-permute-start.4 = (f32[256,128]{1,0:T(8,128)S(1)}, f32[256,128]{1,0:T(8,128)S(1)}, u32[]{:S(2)}, u32[]{:S(2)}) collective-permute-start(f32[256,128]{1,0:T(8,128)S(1)} %get-tuple-element.41), channel_id=1, source_target_pairs={{0,1},{2,3},{1,0},{3,2},{4,5},{6,7},{5,4},{7,6},{8,9},{10,11},{9,8... | collective-permute-start | bytes 393224 | tf_op jit(solution)/shard_map/ppermute | solution.py:598
  36.3 6.9 %collective-permute-start.5 = (f32[256,128]{1,0:T(8,128)S(1)}, f32[256,128]{1,0:T(8,128)S(1)}, u32[]{:S(2)}, u32[]{:S(2)}) collective-permute-start(f32[256,128]{1,0:T(8,128)S(1)} %get-tuple-element.42), channel_id=1, source_target_pairs={{1,2},{2,1},{5,6},{6,5},{9,10},{10,9},{13,14},{14,13},{17,18},{18,... | collective-permute-start | bytes 393224 | tf_op jit(solution)/shard_map/ppermute | solution.py:598
  40.1 7.6 %copy-start.7 = (bf16[16,128]{1,0:T(8,128)(2,1)S(1)}, bf16[16,128]{1,0:T(8,128)(2,1)}, u32[]{:S(2)}) copy-start(bf16[16,128]{1,0:T(8,128)(2,1)} %constant.75.modes_ref) | copy-start | bytes 12292
  43.3 7.8 %collective-permute-start.7 = (f32[160,128]{1,0:T(8,128)S(1)}, f32[160,128]{1,0:T(8,128)S(1)}, u32[]{:S(2)}, u32[]{:S(2)}) collective-permute-start(f32[160,128]{1,0:T(8,128)S(1)} %get-tuple-element.69), channel_id=1, source_target_pairs={{4,8},{12,16},{20,24},{8,4},{16,12},{24,20},{5,9},{13,17},{21,25},... | collective-permute-start | bytes 245768 | tf_op jit(solution)/shard_map/ppermute | solution.py:609
  47.4 3.6 %collective-permute-start.6 = (f32[160,128]{1,0:T(8,128)S(1)}, f32[160,128]{1,0:T(8,128)S(1)}, u32[]{:S(2)}, u32[]{:S(2)}) collective-permute-start(f32[160,128]{1,0:T(8,128)S(1)} %get-tuple-element.70), channel_id=1, source_target_pairs={{0,4},{8,12},{16,20},{24,28},{4,0},{12,8},{20,16},{28,24},{1,5},{9... | collective-permute-start | bytes 245768 | tf_op jit(solution)/shard_map/ppermute | solution.py:609
  51.1 30.9 %copy-start.3 = (bf16[256,512]{1,0:T(8,128)(2,1)S(1)}, bf16[256,512]{1,0:T(8,128)(2,1)}, u32[]{:S(2)}) copy-start(bf16[256,512]{1,0:T(8,128)(2,1)} %constant.63.clone.place_ref) | copy-start | bytes 786436
  52.7 44.2 %copy-start.5 = (bf16[64,128]{1,0:T(8,128)(2,1)S(1)}, bf16[64,128]{1,0:T(8,128)(2,1)}, u32[]{:S(2)}) copy-start(bf16[64,128]{1,0:T(8,128)(2,1)} %constant.66.clone.order_ref) | copy-start | bytes 49156
  85.9 15.6 %copy-start.2 = (bf16[256,512]{1,0:T(8,128)(2,1)S(1)}, bf16[256,512]{1,0:T(8,128)(2,1)}, u32[]{:S(2)}) copy-start(bf16[256,512]{1,0:T(8,128)(2,1)} %constant.65.clone.place_ref) | copy-start | bytes 786436
  85.9 3.5 %collective-permute-start.8 = (f32[128,128]{1,0:T(8,128)S(1)}, f32[128,128]{1,0:T(8,128)S(1)}, u32[]{:S(2)}, u32[]{:S(2)}) collective-permute-start(f32[128,128]{1,0:T(8,128)S(1)} %get-tuple-element.57), channel_id=1, source_target_pairs={{0,1},{2,3},{1,0},{3,2},{4,5},{6,7},{5,4},{7,6},{8,9},{10,11},{9,8... | collective-permute-start | bytes 196616 | tf_op jit(solution)/shard_map/ppermute | solution.py:598
  87.4 5.6 %collective-permute-start.9 = (f32[128,128]{1,0:T(8,128)S(1)}, f32[128,128]{1,0:T(8,128)S(1)}, u32[]{:S(2)}, u32[]{:S(2)}) collective-permute-start(f32[128,128]{1,0:T(8,128)S(1)} %get-tuple-element.58), channel_id=1, source_target_pairs={{1,2},{2,1},{5,6},{6,5},{9,10},{10,9},{13,14},{14,13},{17,18},{18,... | collective-permute-start | bytes 196616 | tf_op jit(solution)/shard_map/ppermute | solution.py:598
  92.9 8.6 %collective-permute-start.10 = (f32[80,128]{1,0:T(8,128)S(1)}, f32[80,128]{1,0:T(8,128)S(1)}, u32[]{:S(2)}, u32[]{:S(2)}) collective-permute-start(f32[80,128]{1,0:T(8,128)S(1)} %pad_maximum_fusion.2), channel_id=1, source_target_pairs={{0,4},{8,12},{16,20},{24,28},{4,0},{12,8},{20,16},{28,24},{1,5},{9... | collective-permute-start | bytes 122888 | tf_op jit(solution)/shard_map/ppermute | solution.py:609
  93.4 8.2 %collective-permute-start.11 = (f32[80,128]{1,0:T(8,128)S(1)}, f32[80,128]{1,0:T(8,128)S(1)}, u32[]{:S(2)}, u32[]{:S(2)}) collective-permute-start(f32[80,128]{1,0:T(8,128)S(1)} %pad_maximum_fusion.3), channel_id=1, source_target_pairs={{4,8},{12,16},{20,24},{8,4},{16,12},{24,20},{5,9},{13,17},{21,25},... | collective-permute-start | bytes 122888 | tf_op jit(solution)/shard_map/ppermute | solution.py:609
